TPU v7x, 128 devices: a whole 4x4x4 slice. The times are simulated.
128 devices in a mesh: sky: 16 (over z, y), exp: 8 (over x, core).
Axes of the slice: x: 4, y: 4, z: 4, core: 2. Of those that a mesh axis runs over, the one named last changes fastest.
Arguments:
- sky_model: bfloat16 [4096, 1024], P('sky'), may hold values from -6 to 6
- exposure_data: bfloat16 [2048, 128, 128], P(('sky', 'exp')), may hold values from -6 to 6
- pixel_mask: int32 [2048, 128, 128], P(('sky', 'exp')), may hold values 0 or 1
- block_owner: int32 [2048, 1], P(('sky', 'exp')), may hold values from 0 to 15; in each aligned block of 16 rows (0 to 15, 16 to 31, ...) at most 2 rows name the same one
- block_local: int32 [2048], P(('sky', 'exp')), may hold values from 0 to 15
- psf_cell: int32 [2048], P(('sky', 'exp')), may hold values from 0 to 15
- psf_table: bfloat16 [128, 1681], P('exp'), may hold values from -0.15625 to 0.15625
Outputs:
- model_grad: float32 [4096, 1024], P('sky', 'exp')
- residual: bfloat16 [2048, 128, 128], P(('sky', 'exp'))
Inputs may be any that keep to these rules, and one draw needn't show every extreme that they name: `block_owner`: among the pieces of one device no sky index is named more than 2 times.
All inputs are finite; a program needn't handle non-finite values. No bound on the sum of `pixel_mask` on one device may be relied on, other than what follows from the above.
Results may differ from a plain program's by a relative error of at most 0.014.
Values may be sent and summed in bfloat16 or wider, within the bound.
No kernel may reach another device: no remote copies, remote signals or barrier semaphores. Data moves between devices by JAX's collectives and lax.ppermute only.
A program may use at most 64 MiB of HBM per device.

v0:
```python
import jax
import jax.numpy as jnp
from jax import lax
from jax.experimental import pallas as pl
from jax.experimental.pallas import tpu as pltpu
from jax.sharding import PartitionSpec as P

B = 128
PSF = 41
HALO = 20
CAP = 2

G = 16
LANES = 128
OUT = B // G
EXT = 11
REACH = 4
LEAD = 28
FWD_ROWS = 88
BLK_ROWS = 96
SLOT_ROWS = 128
PITCH = 72
TILES = 6
RES_LEAD = 40
BATCH = 4
SLOTS = 8
CHUNK = 9
CHUNK_ROWS = 352
SHIFT = 4
SMALL = pl.CostEstimate(flops=1000, bytes_accessed=1000, transcendentals=0)
F32 = jnp.float32
BF16 = jnp.bfloat16


def from_behind(x, axis, by):
    devices = lax.axis_size(axis)
    pairs = [(i, i + by) for i in range(devices) if 0 <= i + by < devices]
    return lax.ppermute(x, axis, pairs)


def swap_groups(x):
    sub = lax.broadcasted_iota(jnp.int32, x.shape, 1)
    group = lax.broadcasted_iota(jnp.int32, x.shape, 2) // G
    for d in (4, 2, 1):
        sub_bit, group_bit = (sub & d) != 0, (group & d) != 0
        up = pltpu.roll(pltpu.roll(x, 8 - d, 1), G * d, 2)
        down = up if d == 4 else pltpu.roll(pltpu.roll(x, d, 1), LANES - G * d, 2)
        x = jnp.where(sub_bit == group_bit, x, jnp.where(group_bit, up, down))
    return x


def regroup_kernel(data_ref, keep_ref, data_out, keep_out, scratch):
    def per_piece(p, carry):
        for source, target in ((data_ref, data_out), (keep_ref, keep_out)):
            blocks = swap_groups(source[p].astype(F32).reshape(2 * OUT, 8, LANES))
            scratch[...] = jnp.zeros_like(scratch)
            for row in range(2 * OUT):
                half = row % 2
                scratch[pl.ds(EXT * (row // 2), 8), half * LANES : (half + 1) * LANES] = blocks[row]
            target[p] = scratch[...].astype(BF16)
        return carry

    lax.fori_loop(0, data_ref.shape[0], per_piece, 0)


def regroup(exposure_data, pixel_mask):
    pieces = exposure_data.shape[0]
    block = pl.BlockSpec((BATCH, B, B), lambda p: (p, 0, 0))
    out = pl.BlockSpec((BATCH, BLK_ROWS, 2 * LANES), lambda p: (p, 0, 0))
    shape = jax.ShapeDtypeStruct((pieces, BLK_ROWS, 2 * LANES), BF16)
    return pl.pallas_call(
        regroup_kernel,
        grid=(pieces // BATCH,),
        in_specs=[block, block],
        out_specs=[out, out],
        out_shape=[shape, shape],
        scratch_shapes=[pltpu.VMEM((BLK_ROWS, 2 * LANES), F32)],
        cost_estimate=SMALL,
        name="regroup",
    )(exposure_data, pixel_mask)


def tap_rows(table):
    cells = table.shape[0]
    kernel = jnp.pad(table.reshape(cells, PSF, PSF), ((0, 0), (0, 7), (G, 23)))
    kernel = kernel.reshape(cells, 24, 2, 5 * G).transpose(0, 2, 1, 3)
    windows = [kernel[..., G * t : G * t + 2 * G].reshape(cells, 2, TILES * LANES) for t in range(REACH)]
    return jnp.stack(windows, 1).astype(F32)


def taps_kernel(rows_ref, out_ref):
    lane = lax.broadcasted_iota(jnp.int32, (G, LANES), 1)
    odd = (lane // G) % 2 == 1

    def per_shift(t, carry):
        before = jnp.zeros((G, LANES), BF16)
        for tile in range(TILES):
            lanes = slice(tile * LANES, (tile + 1) * LANES)
            even_row, odd_row = (
                jnp.broadcast_to(rows_ref[0, t, parity : parity + 1, lanes], (G, LANES))
                for parity in range(2)
            )
            even_row = pltpu.roll(even_row, LANES - G, 1, stride=1, stride_axis=0)
            odd_row = pltpu.roll(odd_row, 0, 1, stride=1, stride_axis=0)
            now = jnp.where(odd, odd_row, even_row).astype(BF16)
            for phase in range(8):
                if phase == 0:
                    part = now
                else:
                    part = pltpu.roll(jnp.where(lane < LANES - G * phase, now, before), G * phase, 1)
                start = pl.multiple_of(t * LANES + phase * G, G)
                out_ref[0, pl.ds(start, G), lanes] = part
            before = now
        return carry

    lax.fori_loop(0, REACH, per_shift, 0)


def build_taps(rows):
    cells = rows.shape[0]
    return pl.pallas_call(
        taps_kernel,
        grid=(cells,),
        in_specs=[pl.BlockSpec((1, REACH, 2, TILES * LANES), lambda c: (c, 0, 0, 0))],
        out_specs=pl.BlockSpec((1, REACH * LANES, TILES * LANES), lambda c: (c, 0, 0)),
        out_shape=jax.ShapeDtypeStruct((cells, REACH * LANES, TILES * LANES), BF16),
        cost_estimate=SMALL,
        name="taps",
    )(rows)


def blocks_kernel(stripe_ref, out_ref):
    def per_row(r, carry):
        start = pl.multiple_of(r * G, G)
        for tile in range(PITCH // 8):
            part = stripe_ref[pl.ds(start, G), tile * LANES : (tile + 1) * LANES].astype(F32)
            out_ref[pl.ds(2 * r, 2), tile * 8 : (tile + 1) * 8, :] = swap_groups(
                part.reshape(2, 8, LANES)
            )
        return carry

    lax.fori_loop(0, stripe_ref.shape[0] // G, per_row, 0)


def stripe_blocks(stripe):
    rows = stripe.shape[0] // 8
    return pl.pallas_call(
        blocks_kernel,
        out_shape=jax.ShapeDtypeStruct((rows, PITCH, LANES), F32),
        in_specs=[pl.BlockSpec(memory_space=pltpu.VMEM)],
        out_specs=pl.BlockSpec(memory_space=pltpu.VMEM),
        cost_estimate=SMALL,
        name="blocks",
    )(stripe)


def cut_kernel(per_row, ids_ref, blocks_ref, out_ref, scratch):
    step = pl.program_id(0)

    def per_slot(n, carry):
        wanted = ids_ref[step * SLOTS + n]

        @pl.when(wanted >= 0)
        def _():
            first_row = wanted // per_row * (2 * OUT)
            first_col = pl.multiple_of(wanted % per_row * OUT, 8)
            for row in range(EXT):
                for half in range(2):
                    part = blocks_ref[first_row + 2 * row + half, pl.ds(first_col, G), :]
                    scratch[pl.ds(EXT * row, G), half * LANES : (half + 1) * LANES] = part
            out_ref[n] = scratch[...].astype(BF16)

        return carry

    lax.fori_loop(0, SLOTS, per_slot, 0)


def cut_patches(ids, blocks, per_row):
    slots = ids.shape[0]
    return pl.pallas_call(
        lambda *refs: cut_kernel(per_row, *refs),
        grid_spec=pltpu.PrefetchScalarGridSpec(
            num_scalar_prefetch=1,
            grid=(slots // SLOTS,),
            in_specs=[pl.BlockSpec(blocks.shape, lambda n, ids: (0, 0, 0))],
            out_specs=pl.BlockSpec((SLOTS, SLOT_ROWS, 2 * LANES), lambda n, ids: (n, 0, 0)),
            scratch_shapes=[pltpu.VMEM((SLOT_ROWS, 2 * LANES), F32)],
        ),
        out_shape=jax.ShapeDtypeStruct((slots, SLOT_ROWS, 2 * LANES), BF16),
        cost_estimate=SMALL,
        name="cut",
    )(ids, blocks)


def convolve(read, taps_ref, rows):
    total = jnp.zeros((rows, 2 * LANES), F32)
    for t in range(REACH):
        taps = slice(t * LANES, (t + 1) * LANES)
        for s in range(REACH - 1):
            upper = taps_ref[0, taps, 2 * s * LANES : (2 * s + 2) * LANES]
            if s == 0:
                lower = jnp.concatenate(
                    [jnp.zeros((LANES, LANES), BF16), taps_ref[0, taps, 0:LANES]], axis=1
                )
            else:
                lower = taps_ref[0, taps, (2 * s - 1) * LANES : (2 * s + 1) * LANES]
            total = total + jnp.dot(
                read(s, t), jnp.concatenate([upper, lower], axis=0), preferred_element_type=F32
            )
    last = jnp.zeros((rows, LANES), F32)
    for t in range(0, REACH, 2):
        field = jnp.concatenate(
            [read(REACH - 1, t)[:, LANES:], read(REACH - 1, t + 1)[:, LANES:]], axis=1
        )
        taps = taps_ref[0, t * LANES : (t + 2) * LANES, (TILES - 1) * LANES :]
        last = last + jnp.dot(field, taps, preferred_element_type=F32)
    return jnp.concatenate([total[:, :LANES] + last, total[:, LANES:]], axis=1)


def piece_kernel(
    slot_ref, cell_ref, patch_ref, forward_ref, adjoint_ref, data_ref, keep_ref, adj_out, res_out, field, resid
):
    @pl.when(pl.program_id(0) == 0)
    def _():
        resid[...] = jnp.zeros_like(resid)

    field[...] = patch_ref[0].astype(F32)

    def read_patch(s, t):
        start = EXT * (REACH - 1 - s) + REACH - 1 - t
        return field[pl.ds(start, FWD_ROWS), :].astype(BF16)

    predicted = convolve(read_patch, forward_ref, FWD_ROWS)
    observed = data_ref[0, :FWD_ROWS].astype(F32)
    keep = keep_ref[0, :FWD_ROWS].astype(F32)
    residual = jnp.where(keep != 0, predicted - observed, 0.0).astype(BF16)
    res_out[0, :FWD_ROWS] = residual
    resid[RES_LEAD : RES_LEAD + FWD_ROWS, :] = residual.astype(F32)

    def read_residual(s, t):
        return resid[pl.ds(RES_LEAD - EXT * s - t, SLOT_ROWS), :].astype(BF16)

    adj_out[0] = convolve(read_residual, adjoint_ref, SLOT_ROWS).astype(BF16)


def pieces(slots, cells, patches, all_taps, data, keep):
    count = data.shape[0]
    cell_count = all_taps.shape[0] // 2
    slot = pl.BlockSpec((1, SLOT_ROWS, 2 * LANES), lambda p, slots, cells: (slots[p], 0, 0))
    taps_shape = (1, REACH * LANES, TILES * LANES)
    forward = pl.BlockSpec(taps_shape, lambda p, slots, cells: (cells[p], 0, 0))
    adjoint = pl.BlockSpec(taps_shape, lambda p, slots, cells: (cells[p] + cell_count, 0, 0))
    block = pl.BlockSpec((1, BLK_ROWS, 2 * LANES), lambda p, slots, cells: (p, 0, 0))
    return pl.pallas_call(
        piece_kernel,
        grid_spec=pltpu.PrefetchScalarGridSpec(
            num_scalar_prefetch=2,
            grid=(count,),
            in_specs=[slot, forward, adjoint, block, block],
            out_specs=[slot, block],
            scratch_shapes=[
                pltpu.VMEM((SLOT_ROWS, 2 * LANES), F32),
                pltpu.VMEM((RES_LEAD + SLOT_ROWS, 2 * LANES), F32),
            ],
        ),
        out_shape=[
            jax.ShapeDtypeStruct(patches.shape, BF16),
            jax.ShapeDtypeStruct(data.shape, BF16),
        ],
        cost_estimate=SMALL,
        name="pieces",
    )(slots, cells, patches, all_taps, all_taps, data, keep)


def ungroup_kernel(res_ref, out_ref, scratch):
    def per_piece(p, carry):
        scratch[...] = res_ref[p].astype(F32)
        for row in range(OUT):
            halves = [
                scratch[pl.ds(EXT * row, 8), half * LANES : (half + 1) * LANES] for half in range(2)
            ]
            rows = swap_groups(jnp.stack(halves, 0)).reshape(G, LANES)
            out_ref[p, row * G : (row + 1) * G, :] = rows.astype(BF16)
        return carry

    lax.fori_loop(0, res_ref.shape[0], per_piece, 0)


def ungroup(residual):
    count = residual.shape[0]
    return pl.pallas_call(
        ungroup_kernel,
        grid=(count // BATCH,),
        in_specs=[pl.BlockSpec((BATCH, BLK_ROWS, 2 * LANES), lambda p: (p, 0, 0))],
        out_specs=pl.BlockSpec((BATCH, B, B), lambda p: (p, 0, 0)),
        out_shape=jax.ShapeDtypeStruct((count, B, B), BF16),
        scratch_shapes=[pltpu.VMEM((BLK_ROWS, 2 * LANES), F32)],
        cost_estimate=SMALL,
        name="ungroup",
    )(residual)


def fold_kernel(per_row, half_rows, ids_ref, slot_ref, out_ref, canvas, scratch, packed):
    step = pl.program_id(0)

    @pl.when(step == 0)
    def _():
        canvas[...] = jnp.zeros_like(canvas)

    inside = lax.broadcasted_iota(jnp.int32, (G, LANES), 0) < EXT

    def per_slot(n, carry):
        named = ids_ref[step * SLOTS + n]

        @pl.when(named >= 0)
        def _():
            first_row = named // per_row * (2 * OUT)
            first_col = pl.multiple_of(named % per_row * OUT, 8)
            scratch[...] = slot_ref[n].astype(F32)
            for row in range(EXT):
                for half in range(2):
                    part = scratch[pl.ds(EXT * row, G), half * LANES : (half + 1) * LANES]
                    part = jnp.where(inside, part, 0.0)
                    at = (first_row + 2 * row + half, pl.ds(first_col, G), slice(None))
                    canvas[at] = canvas[at] + part

        return carry

    lax.fori_loop(0, SLOTS, per_slot, 0)

    @pl.when(step == pl.num_programs(0) - 1)
    def _():
        for chunk in range(per_row):
            first = OUT * chunk + 1
            for row in range(half_rows):
                packed[CHUNK * row : CHUNK * row + G, :] = canvas[row, first : first + G, :]
            out_ref[chunk] = packed[...].astype(BF16)


def fold(ids, received, per_row, half_rows):
    slots = ids.shape[0]
    return pl.pallas_call(
        lambda *refs: fold_kernel(per_row, half_rows, *refs),
        grid_spec=pltpu.PrefetchScalarGridSpec(
            num_scalar_prefetch=1,
            grid=(slots // SLOTS,),
            in_specs=[pl.BlockSpec((SLOTS, SLOT_ROWS, 2 * LANES), lambda n, ids: (n, 0, 0))],
            out_specs=pl.BlockSpec((per_row, CHUNK_ROWS, LANES), lambda n, ids: (0, 0, 0)),
            scratch_shapes=[
                pltpu.VMEM((half_rows, PITCH + 8, LANES), F32),
                pltpu.VMEM((SLOT_ROWS, 2 * LANES), F32),
                pltpu.VMEM((CHUNK_ROWS, LANES), F32),
            ],
        ),
        out_shape=jax.ShapeDtypeStruct((per_row, CHUNK_ROWS, LANES), BF16),
        cost_estimate=SMALL,
        name="fold",
    )(ids, received)


def finish_kernel(half_rows, terms_ref, up_out, middle_out, down_out, summed, canvas):
    total = terms_ref[0].astype(F32)
    for term in range(1, terms_ref.shape[0]):
        total = total + terms_ref[term].astype(F32)
    summed[...] = total
    near = lax.broadcasted_iota(jnp.int32, (8, LANES), 1) < LANES - SHIFT
    for row in range(half_rows):
        first = CHUNK * row
        tiles = swap_groups(summed[first : first + G, :].reshape(2, 8, LANES))
        tile = pltpu.roll(tiles[0], LANES - SHIFT, 1)
        edge = pltpu.roll(tiles[1], LANES - SHIFT, 1)
        canvas[8 * row : 8 * row + 8, :] = jnp.where(near, tile, edge)
    middle = middle_out.shape[0]
    up_out[...] = canvas[:HALO, :].astype(BF16)
    middle_out[...] = canvas[HALO : HALO + middle, :]
    down_out[...] = canvas[HALO + middle : 2 * HALO + middle, :].astype(BF16)


def finish(terms, half_rows, rows):
    rim = jax.ShapeDtypeStruct((HALO, LANES), BF16)
    vmem = pl.BlockSpec(memory_space=pltpu.VMEM)
    return pl.pallas_call(
        lambda *refs: finish_kernel(half_rows, *refs),
        in_specs=[vmem],
        out_specs=[vmem, vmem, vmem],
        out_shape=[rim, jax.ShapeDtypeStruct((rows, LANES), F32), rim],
        scratch_shapes=[
            pltpu.VMEM((CHUNK_ROWS, LANES), F32),
            pltpu.VMEM((8 * half_rows, LANES), F32),
        ],
        cost_estimate=SMALL,
        name="finish",
    )(terms)


def shards(sky_model, exposure_data, pixel_mask, block_owner, block_local, psf_cell, psf_table):
    sky_count = lax.axis_size("sky")
    stripe_rows, stripe_cols = sky_model.shape
    per_row = stripe_cols // B
    block_total = stripe_rows // B * per_row
    piece_count = exposure_data.shape[0]
    owner_sky = block_owner[:, 0]
    code = lax.broadcasted_iota(jnp.int32, (piece_count,), 0) * block_total + block_local
    mine = owner_sky[None, :] == lax.broadcasted_iota(jnp.int32, (sky_count, 1), 0)
    first = jnp.min(jnp.where(mine, code[None, :], piece_count * block_total), axis=1)
    last = jnp.max(jnp.where(mine, code[None, :], -1), axis=1)
    requests = jnp.stack(
        [
            jnp.where(last < 0, -1, first % block_total),
            jnp.where(last > first, last % block_total, -1),
        ],
        axis=1,
    )
    asked = lax.all_to_all(requests, "sky", split_axis=0, concat_axis=0, tiled=True)
    asked = asked.reshape(sky_count * CAP)

    above = from_behind(sky_model[stripe_rows - LEAD :], "sky", 1)
    below = from_behind(sky_model[:HALO], "sky", -1)
    stripe = jnp.concatenate([above, sky_model, below], axis=0)
    stripe = jnp.pad(stripe, ((0, 0), (LEAD, PITCH * G - LEAD - stripe_cols)))
    blocks = stripe_blocks(stripe)
    data, keep = regroup(exposure_data, pixel_mask)
    second = jnp.any(mine & (first[:, None] < code[None, :]), axis=0)
    slot_index = owner_sky * CAP + second.astype(jnp.int32)
    rows = tap_rows(jnp.concatenate([psf_table[:, ::-1], psf_table], axis=0))
    asked, blocks, data, keep, slot_index, rows = lax.optimization_barrier(
        (asked, blocks, data, keep, slot_index, rows)
    )
    outgoing = cut_patches(asked, blocks, per_row)
    patches = lax.all_to_all(outgoing, "sky", split_axis=0, concat_axis=0, tiled=True)
    rows, _ = lax.optimization_barrier((rows, outgoing))
    taps = build_taps(rows)
    adjoints, residuals = pieces(slot_index, psf_cell, patches, taps, data, keep)
    received = lax.all_to_all(adjoints, "sky", split_axis=0, concat_axis=0, tiled=True)
    received, residual = lax.optimization_barrier((received, ungroup(residuals)))

    half_rows = (stripe_rows + LEAD + HALO) // 8
    partial = fold(asked, received, per_row, half_rows)
    terms = lax.all_to_all(partial, "exp", split_axis=0, concat_axis=0, tiled=True)
    up, middle, down = finish(terms, half_rows, stripe_rows)
    from_below = from_behind(up, "sky", -1).astype(F32)
    from_above = from_behind(down, "sky", 1).astype(F32)
    gradient = (
        middle
        + jnp.pad(from_above, ((0, stripe_rows - HALO), (0, 0)))
        + jnp.pad(from_below, ((stripe_rows - HALO, 0), (0, 0)))
    )
    return (gradient, residual)


def solution(mesh):
    in_specs = (
        P("sky", None),
        P(("sky", "exp"), None, None),
        P(("sky", "exp"), None, None),
        P(("sky", "exp"), None),
        P(("sky", "exp")),
        P(("sky", "exp")),
        P("exp", None),
    )
    out_specs = (P("sky", "exp"), P(("sky", "exp"), None, None))
    return jax.shard_map(shards, mesh=mesh, in_specs=in_specs, out_specs=out_specs, check_vma=False)
```

profile of v0, /device:TPU:24, one launch (start us, length us, event | category | flops | bytes accessed | tf_op | source)
XLA Modules:
  0.0 187.7 jit_solution(16877457345849367110)
XLA Ops:
  0.6 0.7 multiply_add_fusion
  1.3 0.8 select_reduce_fusion.1
  2.1 0.7 copy.22
  2.8 8.2 %all-to-all-start = ((s32[16,1,2]{2,1,0:T(1,128)}), s32[16,1,2]{2,1,0:T(1,128)S(1)}, u32[]{:S(2)}, u32[]{:S(2)}) async-start(s32[16,1,2]{2,1,0:T(1,128)} %copy.22), calls=%async_computation | async-start | bytes 16384 | tf_op jit(solution)/shard_map/all_to_all | solution.py:414
  11.0 0.8 slice.19
  11.8 2.8 %collective-permute-start.1 = (bf16[20,1024]{1,0:T(8,128)(2,1)S(1)}, bf16[20,1024]{1,0:T(8,128)(2,1)S(1)}, u32[]{:S(2)}, u32[]{:S(2)}) collective-permute-start(bf16[20,1024]{1,0:T(8,128)(2,1)S(1)} %slice.19), channel_id=1, source_target_pairs={{8,0},{16,8},{24,16},{32,24},{40,32},{48,40},{56,48},{64,56},{72,6... | collective-permute-start | bytes 122888 | tf_op jit(solution)/shard_map/ppermute | solution.py:38
  14.5 0.9 slice.18
  15.4 5.2 %collective-permute-start = (bf16[28,1024]{1,0:T(8,128)(2,1)S(1)}, bf16[28,1024]{1,0:T(8,128)(2,1)S(1)}, u32[]{:S(2)}, u32[]{:S(2)}) collective-permute-start(bf16[28,1024]{1,0:T(8,128)(2,1)S(1)} %slice.18), channel_id=1, source_target_pairs={{0,8},{8,16},{16,24},{24,32},{32,40},{40,48},{48,56},{56,64},{64,7... | collective-permute-start | bytes 172040 | tf_op jit(solution)/shard_map/ppermute | solution.py:38
  20.6 0.7 fusion.7
  21.3 1.2 convert_add_fusion.1.slot_ref
  22.5 5.4 %reverse = bf16[16,1792]{1,0:T(8,128)(2,1)S(1)} reverse(bf16[16,1792]{1,0:T(8,128)(2,1)} %bitcast.23), dimensions={1} | reverse | bytes 114688
  27.9 0.1 slice.28
  28.0 0.8 pad_maximum_fusion
  28.8 0.5 reshape.112
  29.3 0.1 copy.28
  29.4 0.2 pad.23.clone
  29.6 0.4 fusion.10
  30.0 0.3 copy.24
  30.3 0.3 stack_reshape.12
  30.6 0.3 copy.27
  30.9 0.3 stack_reshape.15
  31.2 0.3 copy.26
  31.4 0.3 stack_reshape.14
  31.7 0.3 copy.25
  32.0 0.3 stack_reshape.13
  32.3 1.4 maximum_convert_fusion.rows_ref
  33.7 6.5 %regroup.1 = (bf16[16,96,256]{2,1,0:T(8,128)(2,1)}, bf16[16,96,256]{2,1,0:T(8,128)(2,1)}) custom-call(bf16[16,128,128]{2,1,0:T(8,128)(2,1)} %data_ref.1, s32[16,128,128]{2,1,0:T(8,128)} %keep_ref.1), custom_call_target="tpu_custom_call" | custom-call | flops 1000 | bytes 1000 | tf_op jit(solution)/shard_map/regroup/pallas_call | solution.py:71
  40.2 0.5 broadcast.135
  40.7 0.7 reduce.3
  41.4 1.3 fusion.5.stripe_ref
  42.8 0.6 reshape.111.refs_0_
  43.4 6.7 %blocks.1.refs_1_ = f32[38,72,128]{2,1,0:T(8,128)} custom-call(bf16[304,1152]{1,0:T(8,128)(2,1)} %fusion.5.stripe_ref), custom_call_target="tpu_custom_call" | custom-call | flops 1000 | bytes 1000 | tf_op jit(solution)/shard_map/blocks/pallas_call | solution.py:147
  50.1 4.3 %cut.1 = bf16[32,128,256]{2,1,0:T(8,128)(2,1)} custom-call(s32[32]{0:T(128)} %reshape.111.refs_0_, f32[38,72,128]{2,1,0:T(8,128)} %blocks.1.refs_1_), custom_call_target="tpu_custom_call" | custom-call | flops 1000 | bytes 1000 | tf_op jit(solution)/shard_map/cut/pallas_call | solution.py:180
  54.3 7.0 %all-to-all-start.1 = ((bf16[32,128,256]{2,1,0:T(8,128)(2,1)}), bf16[32,128,256]{2,1,0:T(8,128)(2,1)S(1)}, u32[]{:S(2)}, u32[]{:S(2)}) async-start(bf16[32,128,256]{2,1,0:T(8,128)(2,1)} %cut.1), calls=%async_computation.1 | async-start | bytes 4194304 | tf_op jit(solution)/shard_map/all_to_all | solution.py:430
  61.3 28.2 %taps.1.forward_ref.adjoint_ref = bf16[32,512,768]{2,1,0:T(8,128)(2,1)} custom-call(f32[32,4,2,768]{3,2,1,0:T(2,128)} %maximum_convert_fusion.rows_ref), custom_call_target="tpu_custom_call" | custom-call | flops 1000 | bytes 1000 | tf_op jit(solution)/shard_map/taps/pallas_call | solution.py:121
  89.5 1.4 copy-done
  90.9 23.2 %pieces.1 = (bf16[32,128,256]{2,1,0:T(8,128)(2,1)}, bf16[16,96,256]{2,1,0:T(8,128)(2,1)}) custom-call(s32[16]{0:T(128)} %convert_add_fusion.1.slot_ref, s32[16]{0:T(128)} %cell_ref.1, bf16[32,128,256]{2,1,0:T(8,128)(2,1)} %copy-done, bf16[32,512,768]{2,1,0:T(8,128)(2,1)} %taps.1.forward_ref.adjoint_ref, bf16[32,512,768]{2,1,0:T(8,128)(2,1)} %taps.1.forward_ref.adjoint_ref, ...), custom_call_target="tpu_custom_call" | custom-call | flops 1000 | bytes 1000 | tf_op jit(solution)/shard_map/pieces/pallas_call | solution.py:254
  114.1 7.3 %all-to-all-start.2 = ((bf16[32,128,256]{2,1,0:T(8,128)(2,1)}), bf16[32,128,256]{2,1,0:T(8,128)(2,1)S(1)}, u32[]{:S(2)}, u32[]{:S(2)}) async-start(bf16[32,128,256]{2,1,0:T(8,128)(2,1)} %get-tuple-element.27), calls=%async_computation.2 | async-start | bytes 4194304 | tf_op jit(solution)/shard_map/all_to_all | solution.py:434
  121.4 5.5 %ungroup.1 = bf16[16,128,128]{2,1,0:T(8,128)(2,1)} custom-call(bf16[16,96,256]{2,1,0:T(8,128)(2,1)} %get-tuple-element.28.res_ref), custom_call_target="tpu_custom_call" | custom-call | flops 1000 | bytes 1000 | tf_op jit(solution)/shard_map/ungroup/pallas_call | solution.py:291
  126.9 18.7 %all-to-all-done.2.refs_1_ = bf16[32,128,256]{2,1,0:T(8,128)(2,1)S(1)} async-done(((bf16[32,128,256]{2,1,0:T(8,128)(2,1)}), bf16[32,128,256]{2,1,0:T(8,128)(2,1)S(1)}, u32[]{:S(2)}, u32[]{:S(2)}) %all-to-all-start.2) | async-done | bytes 2097184 | tf_op jit(solution)/shard_map/all_to_all | solution.py:434
  145.6 1.3 copy-done.1
  147.0 4.7 %fold.1 = bf16[8,352,128]{2,1,0:T(8,128)(2,1)} custom-call(s32[32]{0:T(128)} %reshape.111.refs_0_, bf16[32,128,256]{2,1,0:T(8,128)(2,1)} %copy-done.1), custom_call_target="tpu_custom_call" | custom-call | flops 1000 | bytes 1000 | tf_op jit(solution)/shard_map/fold/pallas_call | solution.py:342
  151.7 16.9 %all_to_all.24.refs_0_ = bf16[8,352,128]{2,1,0:T(8,128)(2,1)} all-to-all(bf16[8,352,128]{2,1,0:T(8,128)(2,1)} %fold.1), channel_id=1, replica_groups=mesh['sky'=16,'exp'=8] {'exp'}, dimensions={0} | all-to-all | bytes 1441792 | tf_op jit(solution)/shard_map/all_to_all | solution.py:439
  168.6 4.8 %finish.1 = (bf16[20,128]{1,0:T(8,128)(2,1)}, f32[256,128]{1,0:T(8,128)}, bf16[20,128]{1,0:T(8,128)(2,1)}) custom-call(bf16[8,352,128]{2,1,0:T(8,128)(2,1)} %all_to_all.24.refs_0_), custom_call_target="tpu_custom_call" | custom-call | flops 1000 | bytes 1000 | tf_op jit(solution)/shard_map/finish/pallas_call | solution.py:382
  173.4 4.9 %collective-permute-start.2 = (bf16[20,128]{1,0:T(8,128)(2,1)}, bf16[20,128]{1,0:T(8,128)(2,1)S(1)}, u32[]{:S(2)}, u32[]{:S(2)}) collective-permute-start(bf16[20,128]{1,0:T(8,128)(2,1)} %get-tuple-element.31), channel_id=1, source_target_pairs={{0,8},{8,16},{16,24},{24,32},{32,40},{40,48},{48,56},{56,64},{64,7... | collective-permute-start | bytes 15368 | tf_op jit(solution)/shard_map/ppermute | solution.py:38
  178.3 1.9 %collective-permute-start.3 = (bf16[20,128]{1,0:T(8,128)(2,1)}, bf16[20,128]{1,0:T(8,128)(2,1)S(1)}, u32[]{:S(2)}, u32[]{:S(2)}) collective-permute-start(bf16[20,128]{1,0:T(8,128)(2,1)} %get-tuple-element.32), channel_id=1, source_target_pairs={{8,0},{16,8},{24,16},{32,24},{40,32},{48,40},{56,48},{64,56},{72,6... | collective-permute-start | bytes 15368 | tf_op jit(solution)/shard_map/ppermute | solution.py:38
  180.2 5.9 %collective-permute-done.3 = bf16[20,128]{1,0:T(8,128)(2,1)S(1)} collective-permute-done((bf16[20,128]{1,0:T(8,128)(2,1)}, bf16[20,128]{1,0:T(8,128)(2,1)S(1)}, u32[]{:S(2)}, u32[]{:S(2)}) %collective-permute-start.3) | collective-permute-done | bytes 5152 | tf_op jit(solution)/shard_map/ppermute | solution.py:38
  186.2 1.6 convert_add_fusion
  (11 shorter events, 0.0 us)
Async XLA Ops:
  2.8 37.5 %all-to-all-start = ((s32[16,1,2]{2,1,0:T(1,128)}), s32[16,1,2]{2,1,0:T(1,128)S(1)}, u32[]{:S(2)}, u32[]{:S(2)}) async-start(s32[16,1,2]{2,1,0:T(1,128)} %copy.22), calls=%async_computation | async-start | bytes 16384 | tf_op jit(solution)/shard_map/all_to_all | solution.py:414
  11.8 29.7 %collective-permute-start.1 = (bf16[20,1024]{1,0:T(8,128)(2,1)S(1)}, bf16[20,1024]{1,0:T(8,128)(2,1)S(1)}, u32[]{:S(2)}, u32[]{:S(2)}) collective-permute-start(bf16[20,1024]{1,0:T(8,128)(2,1)S(1)} %slice.19), channel_id=1, source_target_pairs={{8,0},{16,8},{24,16},{32,24},{40,32},{48,40},{56,48},{64,56},{72,6... | collective-permute-start | bytes 122888 | tf_op jit(solution)/shard_map/ppermute | solution.py:38
  15.4 26.0 %collective-permute-start = (bf16[28,1024]{1,0:T(8,128)(2,1)S(1)}, bf16[28,1024]{1,0:T(8,128)(2,1)S(1)}, u32[]{:S(2)}, u32[]{:S(2)}) collective-permute-start(bf16[28,1024]{1,0:T(8,128)(2,1)S(1)} %slice.18), channel_id=1, source_target_pairs={{0,8},{8,16},{16,24},{24,32},{32,40},{40,48},{48,56},{56,64},{64,7... | collective-permute-start | bytes 172040 | tf_op jit(solution)/shard_map/ppermute | solution.py:38
  32.3 9.1 %copy-start.2 = (bf16[256,1024]{1,0:T(8,128)(2,1)S(1)}, bf16[256,1024]{1,0:T(8,128)(2,1)}, u32[]{:S(2)}) copy-start(bf16[256,1024]{1,0:T(8,128)(2,1)} %param.7) | copy-start | bytes 1572868
  54.3 35.2 %all-to-all-start.1 = ((bf16[32,128,256]{2,1,0:T(8,128)(2,1)}), bf16[32,128,256]{2,1,0:T(8,128)(2,1)S(1)}, u32[]{:S(2)}, u32[]{:S(2)}) async-start(bf16[32,128,256]{2,1,0:T(8,128)(2,1)} %cut.1), calls=%async_computation.1 | async-start | bytes 4194304 | tf_op jit(solution)/shard_map/all_to_all | solution.py:430
  89.5 1.4 copy-start
  114.1 31.5 %all-to-all-start.2 = ((bf16[32,128,256]{2,1,0:T(8,128)(2,1)}), bf16[32,128,256]{2,1,0:T(8,128)(2,1)S(1)}, u32[]{:S(2)}, u32[]{:S(2)}) async-start(bf16[32,128,256]{2,1,0:T(8,128)(2,1)} %get-tuple-element.27), calls=%async_computation.2 | async-start | bytes 4194304 | tf_op jit(solution)/shard_map/all_to_all | solution.py:434
  145.6 1.3 copy-start.1
  173.4 6.9 %collective-permute-start.2 = (bf16[20,128]{1,0:T(8,128)(2,1)}, bf16[20,128]{1,0:T(8,128)(2,1)S(1)}, u32[]{:S(2)}, u32[]{:S(2)}) collective-permute-start(bf16[20,128]{1,0:T(8,128)(2,1)} %get-tuple-element.31), channel_id=1, source_target_pairs={{0,8},{8,16},{16,24},{24,32},{32,40},{40,48},{48,56},{56,64},{64,7... | collective-permute-start | bytes 15368 | tf_op jit(solution)/shard_map/ppermute | solution.py:38
  178.3 7.8 %collective-permute-start.3 = (bf16[20,128]{1,0:T(8,128)(2,1)}, bf16[20,128]{1,0:T(8,128)(2,1)S(1)}, u32[]{:S(2)}, u32[]{:S(2)}) collective-permute-start(bf16[20,128]{1,0:T(8,128)(2,1)} %get-tuple-element.32), channel_id=1, source_target_pairs={{8,0},{16,8},{24,16},{32,24},{40,32},{48,40},{56,48},{64,56},{72,6... | collective-permute-start | bytes 15368 | tf_op jit(solution)/shard_map/ppermute | solution.py:38
where the time goes:
time: 191 us; the launch traced here: 188 us
  Pallas kernels  84 us (44%)
  starting transfers between devices  37.2 us (19%)
  waiting for transfers between devices  24.7 us (13%)
  blocking collectives  16.9 us (9%)
  local copies, waits for them, and re-layouts  15.1 us (8%)
  other arithmetic  9.13 us (5%)
    pallas_call x1, Pallas kernels, build_taps(): pl.pallas_call(taps_kernel, grid=(cells,), in_specs=[pl.BlockSpec((1, REA...  28.2 us
    pallas_call x1, Pallas kernels, pieces(): pl.pallas_call(piece_kernel, grid_spec=pltpu.PrefetchScalarGridSpec(num_s...  23.2 us
    all_to_all x1, waiting for transfers between devices, shards(): lax.all_to_all(adjoints, 'sky', split_axis=0, concat_axis=0, tiled=True)  18.7 us
    all_to_all x1, blocking collectives, shards(): lax.all_to_all(partial, 'exp', split_axis=0, concat_axis=0, tiled=True)  16.9 us
    ppermute x4, starting transfers between devices, from_behind(): return lax.ppermute(x, axis, pairs)  14.8 us
    unnamed x9, local copies, waits for them, and re-layouts  8.31 us
    all_to_all x1, starting transfers between devices, shards(): lax.all_to_all(requests, 'sky', split_axis=0, concat_axis=0, tiled=True)  8.18 us
    all_to_all x1, starting transfers between devices, shards(): lax.all_to_all(adjoints, 'sky', split_axis=0, concat_axis=0, tiled=True)  7.28 us
  transfers between devices with their start and end apart: 7, of which 2 were waited for; matrix products, arithmetic and copies ran while one was open for 8% of the time, Pallas kernels for 21%

commit v1 on v0

--- a/solution.py
+++ b/solution.py
@@ -22,11 +22,13 @@
 PITCH = 72
 TILES = 6
 RES_LEAD = 40
+TAP_ROWS = 48
 BATCH = 4
 SLOTS = 8
 CHUNK = 9
 CHUNK_ROWS = 352
 SHIFT = 4
+VMEM_ALL = 60 << 20
 SMALL = pl.CostEstimate(flops=1000, bytes_accessed=1000, transcendentals=0)
 F32 = jnp.float32
 BF16 = jnp.bfloat16
@@ -49,15 +51,15 @@
     return x
 
 
-def regroup_kernel(data_ref, keep_ref, data_out, keep_out, scratch):
+def regroup_kernel(data_ref, keep_ref, out_ref, scratch):
     def per_piece(p, carry):
-        for source, target in ((data_ref, data_out), (keep_ref, keep_out)):
-            blocks = swap_groups(source[p].astype(F32).reshape(2 * OUT, 8, LANES))
-            scratch[...] = jnp.zeros_like(scratch)
-            for row in range(2 * OUT):
-                half = row % 2
-                scratch[pl.ds(EXT * (row // 2), 8), half * LANES : (half + 1) * LANES] = blocks[row]
-            target[p] = scratch[...].astype(BF16)
+        known = jnp.where(keep_ref[p] != 0, data_ref[p].astype(F32), jnp.inf)
+        blocks = swap_groups(known.reshape(2 * OUT, 8, LANES))
+        scratch[...] = jnp.full_like(scratch, jnp.inf)
+        for row in range(2 * OUT):
+            half = row % 2
+            scratch[pl.ds(EXT * (row // 2), 8), half * LANES : (half + 1) * LANES] = blocks[row]
+        out_ref[p] = scratch[...].astype(BF16)
         return carry
 
     lax.fori_loop(0, data_ref.shape[0], per_piece, 0)
@@ -66,67 +68,90 @@
 def regroup(exposure_data, pixel_mask):
     pieces = exposure_data.shape[0]
     block = pl.BlockSpec((BATCH, B, B), lambda p: (p, 0, 0))
-    out = pl.BlockSpec((BATCH, BLK_ROWS, 2 * LANES), lambda p: (p, 0, 0))
-    shape = jax.ShapeDtypeStruct((pieces, BLK_ROWS, 2 * LANES), BF16)
     return pl.pallas_call(
         regroup_kernel,
         grid=(pieces // BATCH,),
         in_specs=[block, block],
-        out_specs=[out, out],
-        out_shape=[shape, shape],
+        out_specs=pl.BlockSpec((BATCH, BLK_ROWS, 2 * LANES), lambda p: (p, 0, 0)),
+        out_shape=jax.ShapeDtypeStruct((pieces, BLK_ROWS, 2 * LANES), BF16),
         scratch_shapes=[pltpu.VMEM((BLK_ROWS, 2 * LANES), F32)],
         cost_estimate=SMALL,
         name="regroup",
     )(exposure_data, pixel_mask)
 
 
-def tap_rows(table):
-    cells = table.shape[0]
-    kernel = jnp.pad(table.reshape(cells, PSF, PSF), ((0, 0), (0, 7), (G, 23)))
-    kernel = kernel.reshape(cells, 24, 2, 5 * G).transpose(0, 2, 1, 3)
-    windows = [kernel[..., G * t : G * t + 2 * G].reshape(cells, 2, TILES * LANES) for t in range(REACH)]
-    return jnp.stack(windows, 1).astype(F32)
-
-
-def taps_kernel(rows_ref, out_ref):
+def taps_kernel(kernel_ref, out_ref, windows, rows):
     lane = lax.broadcasted_iota(jnp.int32, (G, LANES), 1)
     odd = (lane // G) % 2 == 1
-
-    def per_shift(t, carry):
-        before = jnp.zeros((G, LANES), BF16)
-        for tile in range(TILES):
-            lanes = slice(tile * LANES, (tile + 1) * LANES)
-            even_row, odd_row = (
-                jnp.broadcast_to(rows_ref[0, t, parity : parity + 1, lanes], (G, LANES))
-                for parity in range(2)
-            )
-            even_row = pltpu.roll(even_row, LANES - G, 1, stride=1, stride_axis=0)
-            odd_row = pltpu.roll(odd_row, 0, 1, stride=1, stride_axis=0)
-            now = jnp.where(odd, odd_row, even_row).astype(BF16)
-            for phase in range(8):
-                if phase == 0:
-                    part = now
-                else:
-                    part = pltpu.roll(jnp.where(lane < LANES - G * phase, now, before), G * phase, 1)
-                start = pl.multiple_of(t * LANES + phase * G, G)
-                out_ref[0, pl.ds(start, G), lanes] = part
-            before = now
-        return carry
-
-    lax.fori_loop(0, REACH, per_shift, 0)
-
-
-def build_taps(rows):
-    cells = rows.shape[0]
+    wide = lax.broadcasted_iota(jnp.int32, (TAP_ROWS, LANES), 1) // (2 * G)
+    quarter = lax.broadcasted_iota(jnp.int32, (TILES, LANES), 1) // (2 * G)
+
+    def flip(size):
+        first = lax.broadcasted_iota(jnp.int32, (size, size), 0)
+        second = lax.broadcasted_iota(jnp.int32, (size, size), 1)
+        return (first + second == PSF - 1).astype(BF16)
+
+    plain = kernel_ref[0]
+    turned = jnp.dot(flip(TAP_ROWS), plain, preferred_element_type=F32).astype(BF16)
+    turned = jnp.dot(turned, flip(LANES), preferred_element_type=F32)
+    for way, kernel in enumerate((turned, plain.astype(F32))):
+        spread = pltpu.roll(kernel, G, 1)
+        for t in range(1, REACH):
+            spread = jnp.where(wide == t, pltpu.roll(kernel, G * t + G, 1), spread)
+        windows[...] = spread
+        for parity in range(2):
+            picked = [windows[pl.ds(parity + 2 * q, TILES, stride=8), :] for q in range(4)]
+            for t in range(REACH):
+                row = picked[0] if t == 0 else pltpu.roll(picked[0], 2 * G * (4 - t), 1)
+                for q in range(1, 4):
+                    by = (q - t) % 4
+                    part = picked[q] if by == 0 else pltpu.roll(picked[q], 2 * G * by, 1)
+                    row = jnp.where(quarter == q, part, row)
+                rows[t, parity, :TILES, :] = row
+
+        def per_shift(t, carry):
+            before = [jnp.zeros((G, LANES), F32)] * 8
+            for tile in range(TILES):
+                even_row, odd_row = (
+                    jnp.broadcast_to(rows[t, parity, tile : tile + 1, :], (G, LANES))
+                    for parity in range(2)
+                )
+                even_row = pltpu.roll(even_row, LANES - G, 1, stride=1, stride_axis=0)
+                odd_row = pltpu.roll(odd_row, 0, 1, stride=1, stride_axis=0)
+                now = jnp.where(odd, odd_row, even_row)
+                turns = [now] + [pltpu.roll(now, G * phase, 1) for phase in range(1, 8)]
+                for phase in range(8):
+                    part = turns[phase]
+                    if phase > 0:
+                        part = jnp.where(lane < G * phase, before[phase], part)
+                    start = pl.multiple_of(t * LANES + phase * G, G)
+                    lanes = slice(tile * LANES, (tile + 1) * LANES)
+                    out_ref[way, 0, pl.ds(start, G), lanes] = part.astype(BF16)
+                before = turns
+            return carry
+
+        lax.fori_loop(0, REACH, per_shift, 0)
+
+
+def build_taps(table):
+    cells = table.shape[0]
+    kernels = jnp.pad(
+        table.reshape(cells, PSF, PSF), ((0, 0), (0, TAP_ROWS - PSF), (0, LANES - PSF))
+    )
     return pl.pallas_call(
         taps_kernel,
         grid=(cells,),
-        in_specs=[pl.BlockSpec((1, REACH, 2, TILES * LANES), lambda c: (c, 0, 0, 0))],
-        out_specs=pl.BlockSpec((1, REACH * LANES, TILES * LANES), lambda c: (c, 0, 0)),
-        out_shape=jax.ShapeDtypeStruct((cells, REACH * LANES, TILES * LANES), BF16),
+        in_specs=[pl.BlockSpec((1, TAP_ROWS, LANES), lambda c: (c, 0, 0))],
+        out_specs=pl.BlockSpec((2, 1, REACH * LANES, TILES * LANES), lambda c: (0, c, 0, 0)),
+        out_shape=jax.ShapeDtypeStruct((2, cells, REACH * LANES, TILES * LANES), BF16),
+        scratch_shapes=[
+            pltpu.VMEM((TAP_ROWS, LANES), F32),
+            pltpu.VMEM((REACH, 2, 8, LANES), F32),
+        ],
+        compiler_params=pltpu.CompilerParams(vmem_limit_bytes=VMEM_ALL),
         cost_estimate=SMALL,
         name="taps",
-    )(rows)
+    )(kernels)
 
 
 def blocks_kernel(stripe_ref, out_ref):
@@ -197,13 +222,13 @@
     for t in range(REACH):
         taps = slice(t * LANES, (t + 1) * LANES)
         for s in range(REACH - 1):
-            upper = taps_ref[0, taps, 2 * s * LANES : (2 * s + 2) * LANES]
+            upper = taps_ref[0, 0, taps, 2 * s * LANES : (2 * s + 2) * LANES]
             if s == 0:
                 lower = jnp.concatenate(
-                    [jnp.zeros((LANES, LANES), BF16), taps_ref[0, taps, 0:LANES]], axis=1
+                    [jnp.zeros((LANES, LANES), BF16), taps_ref[0, 0, taps, 0:LANES]], axis=1
                 )
             else:
-                lower = taps_ref[0, taps, (2 * s - 1) * LANES : (2 * s + 1) * LANES]
+                lower = taps_ref[0, 0, taps, (2 * s - 1) * LANES : (2 * s + 1) * LANES]
             total = total + jnp.dot(
                 read(s, t), jnp.concatenate([upper, lower], axis=0), preferred_element_type=F32
             )
@@ -212,13 +237,13 @@
         field = jnp.concatenate(
             [read(REACH - 1, t)[:, LANES:], read(REACH - 1, t + 1)[:, LANES:]], axis=1
         )
-        taps = taps_ref[0, t * LANES : (t + 2) * LANES, (TILES - 1) * LANES :]
+        taps = taps_ref[0, 0, t * LANES : (t + 2) * LANES, (TILES - 1) * LANES :]
         last = last + jnp.dot(field, taps, preferred_element_type=F32)
     return jnp.concatenate([total[:, :LANES] + last, total[:, LANES:]], axis=1)
 
 
 def piece_kernel(
-    slot_ref, cell_ref, patch_ref, forward_ref, adjoint_ref, data_ref, keep_ref, adj_out, res_out, field, resid
+    slot_ref, cell_ref, patch_ref, forward_ref, adjoint_ref, data_ref, adj_out, res_out, field, resid
 ):
     @pl.when(pl.program_id(0) == 0)
     def _():
@@ -232,8 +257,7 @@
 
     predicted = convolve(read_patch, forward_ref, FWD_ROWS)
     observed = data_ref[0, :FWD_ROWS].astype(F32)
-    keep = keep_ref[0, :FWD_ROWS].astype(F32)
-    residual = jnp.where(keep != 0, predicted - observed, 0.0).astype(BF16)
+    residual = jnp.where(observed < jnp.inf, predicted - observed, 0.0).astype(BF16)
     res_out[0, :FWD_ROWS] = residual
     resid[RES_LEAD : RES_LEAD + FWD_ROWS, :] = residual.astype(F32)
 
@@ -243,20 +267,19 @@
     adj_out[0] = convolve(read_residual, adjoint_ref, SLOT_ROWS).astype(BF16)
 
 
-def pieces(slots, cells, patches, all_taps, data, keep):
+def pieces(slots, cells, patches, taps, data):
     count = data.shape[0]
-    cell_count = all_taps.shape[0] // 2
     slot = pl.BlockSpec((1, SLOT_ROWS, 2 * LANES), lambda p, slots, cells: (slots[p], 0, 0))
-    taps_shape = (1, REACH * LANES, TILES * LANES)
-    forward = pl.BlockSpec(taps_shape, lambda p, slots, cells: (cells[p], 0, 0))
-    adjoint = pl.BlockSpec(taps_shape, lambda p, slots, cells: (cells[p] + cell_count, 0, 0))
+    taps_shape = (1, 1, REACH * LANES, TILES * LANES)
+    forward = pl.BlockSpec(taps_shape, lambda p, slots, cells: (0, cells[p], 0, 0))
+    adjoint = pl.BlockSpec(taps_shape, lambda p, slots, cells: (1, cells[p], 0, 0))
     block = pl.BlockSpec((1, BLK_ROWS, 2 * LANES), lambda p, slots, cells: (p, 0, 0))
     return pl.pallas_call(
         piece_kernel,
         grid_spec=pltpu.PrefetchScalarGridSpec(
             num_scalar_prefetch=2,
             grid=(count,),
-            in_specs=[slot, forward, adjoint, block, block],
+            in_specs=[slot, forward, adjoint, block],
             out_specs=[slot, block],
             scratch_shapes=[
                 pltpu.VMEM((SLOT_ROWS, 2 * LANES), F32),
@@ -269,7 +292,7 @@
         ],
         cost_estimate=SMALL,
         name="pieces",
-    )(slots, cells, patches, all_taps, all_taps, data, keep)
+    )(slots, cells, patches, taps, taps, data)
 
 
 def ungroup_kernel(res_ref, out_ref, scratch):
@@ -295,22 +318,18 @@
         out_specs=pl.BlockSpec((BATCH, B, B), lambda p: (p, 0, 0)),
         out_shape=jax.ShapeDtypeStruct((count, B, B), BF16),
         scratch_shapes=[pltpu.VMEM((BLK_ROWS, 2 * LANES), F32)],
+        compiler_params=pltpu.CompilerParams(vmem_limit_bytes=VMEM_ALL),
         cost_estimate=SMALL,
         name="ungroup",
     )(residual)
 
 
 def fold_kernel(per_row, half_rows, ids_ref, slot_ref, out_ref, canvas, scratch, packed):
-    step = pl.program_id(0)
-
-    @pl.when(step == 0)
-    def _():
-        canvas[...] = jnp.zeros_like(canvas)
-
+    canvas[...] = jnp.zeros_like(canvas)
     inside = lax.broadcasted_iota(jnp.int32, (G, LANES), 0) < EXT
 
     def per_slot(n, carry):
-        named = ids_ref[step * SLOTS + n]
+        named = ids_ref[n]
 
         @pl.when(named >= 0)
         def _():
@@ -326,32 +345,27 @@
 
         return carry
 
-    lax.fori_loop(0, SLOTS, per_slot, 0)
-
-    @pl.when(step == pl.num_programs(0) - 1)
-    def _():
-        for chunk in range(per_row):
-            first = OUT * chunk + 1
-            for row in range(half_rows):
-                packed[CHUNK * row : CHUNK * row + G, :] = canvas[row, first : first + G, :]
-            out_ref[chunk] = packed[...].astype(BF16)
+    lax.fori_loop(0, slot_ref.shape[0], per_slot, 0)
+    for chunk in range(per_row):
+        first = OUT * chunk + 1
+        for row in range(half_rows):
+            packed[CHUNK * row : CHUNK * row + G, :] = canvas[row, first : first + G, :]
+        out_ref[chunk] = packed[...].astype(BF16)
 
 
 def fold(ids, received, per_row, half_rows):
-    slots = ids.shape[0]
     return pl.pallas_call(
         lambda *refs: fold_kernel(per_row, half_rows, *refs),
-        grid_spec=pltpu.PrefetchScalarGridSpec(
-            num_scalar_prefetch=1,
-            grid=(slots // SLOTS,),
-            in_specs=[pl.BlockSpec((SLOTS, SLOT_ROWS, 2 * LANES), lambda n, ids: (n, 0, 0))],
-            out_specs=pl.BlockSpec((per_row, CHUNK_ROWS, LANES), lambda n, ids: (0, 0, 0)),
-            scratch_shapes=[
-                pltpu.VMEM((half_rows, PITCH + 8, LANES), F32),
-                pltpu.VMEM((SLOT_ROWS, 2 * LANES), F32),
-                pltpu.VMEM((CHUNK_ROWS, LANES), F32),
-            ],
-        ),
+        in_specs=[
+            pl.BlockSpec(memory_space=pltpu.SMEM),
+            pl.BlockSpec(memory_space=pltpu.VMEM),
+        ],
+        out_specs=pl.BlockSpec(memory_space=pltpu.VMEM),
+        scratch_shapes=[
+            pltpu.VMEM((half_rows, PITCH + 8, LANES), F32),
+            pltpu.VMEM((SLOT_ROWS, 2 * LANES), F32),
+            pltpu.VMEM((CHUNK_ROWS, LANES), F32),
+        ],
         out_shape=jax.ShapeDtypeStruct((per_row, CHUNK_ROWS, LANES), BF16),
         cost_estimate=SMALL,
         name="fold",
@@ -364,12 +378,19 @@
         total = total + terms_ref[term].astype(F32)
     summed[...] = total
     near = lax.broadcasted_iota(jnp.int32, (8, LANES), 1) < LANES - SHIFT
-    for row in range(half_rows):
-        first = CHUNK * row
-        tiles = swap_groups(summed[first : first + G, :].reshape(2, 8, LANES))
-        tile = pltpu.roll(tiles[0], LANES - SHIFT, 1)
-        edge = pltpu.roll(tiles[1], LANES - SHIFT, 1)
-        canvas[8 * row : 8 * row + 8, :] = jnp.where(near, tile, edge)
+    for first in range(0, half_rows, 8):
+        count = min(8, half_rows - first)
+        starts = [CHUNK * (first + row) for row in range(count)]
+        tiles = swap_groups(jnp.stack([summed[start : start + 8, :] for start in starts], 0))
+        edges = summed[pl.ds(starts[0] + 8, count, stride=CHUNK), :]
+        if count < 8:
+            edges = jnp.concatenate([edges, jnp.zeros((8 - count, LANES), F32)], axis=0)
+        edges = swap_groups(edges.reshape(1, 8, LANES)).reshape(8, LANES)
+        for row in range(count):
+            tile = pltpu.roll(tiles[row], LANES - SHIFT, 1)
+            edge = pltpu.roll(edges, (LANES - SHIFT - G * row) % LANES, 1)
+            start = 8 * (first + row)
+            canvas[start : start + 8, :] = jnp.where(near, tile, edge)
     middle = middle_out.shape[0]
     up_out[...] = canvas[:HALO, :].astype(BF16)
     middle_out[...] = canvas[HALO : HALO + middle, :]
@@ -419,18 +440,17 @@
     stripe = jnp.concatenate([above, sky_model, below], axis=0)
     stripe = jnp.pad(stripe, ((0, 0), (LEAD, PITCH * G - LEAD - stripe_cols)))
     blocks = stripe_blocks(stripe)
-    data, keep = regroup(exposure_data, pixel_mask)
     second = jnp.any(mine & (first[:, None] < code[None, :]), axis=0)
     slot_index = owner_sky * CAP + second.astype(jnp.int32)
-    rows = tap_rows(jnp.concatenate([psf_table[:, ::-1], psf_table], axis=0))
-    asked, blocks, data, keep, slot_index, rows = lax.optimization_barrier(
-        (asked, blocks, data, keep, slot_index, rows)
+    asked, blocks, slot_index = lax.optimization_barrier((asked, blocks, slot_index))
+    outgoing = cut_patches(asked, blocks, per_row)
+    exposure_data, pixel_mask, psf_table, _ = lax.optimization_barrier(
+        (exposure_data, pixel_mask, psf_table, outgoing)
     )
-    outgoing = cut_patches(asked, blocks, per_row)
     patches = lax.all_to_all(outgoing, "sky", split_axis=0, concat_axis=0, tiled=True)
-    rows, _ = lax.optimization_barrier((rows, outgoing))
-    taps = build_taps(rows)
-    adjoints, residuals = pieces(slot_index, psf_cell, patches, taps, data, keep)
+    taps = build_taps(psf_table)
+    data = regroup(exposure_data, pixel_mask)
+    adjoints, residuals = pieces(slot_index, psf_cell, patches, taps, data)
     received = lax.all_to_all(adjoints, "sky", split_axis=0, concat_axis=0, tiled=True)
     received, residual = lax.optimization_barrier((received, ungroup(residuals)))
 

time: 191 us -> 184 us (0.963); the launches traced: 188 us -> 183 us
  local copies, waits for them, and re-layouts: 15.1 us -> 7.11 us
  Pallas kernels: 84 us -> 87.3 us
    pallas_call x2, Pallas kernels: 33 us -> 39.8 us  [the longest x1 36.1 us: build_taps(): pl.pallas_call(taps_kernel, grid=(cells,), in_specs=[pl.BlockSpec((1, TAP...]
    unnamed x9 -> x6, local copies, waits for them, and re-layouts: 8.31 us -> 2.7 us
    pallas_call x1, Pallas kernels: 4.8 us -> 2.31 us  [finish(): pl.pallas_call(lambda *refs: finish_kernel(half_rows, *refs), in_specs=[v...]
  transfers between devices with their start and end apart: 7 -> 7, of which waited for: 2 -> 2; matrix products, arithmetic and copies ran while one was open for 8% -> 3% of each run, Pallas kernels for 21% -> 26%
where the time goes in v1:
time: 184 us; the launch traced here: 183 us
  Pallas kernels  87.3 us (47%)
  starting transfers between devices  37.8 us (21%)
  waiting for transfers between devices  24.6 us (13%)
  blocking collectives  17.3 us (9%)
  other arithmetic  8.05 us (4%)
  local copies, waits for them, and re-layouts  7.11 us (4%)
    pallas_call x1, Pallas kernels, build_taps(): pl.pallas_call(taps_kernel, grid=(cells,), in_specs=[pl.BlockSpec((1, TAP...  36.1 us
    pallas_call x1, Pallas kernels, pieces(): pl.pallas_call(piece_kernel, grid_spec=pltpu.PrefetchScalarGridSpec(num_s...  23 us
    all_to_all x1, waiting for transfers between devices, shards(): lax.all_to_all(adjoints, 'sky', split_axis=0, concat_axis=0, tiled=True)  18.7 us
    all_to_all x1, blocking collectives, shards(): lax.all_to_all(partial, 'exp', split_axis=0, concat_axis=0, tiled=True)  17.3 us
    ppermute x4, starting transfers between devices, from_behind(): return lax.ppermute(x, axis, pairs)  15.2 us
    all_to_all x1, starting transfers between devices, shards(): lax.all_to_all(requests, 'sky', split_axis=0, concat_axis=0, tiled=True)  8.18 us
    all_to_all x1, starting transfers between devices, shards(): lax.all_to_all(adjoints, 'sky', split_axis=0, concat_axis=0, tiled=True)  7.21 us
    all_to_all x1, starting transfers between devices, shards(): lax.all_to_all(outgoing, 'sky', split_axis=0, concat_axis=0, tiled=True)  7.2 us
  transfers between devices with their start and end apart: 7, of which 2 were waited for; matrix products, arithmetic and copies ran while one was open for 3% of the time, Pallas kernels for 26%

profile of v1, /device:TPU:24, one launch (start us, length us, event | category | flops | bytes accessed | tf_op | source)
XLA Modules:
  0.0 182.9 jit_solution(14178233921103270845)
XLA Ops:
  0.6 0.7 multiply_add_fusion
  1.3 0.8 select_reduce_fusion.1
  2.1 0.7 copy.12
  2.8 8.2 %all-to-all-start = ((s32[16,1,2]{2,1,0:T(1,128)}), s32[16,1,2]{2,1,0:T(1,128)S(1)}, u32[]{:S(2)}, u32[]{:S(2)}) async-start(s32[16,1,2]{2,1,0:T(1,128)} %copy.12), calls=%async_computation | async-start | bytes 16384 | tf_op jit(solution)/shard_map/all_to_all | solution.py:435
  11.0 0.8 slice.7
  11.8 2.8 %collective-permute-start.1 = (bf16[20,1024]{1,0:T(8,128)(2,1)S(1)}, bf16[20,1024]{1,0:T(8,128)(2,1)S(1)}, u32[]{:S(2)}, u32[]{:S(2)}) collective-permute-start(bf16[20,1024]{1,0:T(8,128)(2,1)S(1)} %slice.7), channel_id=1, source_target_pairs={{8,0},{16,8},{24,16},{32,24},{40,32},{48,40},{56,48},{64,56},{72,6... | collective-permute-start | bytes 122888 | tf_op jit(solution)/shard_map/ppermute | solution.py:40
  14.5 0.9 slice.6
  15.4 5.2 %collective-permute-start = (bf16[28,1024]{1,0:T(8,128)(2,1)S(1)}, bf16[28,1024]{1,0:T(8,128)(2,1)S(1)}, u32[]{:S(2)}, u32[]{:S(2)}) collective-permute-start(bf16[28,1024]{1,0:T(8,128)(2,1)S(1)} %slice.6), channel_id=1, source_target_pairs={{0,8},{8,16},{16,24},{24,32},{32,40},{40,48},{48,56},{56,64},{64,7... | collective-permute-start | bytes 172040 | tf_op jit(solution)/shard_map/ppermute | solution.py:40
  20.6 0.7 fusion.7
  21.3 1.2 convert_add_fusion.1.slot_ref
  22.6 0.0 all-to-all-done
  22.6 0.5 broadcast.135
  23.1 0.7 reduce.3
  23.8 0.0 collective-permute-done.1
  23.8 0.0 collective-permute-done
  23.8 2.4 %fusion.5.stripe_ref = bf16[304,1152]{1,0:T(8,128)(2,1)} fusion(bf16[20,1024]{1,0:T(8,128)(2,1)S(1)} %collective-permute-done.1, bf16[256,1024]{1,0:T(8,128)(2,1)} %param.7, bf16[28,1024]{1,0:T(8,128)(2,1)S(1)} %collective-permute-done), kind=kLoop, calls=%fused_computation.7 | loop fusion | flops 4202496 | bytes 1323008 | tf_op jit(solution)/shard_map/concatenate | solution.py:440
  26.1 0.6 reshape.108.refs_0_
  26.7 6.7 %blocks.1.refs_1_ = f32[38,72,128]{2,1,0:T(8,128)} custom-call(bf16[304,1152]{1,0:T(8,128)(2,1)} %fusion.5.stripe_ref), custom_call_target="tpu_custom_call" | custom-call | flops 1000 | bytes 1000 | tf_op jit(solution)/shard_map/blocks/pallas_call | solution.py:172
  33.5 4.2 %cut.1 = bf16[32,128,256]{2,1,0:T(8,128)(2,1)} custom-call(s32[32]{0:T(128)} %reshape.108.refs_0_, f32[38,72,128]{2,1,0:T(8,128)} %blocks.1.refs_1_), custom_call_target="tpu_custom_call" | custom-call | flops 1000 | bytes 1000 | tf_op jit(solution)/shard_map/cut/pallas_call | solution.py:205
  37.6 0.0 copy-start.2
  37.6 7.2 %all-to-all-start.1 = ((bf16[32,128,256]{2,1,0:T(8,128)(2,1)}), bf16[32,128,256]{2,1,0:T(8,128)(2,1)S(1)}, u32[]{:S(2)}, u32[]{:S(2)}) async-start(bf16[32,128,256]{2,1,0:T(8,128)(2,1)} %cut.1), calls=%async_computation.1 | async-start | bytes 4194304 | tf_op jit(solution)/shard_map/all_to_all | solution.py:450
  44.8 0.0 copy-done.2
  44.8 0.2 reshape.109
  45.1 0.7 pad.23.kernel_ref
  45.8 36.1 %taps.1.forward_ref.adjoint_ref = bf16[2,16,512,768]{3,2,1,0:T(8,128)(2,1)} custom-call(bf16[16,48,128]{2,1,0:T(8,128)(2,1)} %pad.23.kernel_ref), custom_call_target="tpu_custom_call" | custom-call | flops 1000 | bytes 1000 | tf_op jit(solution)/shard_map/taps/pallas_call | solution.py:141
  81.9 5.9 %regroup.1.data_ref = bf16[16,96,256]{2,1,0:T(8,128)(2,1)} custom-call(bf16[16,128,128]{2,1,0:T(8,128)(2,1)} %data_ref, s32[16,128,128]{2,1,0:T(8,128)} %keep_ref), custom_call_target="tpu_custom_call" | custom-call | flops 1000 | bytes 1000 | tf_op jit(solution)/shard_map/regroup/pallas_call | solution.py:71
  87.8 0.0 all-to-all-done.1.patch_ref
  87.8 0.0 copy-start
  87.8 1.4 copy-done
  89.2 23.0 %pieces.1 = (bf16[32,128,256]{2,1,0:T(8,128)(2,1)}, bf16[16,96,256]{2,1,0:T(8,128)(2,1)}) custom-call(s32[16]{0:T(128)} %convert_add_fusion.1.slot_ref, s32[16]{0:T(128)} %cell_ref.1, bf16[32,128,256]{2,1,0:T(8,128)(2,1)} %copy-done, bf16[2,16,512,768]{3,2,1,0:T(8,128)(2,1)} %taps.1.forward_ref.adjoint_ref, ...), custom_call_target="tpu_custom_call" | custom-call | flops 1000 | bytes 1000 | tf_op jit(solution)/shard_map/pieces/pallas_call | solution.py:277
  112.1 7.2 %all-to-all-start.2 = ((bf16[32,128,256]{2,1,0:T(8,128)(2,1)}), bf16[32,128,256]{2,1,0:T(8,128)(2,1)S(1)}, u32[]{:S(2)}, u32[]{:S(2)}) async-start(bf16[32,128,256]{2,1,0:T(8,128)(2,1)} %get-tuple-element.21), calls=%async_computation.2 | async-start | bytes 4194304 | tf_op jit(solution)/shard_map/all_to_all | solution.py:454
  119.4 5.5 %ungroup.1 = bf16[16,128,128]{2,1,0:T(8,128)(2,1)} custom-call(bf16[16,96,256]{2,1,0:T(8,128)(2,1)} %get-tuple-element.22.res_ref), custom_call_target="tpu_custom_call" | custom-call | flops 1000 | bytes 1000 | tf_op jit(solution)/shard_map/ungroup/pallas_call | solution.py:314
  124.9 18.7 %all-to-all-done.2.refs_1_ = bf16[32,128,256]{2,1,0:T(8,128)(2,1)S(1)} async-done(((bf16[32,128,256]{2,1,0:T(8,128)(2,1)}), bf16[32,128,256]{2,1,0:T(8,128)(2,1)S(1)}, u32[]{:S(2)}, u32[]{:S(2)}) %all-to-all-start.2) | async-done | bytes 2097184 | tf_op jit(solution)/shard_map/all_to_all | solution.py:454
  143.6 0.0 copy-start.1
  143.6 1.3 copy-done.1
  144.9 3.7 %fold.1 = bf16[8,352,128]{2,1,0:T(8,128)(2,1)} custom-call(s32[32]{0:T(128)} %reshape.108.refs_0_, bf16[32,128,256]{2,1,0:T(8,128)(2,1)} %copy-done.1), custom_call_target="tpu_custom_call" | custom-call | flops 1000 | bytes 1000 | tf_op jit(solution)/shard_map/fold/pallas_call | solution.py:357
  148.6 17.3 %all_to_all.24.refs_0_ = bf16[8,352,128]{2,1,0:T(8,128)(2,1)} all-to-all(bf16[8,352,128]{2,1,0:T(8,128)(2,1)} %fold.1), channel_id=1, replica_groups=mesh['sky'=16,'exp'=8] {'exp'}, dimensions={0} | all-to-all | bytes 1441792 | tf_op jit(solution)/shard_map/all_to_all | solution.py:459
  165.8 2.3 %finish.1 = (bf16[20,128]{1,0:T(8,128)(2,1)}, f32[256,128]{1,0:T(8,128)}, bf16[20,128]{1,0:T(8,128)(2,1)}) custom-call(bf16[8,352,128]{2,1,0:T(8,128)(2,1)} %all_to_all.24.refs_0_), custom_call_target="tpu_custom_call" | custom-call | flops 1000 | bytes 1000 | tf_op jit(solution)/shard_map/finish/pallas_call | solution.py:403
  168.2 5.4 %collective-permute-start.2 = (bf16[20,128]{1,0:T(8,128)(2,1)}, bf16[20,128]{1,0:T(8,128)(2,1)S(1)}, u32[]{:S(2)}, u32[]{:S(2)}) collective-permute-start(bf16[20,128]{1,0:T(8,128)(2,1)} %get-tuple-element.25), channel_id=1, source_target_pairs={{0,8},{8,16},{16,24},{24,32},{32,40},{40,48},{48,56},{56,64},{64,7... | collective-permute-start | bytes 15368 | tf_op jit(solution)/shard_map/ppermute | solution.py:40
  173.5 1.9 %collective-permute-start.3 = (bf16[20,128]{1,0:T(8,128)(2,1)}, bf16[20,128]{1,0:T(8,128)(2,1)S(1)}, u32[]{:S(2)}, u32[]{:S(2)}) collective-permute-start(bf16[20,128]{1,0:T(8,128)(2,1)} %get-tuple-element.26), channel_id=1, source_target_pairs={{8,0},{16,8},{24,16},{32,24},{40,32},{48,40},{56,48},{64,56},{72,6... | collective-permute-start | bytes 15368 | tf_op jit(solution)/shard_map/ppermute | solution.py:40
  175.5 0.0 collective-permute-done.2
  175.5 5.9 %collective-permute-done.3 = bf16[20,128]{1,0:T(8,128)(2,1)S(1)} collective-permute-done((bf16[20,128]{1,0:T(8,128)(2,1)}, bf16[20,128]{1,0:T(8,128)(2,1)S(1)}, u32[]{:S(2)}, u32[]{:S(2)}) %collective-permute-start.3) | collective-permute-done | bytes 5152 | tf_op jit(solution)/shard_map/ppermute | solution.py:40
  181.4 1.6 convert_add_fusion
  (2 shorter events, 0.0 us)
Async XLA Ops:
  2.8 19.8 %all-to-all-start = ((s32[16,1,2]{2,1,0:T(1,128)}), s32[16,1,2]{2,1,0:T(1,128)S(1)}, u32[]{:S(2)}, u32[]{:S(2)}) async-start(s32[16,1,2]{2,1,0:T(1,128)} %copy.12), calls=%async_computation | async-start | bytes 16384 | tf_op jit(solution)/shard_map/all_to_all | solution.py:435
  11.8 12.0 %collective-permute-start.1 = (bf16[20,1024]{1,0:T(8,128)(2,1)S(1)}, bf16[20,1024]{1,0:T(8,128)(2,1)S(1)}, u32[]{:S(2)}, u32[]{:S(2)}) collective-permute-start(bf16[20,1024]{1,0:T(8,128)(2,1)S(1)} %slice.7), channel_id=1, source_target_pairs={{8,0},{16,8},{24,16},{32,24},{40,32},{48,40},{56,48},{64,56},{72,6... | collective-permute-start | bytes 122888 | tf_op jit(solution)/shard_map/ppermute | solution.py:40
  15.4 8.4 %collective-permute-start = (bf16[28,1024]{1,0:T(8,128)(2,1)S(1)}, bf16[28,1024]{1,0:T(8,128)(2,1)S(1)}, u32[]{:S(2)}, u32[]{:S(2)}) collective-permute-start(bf16[28,1024]{1,0:T(8,128)(2,1)S(1)} %slice.6), channel_id=1, source_target_pairs={{0,8},{8,16},{16,24},{24,32},{32,40},{40,48},{48,56},{56,64},{64,7... | collective-permute-start | bytes 172040 | tf_op jit(solution)/shard_map/ppermute | solution.py:40
  37.6 7.2 %copy-start.2 = (bf16[16,1681]{1,0:T(8,128)(2,1)S(1)}, bf16[16,1681]{1,0:T(8,128)(2,1)}, u32[]{:S(2)}) copy-start(bf16[16,1681]{1,0:T(8,128)(2,1)} %param.13) | copy-start | bytes 161380
  37.6 50.2 %all-to-all-start.1 = ((bf16[32,128,256]{2,1,0:T(8,128)(2,1)}), bf16[32,128,256]{2,1,0:T(8,128)(2,1)S(1)}, u32[]{:S(2)}, u32[]{:S(2)}) async-start(bf16[32,128,256]{2,1,0:T(8,128)(2,1)} %cut.1), calls=%async_computation.1 | async-start | bytes 4194304 | tf_op jit(solution)/shard_map/all_to_all | solution.py:450
  87.8 1.4 copy-start
  112.1 31.4 %all-to-all-start.2 = ((bf16[32,128,256]{2,1,0:T(8,128)(2,1)}), bf16[32,128,256]{2,1,0:T(8,128)(2,1)S(1)}, u32[]{:S(2)}, u32[]{:S(2)}) async-start(bf16[32,128,256]{2,1,0:T(8,128)(2,1)} %get-tuple-element.21), calls=%async_computation.2 | async-start | bytes 4194304 | tf_op jit(solution)/shard_map/all_to_all | solution.py:454
  143.6 1.3 copy-start.1
  168.2 7.3 %collective-permute-start.2 = (bf16[20,128]{1,0:T(8,128)(2,1)}, bf16[20,128]{1,0:T(8,128)(2,1)S(1)}, u32[]{:S(2)}, u32[]{:S(2)}) collective-permute-start(bf16[20,128]{1,0:T(8,128)(2,1)} %get-tuple-element.25), channel_id=1, source_target_pairs={{0,8},{8,16},{16,24},{24,32},{32,40},{40,48},{48,56},{56,64},{64,7... | collective-permute-start | bytes 15368 | tf_op jit(solution)/shard_map/ppermute | solution.py:40
  173.5 7.8 %collective-permute-start.3 = (bf16[20,128]{1,0:T(8,128)(2,1)}, bf16[20,128]{1,0:T(8,128)(2,1)S(1)}, u32[]{:S(2)}, u32[]{:S(2)}) collective-permute-start(bf16[20,128]{1,0:T(8,128)(2,1)} %get-tuple-element.26), channel_id=1, source_target_pairs={{8,0},{16,8},{24,16},{32,24},{40,32},{48,40},{56,48},{64,56},{72,6... | collective-permute-start | bytes 15368 | tf_op jit(solution)/shard_map/ppermute | solution.py:40

commit v2 on v1

--- a/solution.py
+++ b/solution.py
@@ -15,7 +15,7 @@
 OUT = B // G
 EXT = 11
 REACH = 4
-LEAD = 28
+TAIL = 8
 FWD_ROWS = 88
 BLK_ROWS = 96
 SLOT_ROWS = 128
@@ -86,51 +86,43 @@
     wide = lax.broadcasted_iota(jnp.int32, (TAP_ROWS, LANES), 1) // (2 * G)
     quarter = lax.broadcasted_iota(jnp.int32, (TILES, LANES), 1) // (2 * G)
 
-    def flip(size):
-        first = lax.broadcasted_iota(jnp.int32, (size, size), 0)
-        second = lax.broadcasted_iota(jnp.int32, (size, size), 1)
-        return (first + second == PSF - 1).astype(BF16)
-
-    plain = kernel_ref[0]
-    turned = jnp.dot(flip(TAP_ROWS), plain, preferred_element_type=F32).astype(BF16)
-    turned = jnp.dot(turned, flip(LANES), preferred_element_type=F32)
-    for way, kernel in enumerate((turned, plain.astype(F32))):
-        spread = pltpu.roll(kernel, G, 1)
-        for t in range(1, REACH):
-            spread = jnp.where(wide == t, pltpu.roll(kernel, G * t + G, 1), spread)
-        windows[...] = spread
-        for parity in range(2):
-            picked = [windows[pl.ds(parity + 2 * q, TILES, stride=8), :] for q in range(4)]
-            for t in range(REACH):
-                row = picked[0] if t == 0 else pltpu.roll(picked[0], 2 * G * (4 - t), 1)
-                for q in range(1, 4):
-                    by = (q - t) % 4
-                    part = picked[q] if by == 0 else pltpu.roll(picked[q], 2 * G * by, 1)
-                    row = jnp.where(quarter == q, part, row)
-                rows[t, parity, :TILES, :] = row
-
-        def per_shift(t, carry):
-            before = [jnp.zeros((G, LANES), F32)] * 8
-            for tile in range(TILES):
-                even_row, odd_row = (
-                    jnp.broadcast_to(rows[t, parity, tile : tile + 1, :], (G, LANES))
-                    for parity in range(2)
-                )
-                even_row = pltpu.roll(even_row, LANES - G, 1, stride=1, stride_axis=0)
-                odd_row = pltpu.roll(odd_row, 0, 1, stride=1, stride_axis=0)
-                now = jnp.where(odd, odd_row, even_row)
-                turns = [now] + [pltpu.roll(now, G * phase, 1) for phase in range(1, 8)]
-                for phase in range(8):
-                    part = turns[phase]
-                    if phase > 0:
-                        part = jnp.where(lane < G * phase, before[phase], part)
-                    start = pl.multiple_of(t * LANES + phase * G, G)
-                    lanes = slice(tile * LANES, (tile + 1) * LANES)
-                    out_ref[way, 0, pl.ds(start, G), lanes] = part.astype(BF16)
-                before = turns
-            return carry
-
-        lax.fori_loop(0, REACH, per_shift, 0)
+    kernel = kernel_ref[0].astype(F32)
+    spread = pltpu.roll(kernel, G, 1)
+    for t in range(1, REACH):
+        spread = jnp.where(wide == t, pltpu.roll(kernel, G * t + G, 1), spread)
+    windows[...] = spread
+    for parity in range(2):
+        picked = [windows[pl.ds(parity + 2 * q, TILES, stride=8), :] for q in range(4)]
+        for t in range(REACH):
+            row = picked[0] if t == 0 else pltpu.roll(picked[0], 2 * G * (4 - t), 1)
+            for q in range(1, 4):
+                by = (q - t) % 4
+                part = picked[q] if by == 0 else pltpu.roll(picked[q], 2 * G * by, 1)
+                row = jnp.where(quarter == q, part, row)
+            rows[t, parity, :TILES, :] = row
+
+    def per_shift(t, carry):
+        before = [jnp.zeros((G, LANES), F32)] * 8
+        for tile in range(TILES):
+            even_row, odd_row = (
+                jnp.broadcast_to(rows[t, parity, tile : tile + 1, :], (G, LANES))
+                for parity in range(2)
+            )
+            even_row = pltpu.roll(even_row, LANES - G, 1, stride=1, stride_axis=0)
+            odd_row = pltpu.roll(odd_row, 0, 1, stride=1, stride_axis=0)
+            now = jnp.where(odd, odd_row, even_row)
+            turns = [now] + [pltpu.roll(now, G * phase, 1) for phase in range(1, 8)]
+            for phase in range(8):
+                part = turns[phase]
+                if phase > 0:
+                    part = jnp.where(lane < G * phase, before[phase], part)
+                start = pl.multiple_of(t * LANES + phase * G, G)
+                lanes = slice(tile * LANES, (tile + 1) * LANES)
+                out_ref[0, pl.ds(start, G), lanes] = part.astype(BF16)
+            before = turns
+        return carry
+
+    lax.fori_loop(0, REACH, per_shift, 0)
 
 
 def build_taps(table):
@@ -142,8 +134,8 @@
         taps_kernel,
         grid=(cells,),
         in_specs=[pl.BlockSpec((1, TAP_ROWS, LANES), lambda c: (c, 0, 0))],
-        out_specs=pl.BlockSpec((2, 1, REACH * LANES, TILES * LANES), lambda c: (0, c, 0, 0)),
-        out_shape=jax.ShapeDtypeStruct((2, cells, REACH * LANES, TILES * LANES), BF16),
+        out_specs=pl.BlockSpec((1, REACH * LANES, TILES * LANES), lambda c: (c, 0, 0)),
+        out_shape=jax.ShapeDtypeStruct((cells, REACH * LANES, TILES * LANES), BF16),
         scratch_shapes=[
             pltpu.VMEM((TAP_ROWS, LANES), F32),
             pltpu.VMEM((REACH, 2, 8, LANES), F32),
@@ -217,33 +209,64 @@
     )(ids, blocks)
 
 
+def block_taps(taps_ref, s, t):
+    taps = slice(t * LANES, (t + 1) * LANES)
+    upper = taps_ref[0, taps, 2 * s * LANES : (2 * s + 2) * LANES]
+    if s == 0:
+        lower = jnp.concatenate(
+            [jnp.zeros((LANES, LANES), BF16), taps_ref[0, taps, 0:LANES]], axis=1
+        )
+    else:
+        lower = taps_ref[0, taps, (2 * s - 1) * LANES : (2 * s + 1) * LANES]
+    return jnp.concatenate([upper, lower], axis=0)
+
+
+def last_taps(taps_ref, t):
+    return taps_ref[0, t * LANES : (t + 1) * LANES, (TILES - 1) * LANES :]
+
+
+def correlate(read, taps_ref, rows):
+    across = (((1,), (1,)), ((), ()))
+    total = jnp.zeros((rows, 2 * LANES), F32)
+    for t in range(REACH):
+        for s in range(REACH - 1):
+            total = total + lax.dot_general(
+                read(s, t), block_taps(taps_ref, s, t), across, preferred_element_type=F32
+            )
+    last = jnp.zeros((rows, LANES), F32)
+    for t in range(0, REACH, 2):
+        field = [read(REACH - 1, t + i)[:, :LANES] for i in range(2)]
+        taps = [last_taps(taps_ref, t + i) for i in range(2)]
+        last = last + lax.dot_general(
+            jnp.concatenate(field, axis=1),
+            jnp.concatenate(taps, axis=1),
+            across,
+            preferred_element_type=F32,
+        )
+    return jnp.concatenate([total[:, :LANES], total[:, LANES:] + last], axis=1)
+
+
 def convolve(read, taps_ref, rows):
     total = jnp.zeros((rows, 2 * LANES), F32)
     for t in range(REACH):
-        taps = slice(t * LANES, (t + 1) * LANES)
         for s in range(REACH - 1):
-            upper = taps_ref[0, 0, taps, 2 * s * LANES : (2 * s + 2) * LANES]
-            if s == 0:
-                lower = jnp.concatenate(
-                    [jnp.zeros((LANES, LANES), BF16), taps_ref[0, 0, taps, 0:LANES]], axis=1
-                )
-            else:
-                lower = taps_ref[0, 0, taps, (2 * s - 1) * LANES : (2 * s + 1) * LANES]
             total = total + jnp.dot(
-                read(s, t), jnp.concatenate([upper, lower], axis=0), preferred_element_type=F32
+                read(s, t), block_taps(taps_ref, s, t), preferred_element_type=F32
             )
     last = jnp.zeros((rows, LANES), F32)
     for t in range(0, REACH, 2):
-        field = jnp.concatenate(
-            [read(REACH - 1, t)[:, LANES:], read(REACH - 1, t + 1)[:, LANES:]], axis=1
+        field = [read(REACH - 1, t + i)[:, LANES:] for i in range(2)]
+        taps = [last_taps(taps_ref, t + i) for i in range(2)]
+        last = last + jnp.dot(
+            jnp.concatenate(field, axis=1),
+            jnp.concatenate(taps, axis=0),
+            preferred_element_type=F32,
         )
-        taps = taps_ref[0, 0, t * LANES : (t + 2) * LANES, (TILES - 1) * LANES :]
-        last = last + jnp.dot(field, taps, preferred_element_type=F32)
     return jnp.concatenate([total[:, :LANES] + last, total[:, LANES:]], axis=1)
 
 
 def piece_kernel(
-    slot_ref, cell_ref, patch_ref, forward_ref, adjoint_ref, data_ref, adj_out, res_out, field, resid
+    slot_ref, cell_ref, patch_ref, taps_ref, data_ref, adj_out, res_out, field, resid
 ):
     @pl.when(pl.program_id(0) == 0)
     def _():
@@ -252,10 +275,9 @@
     field[...] = patch_ref[0].astype(F32)
 
     def read_patch(s, t):
-        start = EXT * (REACH - 1 - s) + REACH - 1 - t
-        return field[pl.ds(start, FWD_ROWS), :].astype(BF16)
-
-    predicted = convolve(read_patch, forward_ref, FWD_ROWS)
+        return field[pl.ds(EXT * s + t, FWD_ROWS), :].astype(BF16)
+
+    predicted = correlate(read_patch, taps_ref, FWD_ROWS)
     observed = data_ref[0, :FWD_ROWS].astype(F32)
     residual = jnp.where(observed < jnp.inf, predicted - observed, 0.0).astype(BF16)
     res_out[0, :FWD_ROWS] = residual
@@ -264,22 +286,22 @@
     def read_residual(s, t):
         return resid[pl.ds(RES_LEAD - EXT * s - t, SLOT_ROWS), :].astype(BF16)
 
-    adj_out[0] = convolve(read_residual, adjoint_ref, SLOT_ROWS).astype(BF16)
+    adj_out[0] = convolve(read_residual, taps_ref, SLOT_ROWS).astype(BF16)
 
 
 def pieces(slots, cells, patches, taps, data):
     count = data.shape[0]
     slot = pl.BlockSpec((1, SLOT_ROWS, 2 * LANES), lambda p, slots, cells: (slots[p], 0, 0))
-    taps_shape = (1, 1, REACH * LANES, TILES * LANES)
-    forward = pl.BlockSpec(taps_shape, lambda p, slots, cells: (0, cells[p], 0, 0))
-    adjoint = pl.BlockSpec(taps_shape, lambda p, slots, cells: (1, cells[p], 0, 0))
+    cell = pl.BlockSpec(
+        (1, REACH * LANES, TILES * LANES), lambda p, slots, cells: (cells[p], 0, 0)
+    )
     block = pl.BlockSpec((1, BLK_ROWS, 2 * LANES), lambda p, slots, cells: (p, 0, 0))
     return pl.pallas_call(
         piece_kernel,
         grid_spec=pltpu.PrefetchScalarGridSpec(
             num_scalar_prefetch=2,
             grid=(count,),
-            in_specs=[slot, forward, adjoint, block],
+            in_specs=[slot, cell, block],
             out_specs=[slot, block],
             scratch_shapes=[
                 pltpu.VMEM((SLOT_ROWS, 2 * LANES), F32),
@@ -292,7 +314,7 @@
         ],
         cost_estimate=SMALL,
         name="pieces",
-    )(slots, cells, patches, taps, taps, data)
+    )(slots, cells, patches, taps, data)
 
 
 def ungroup_kernel(res_ref, out_ref, scratch):
@@ -435,10 +457,10 @@
     asked = lax.all_to_all(requests, "sky", split_axis=0, concat_axis=0, tiled=True)
     asked = asked.reshape(sky_count * CAP)
 
-    above = from_behind(sky_model[stripe_rows - LEAD :], "sky", 1)
+    above = from_behind(sky_model[stripe_rows - HALO :], "sky", 1)
     below = from_behind(sky_model[:HALO], "sky", -1)
     stripe = jnp.concatenate([above, sky_model, below], axis=0)
-    stripe = jnp.pad(stripe, ((0, 0), (LEAD, PITCH * G - LEAD - stripe_cols)))
+    stripe = jnp.pad(stripe, ((0, TAIL), (HALO, PITCH * G - HALO - stripe_cols)))
     blocks = stripe_blocks(stripe)
     second = jnp.any(mine & (first[:, None] < code[None, :]), axis=0)
     slot_index = owner_sky * CAP + second.astype(jnp.int32)
@@ -454,7 +476,7 @@
     received = lax.all_to_all(adjoints, "sky", split_axis=0, concat_axis=0, tiled=True)
     received, residual = lax.optimization_barrier((received, ungroup(residuals)))
 
-    half_rows = (stripe_rows + LEAD + HALO) // 8
+    half_rows = (stripe_rows + 2 * HALO + TAIL) // 8
     partial = fold(asked, received, per_row, half_rows)
     terms = lax.all_to_all(partial, "exp", split_axis=0, concat_axis=0, tiled=True)
     up, middle, down = finish(terms, half_rows, stripe_rows)

time: 184 us -> 169 us (0.918)
  Pallas kernels: 87.3 us -> 71.5 us
  waiting for transfers between devices: 24.6 us -> 28 us
    pallas_call x1, Pallas kernels: 36.1 us -> 16.9 us  [build_taps(): pl.pallas_call(taps_kernel, grid=(cells,), in_specs=[pl.BlockSpec((1, TAP...]
    pallas_call x1, Pallas kernels: 23 us -> 26.3 us  [pieces(): pl.pallas_call(piece_kernel, grid_spec=pltpu.PrefetchScalarGridSpec(num_s...]
    ppermute x4, waiting for transfers between devices: 5.91 us -> 8.38 us  [from_behind(): return lax.ppermute(x, axis, pairs)]
  transfers between devices with their start and end apart: 7 -> 7, of which waited for: 2 -> 3; matrix products, arithmetic and copies ran while one was open for 3% -> 3% of each run, Pallas kernels for 26% -> 17%
where the time goes in v2:
time: 169 us; the launch traced here: 168 us
  Pallas kernels  71.5 us (42%)
  starting transfers between devices  36.5 us (22%)
  waiting for transfers between devices  28 us (17%)
  blocking collectives  17 us (10%)
  other arithmetic  7.98 us (5%)
  local copies, waits for them, and re-layouts  6.27 us (4%)
    pallas_call x1, Pallas kernels, pieces(): pl.pallas_call(piece_kernel, grid_spec=pltpu.PrefetchScalarGridSpec(num_s...  26.3 us
    all_to_all x1, waiting for transfers between devices, shards(): lax.all_to_all(adjoints, 'sky', split_axis=0, concat_axis=0, tiled=True)  19.6 us
    all_to_all x1, blocking collectives, shards(): lax.all_to_all(partial, 'exp', split_axis=0, concat_axis=0, tiled=True)  17 us
    pallas_call x1, Pallas kernels, build_taps(): pl.pallas_call(taps_kernel, grid=(cells,), in_specs=[pl.BlockSpec((1, TAP...  16.9 us
    ppermute x4, starting transfers between devices, from_behind(): return lax.ppermute(x, axis, pairs)  13.9 us
    ppermute x4, waiting for transfers between devices, from_behind(): return lax.ppermute(x, axis, pairs)  8.38 us
    all_to_all x1, starting transfers between devices, shards(): lax.all_to_all(requests, 'sky', split_axis=0, concat_axis=0, tiled=True)  8.18 us
    all_to_all x1, starting transfers between devices, shards(): lax.all_to_all(adjoints, 'sky', split_axis=0, concat_axis=0, tiled=True)  7.61 us
  transfers between devices with their start and end apart: 7, of which 3 were waited for; matrix products, arithmetic and copies ran while one was open for 3% of the time, Pallas kernels for 17%

profile of v2, /device:TPU:24, one launch (start us, length us, event | category | flops | bytes accessed | tf_op | source)
XLA Modules:
  0.0 168.1 jit_solution(2432619157181188052)
XLA Ops:
  0.6 0.7 multiply_add_fusion
  1.3 0.8 select_reduce_fusion.1
  2.1 0.7 copy.12
  2.8 8.2 %all-to-all-start = ((s32[16,1,2]{2,1,0:T(1,128)}), s32[16,1,2]{2,1,0:T(1,128)S(1)}, u32[]{:S(2)}, u32[]{:S(2)}) async-start(s32[16,1,2]{2,1,0:T(1,128)} %copy.12), calls=%async_computation | async-start | bytes 16384 | tf_op jit(solution)/shard_map/all_to_all | solution.py:457
  11.0 0.8 fusion.14
  11.8 3.4 %collective-permute-start = (bf16[20,1024]{1,0:T(8,128)(2,1)S(1)}, bf16[20,1024]{1,0:T(8,128)(2,1)S(1)}, u32[]{:S(2)}, u32[]{:S(2)}) collective-permute-start(bf16[20,1024]{1,0:T(8,128)(2,1)S(1)} %get-tuple-element.30), channel_id=1, source_target_pairs={{0,8},{8,16},{16,24},{24,32},{32,40},{40,48},{48,56},{56,64},{64,7... | collective-permute-start | bytes 122888 | tf_op jit(solution)/shard_map/ppermute | solution.py:40
  15.2 2.5 %collective-permute-start.1 = (bf16[20,1024]{1,0:T(8,128)(2,1)S(1)}, bf16[20,1024]{1,0:T(8,128)(2,1)S(1)}, u32[]{:S(2)}, u32[]{:S(2)}) collective-permute-start(bf16[20,1024]{1,0:T(8,128)(2,1)S(1)} %get-tuple-element.31), channel_id=1, source_target_pairs={{8,0},{16,8},{24,16},{32,24},{40,32},{48,40},{56,48},{64,56},{72,6... | collective-permute-start | bytes 122888 | tf_op jit(solution)/shard_map/ppermute | solution.py:40
  17.7 0.7 fusion.11
  18.4 1.2 convert_add_fusion.1.slot_ref
  19.6 0.0 all-to-all-done
  19.6 0.5 broadcast.142
  20.1 0.7 reduce.3
  20.8 0.0 collective-permute-done
  20.8 2.5 %collective-permute-done.1 = bf16[20,1024]{1,0:T(8,128)(2,1)S(1)} collective-permute-done((bf16[20,1024]{1,0:T(8,128)(2,1)S(1)}, bf16[20,1024]{1,0:T(8,128)(2,1)S(1)}, u32[]{:S(2)}, u32[]{:S(2)}) %collective-permute-start.1) | collective-permute-done | bytes 40992 | tf_op jit(solution)/shard_map/ppermute | solution.py:40
  23.3 2.3 %fusion.7.stripe_ref = bf16[304,1152]{1,0:T(8,128)(2,1)} fusion(bf16[20,1024]{1,0:T(8,128)(2,1)S(1)} %collective-permute-done.1, bf16[256,1024]{1,0:T(8,128)(2,1)} %param.7, bf16[20,1024]{1,0:T(8,128)(2,1)S(1)} %collective-permute-done), kind=kLoop, calls=%fused_computation.10 | loop fusion | flops 5953536 | bytes 1306624 | tf_op jit(solution)/shard_map/concatenate | solution.py:462
  25.6 0.6 reshape.108.refs_0_
  26.2 6.7 %blocks.1.refs_1_ = f32[38,72,128]{2,1,0:T(8,128)} custom-call(bf16[304,1152]{1,0:T(8,128)(2,1)} %fusion.7.stripe_ref), custom_call_target="tpu_custom_call" | custom-call | flops 1000 | bytes 1000 | tf_op jit(solution)/shard_map/blocks/pallas_call | solution.py:164
  32.9 4.2 %cut.1 = bf16[32,128,256]{2,1,0:T(8,128)(2,1)} custom-call(s32[32]{0:T(128)} %reshape.108.refs_0_, f32[38,72,128]{2,1,0:T(8,128)} %blocks.1.refs_1_), custom_call_target="tpu_custom_call" | custom-call | flops 1000 | bytes 1000 | tf_op jit(solution)/shard_map/cut/pallas_call | solution.py:197
  37.2 0.0 copy-start.2
  37.2 6.8 %all-to-all-start.1 = ((bf16[32,128,256]{2,1,0:T(8,128)(2,1)}), bf16[32,128,256]{2,1,0:T(8,128)(2,1)S(1)}, u32[]{:S(2)}, u32[]{:S(2)}) async-start(bf16[32,128,256]{2,1,0:T(8,128)(2,1)} %cut.1), calls=%async_computation.1 | async-start | bytes 4194304 | tf_op jit(solution)/shard_map/all_to_all | solution.py:472
  44.0 0.0 copy-done.2
  44.0 0.2 reshape.109
  44.2 0.7 pad.23.kernel_ref
  44.9 16.9 %taps.1.taps_ref = bf16[16,512,768]{2,1,0:T(8,128)(2,1)} custom-call(bf16[16,48,128]{2,1,0:T(8,128)(2,1)} %pad.23.kernel_ref), custom_call_target="tpu_custom_call" | custom-call | flops 1000 | bytes 1000 | tf_op jit(solution)/shard_map/taps/pallas_call | solution.py:133
  61.9 5.9 %regroup.1.data_ref = bf16[16,96,256]{2,1,0:T(8,128)(2,1)} custom-call(bf16[16,128,128]{2,1,0:T(8,128)(2,1)} %data_ref, s32[16,128,128]{2,1,0:T(8,128)} %keep_ref), custom_call_target="tpu_custom_call" | custom-call | flops 1000 | bytes 1000 | tf_op jit(solution)/shard_map/regroup/pallas_call | solution.py:71
  67.8 0.0 all-to-all-done.1.patch_ref
  67.8 0.0 copy-start.1
  67.8 1.3 copy-done.1
  69.1 26.3 %pieces.1 = (bf16[32,128,256]{2,1,0:T(8,128)(2,1)}, bf16[16,96,256]{2,1,0:T(8,128)(2,1)}) custom-call(s32[16]{0:T(128)} %convert_add_fusion.1.slot_ref, s32[16]{0:T(128)} %cell_ref.1, bf16[32,128,256]{2,1,0:T(8,128)(2,1)} %copy-done.1, bf16[16,512,768]{2,1,0:T(8,128)(2,1)} %taps.1.taps_ref, bf16[16,96,256]{2,1,0:T(8,128)(2,1)} %regroup.1.data_ref), custom_call_target="tpu_custom_call" | custom-call | flops 1000 | bytes 1000 | tf_op jit(solution)/shard_map/pieces/pallas_call | solution.py:299
  95.5 7.6 %all-to-all-start.2 = ((bf16[32,128,256]{2,1,0:T(8,128)(2,1)}), bf16[32,128,256]{2,1,0:T(8,128)(2,1)S(1)}, u32[]{:S(2)}, u32[]{:S(2)}) async-start(bf16[32,128,256]{2,1,0:T(8,128)(2,1)} %get-tuple-element.21), calls=%async_computation.2 | async-start | bytes 4194304 | tf_op jit(solution)/shard_map/all_to_all | solution.py:476
  103.1 5.5 %ungroup.1 = bf16[16,128,128]{2,1,0:T(8,128)(2,1)} custom-call(bf16[16,96,256]{2,1,0:T(8,128)(2,1)} %get-tuple-element.22.res_ref), custom_call_target="tpu_custom_call" | custom-call | flops 1000 | bytes 1000 | tf_op jit(solution)/shard_map/ungroup/pallas_call | solution.py:336
  108.6 19.6 %all-to-all-done.2.refs_1_ = bf16[32,128,256]{2,1,0:T(8,128)(2,1)S(1)} async-done(((bf16[32,128,256]{2,1,0:T(8,128)(2,1)}), bf16[32,128,256]{2,1,0:T(8,128)(2,1)S(1)}, u32[]{:S(2)}, u32[]{:S(2)}) %all-to-all-start.2) | async-done | bytes 2097184 | tf_op jit(solution)/shard_map/all_to_all | solution.py:476
  128.1 0.0 copy-start
  128.1 1.4 copy-done
  129.5 3.6 %fold.1 = bf16[8,352,128]{2,1,0:T(8,128)(2,1)} custom-call(s32[32]{0:T(128)} %reshape.108.refs_0_, bf16[32,128,256]{2,1,0:T(8,128)(2,1)} %copy-done), custom_call_target="tpu_custom_call" | custom-call | flops 1000 | bytes 1000 | tf_op jit(solution)/shard_map/fold/pallas_call | solution.py:379
  133.1 17.0 %all_to_all.24.refs_0_ = bf16[8,352,128]{2,1,0:T(8,128)(2,1)} all-to-all(bf16[8,352,128]{2,1,0:T(8,128)(2,1)} %fold.1), channel_id=1, replica_groups=mesh['sky'=16,'exp'=8] {'exp'}, dimensions={0} | all-to-all | bytes 1441792 | tf_op jit(solution)/shard_map/all_to_all | solution.py:481
  150.1 2.3 %finish.1 = (bf16[20,128]{1,0:T(8,128)(2,1)}, f32[256,128]{1,0:T(8,128)}, bf16[20,128]{1,0:T(8,128)(2,1)}) custom-call(bf16[8,352,128]{2,1,0:T(8,128)(2,1)} %all_to_all.24.refs_0_), custom_call_target="tpu_custom_call" | custom-call | flops 1000 | bytes 1000 | tf_op jit(solution)/shard_map/finish/pallas_call | solution.py:425
  152.5 6.2 %collective-permute-start.2 = (bf16[20,128]{1,0:T(8,128)(2,1)}, bf16[20,128]{1,0:T(8,128)(2,1)S(1)}, u32[]{:S(2)}, u32[]{:S(2)}) collective-permute-start(bf16[20,128]{1,0:T(8,128)(2,1)} %get-tuple-element.25), channel_id=1, source_target_pairs={{0,8},{8,16},{16,24},{24,32},{32,40},{40,48},{48,56},{56,64},{64,7... | collective-permute-start | bytes 15368 | tf_op jit(solution)/shard_map/ppermute | solution.py:40
  158.7 1.9 %collective-permute-start.3 = (bf16[20,128]{1,0:T(8,128)(2,1)}, bf16[20,128]{1,0:T(8,128)(2,1)S(1)}, u32[]{:S(2)}, u32[]{:S(2)}) collective-permute-start(bf16[20,128]{1,0:T(8,128)(2,1)} %get-tuple-element.26), channel_id=1, source_target_pairs={{8,0},{16,8},{24,16},{32,24},{40,32},{48,40},{56,48},{64,56},{72,6... | collective-permute-start | bytes 15368 | tf_op jit(solution)/shard_map/ppermute | solution.py:40
  160.6 0.0 collective-permute-done.2
  160.6 5.9 %collective-permute-done.3 = bf16[20,128]{1,0:T(8,128)(2,1)S(1)} collective-permute-done((bf16[20,128]{1,0:T(8,128)(2,1)}, bf16[20,128]{1,0:T(8,128)(2,1)S(1)}, u32[]{:S(2)}, u32[]{:S(2)}) %collective-permute-start.3) | collective-permute-done | bytes 5152 | tf_op jit(solution)/shard_map/ppermute | solution.py:40
  166.5 1.6 convert_add_fusion
  (2 shorter events, 0.0 us)
Async XLA Ops:
  2.8 16.8 %all-to-all-start = ((s32[16,1,2]{2,1,0:T(1,128)}), s32[16,1,2]{2,1,0:T(1,128)S(1)}, u32[]{:S(2)}, u32[]{:S(2)}) async-start(s32[16,1,2]{2,1,0:T(1,128)} %copy.12), calls=%async_computation | async-start | bytes 16384 | tf_op jit(solution)/shard_map/all_to_all | solution.py:457
  11.8 9.0 %collective-permute-start = (bf16[20,1024]{1,0:T(8,128)(2,1)S(1)}, bf16[20,1024]{1,0:T(8,128)(2,1)S(1)}, u32[]{:S(2)}, u32[]{:S(2)}) collective-permute-start(bf16[20,1024]{1,0:T(8,128)(2,1)S(1)} %get-tuple-element.30), channel_id=1, source_target_pairs={{0,8},{8,16},{16,24},{24,32},{32,40},{40,48},{48,56},{56,64},{64,7... | collective-permute-start | bytes 122888 | tf_op jit(solution)/shard_map/ppermute | solution.py:40
  15.2 8.1 %collective-permute-start.1 = (bf16[20,1024]{1,0:T(8,128)(2,1)S(1)}, bf16[20,1024]{1,0:T(8,128)(2,1)S(1)}, u32[]{:S(2)}, u32[]{:S(2)}) collective-permute-start(bf16[20,1024]{1,0:T(8,128)(2,1)S(1)} %get-tuple-element.31), channel_id=1, source_target_pairs={{8,0},{16,8},{24,16},{32,24},{40,32},{48,40},{56,48},{64,56},{72,6... | collective-permute-start | bytes 122888 | tf_op jit(solution)/shard_map/ppermute | solution.py:40
  37.2 6.8 %copy-start.2 = (bf16[16,1681]{1,0:T(8,128)(2,1)S(1)}, bf16[16,1681]{1,0:T(8,128)(2,1)}, u32[]{:S(2)}) copy-start(bf16[16,1681]{1,0:T(8,128)(2,1)} %param.13) | copy-start | bytes 161380
  37.2 30.6 %all-to-all-start.1 = ((bf16[32,128,256]{2,1,0:T(8,128)(2,1)}), bf16[32,128,256]{2,1,0:T(8,128)(2,1)S(1)}, u32[]{:S(2)}, u32[]{:S(2)}) async-start(bf16[32,128,256]{2,1,0:T(8,128)(2,1)} %cut.1), calls=%async_computation.1 | async-start | bytes 4194304 | tf_op jit(solution)/shard_map/all_to_all | solution.py:472
  67.8 1.3 copy-start.1
  95.5 32.7 %all-to-all-start.2 = ((bf16[32,128,256]{2,1,0:T(8,128)(2,1)}), bf16[32,128,256]{2,1,0:T(8,128)(2,1)S(1)}, u32[]{:S(2)}, u32[]{:S(2)}) async-start(bf16[32,128,256]{2,1,0:T(8,128)(2,1)} %get-tuple-element.21), calls=%async_computation.2 | async-start | bytes 4194304 | tf_op jit(solution)/shard_map/all_to_all | solution.py:476
  128.1 1.4 copy-start
  152.5 8.1 %collective-permute-start.2 = (bf16[20,128]{1,0:T(8,128)(2,1)}, bf16[20,128]{1,0:T(8,128)(2,1)S(1)}, u32[]{:S(2)}, u32[]{:S(2)}) collective-permute-start(bf16[20,128]{1,0:T(8,128)(2,1)} %get-tuple-element.25), channel_id=1, source_target_pairs={{0,8},{8,16},{16,24},{24,32},{32,40},{40,48},{48,56},{56,64},{64,7... | collective-permute-start | bytes 15368 | tf_op jit(solution)/shard_map/ppermute | solution.py:40
  158.7 7.8 %collective-permute-start.3 = (bf16[20,128]{1,0:T(8,128)(2,1)}, bf16[20,128]{1,0:T(8,128)(2,1)S(1)}, u32[]{:S(2)}, u32[]{:S(2)}) collective-permute-start(bf16[20,128]{1,0:T(8,128)(2,1)} %get-tuple-element.26), channel_id=1, source_target_pairs={{8,0},{16,8},{24,16},{32,24},{40,32},{48,40},{56,48},{64,56},{72,6... | collective-permute-start | bytes 15368 | tf_op jit(solution)/shard_map/ppermute | solution.py:40

commit v3 on v2

--- a/solution.py
+++ b/solution.py
@@ -16,22 +16,29 @@
 EXT = 11
 REACH = 4
 TAIL = 8
-FWD_ROWS = 88
-BLK_ROWS = 96
+BLOCKS = OUT * OUT
 SLOT_ROWS = 128
 PITCH = 72
 TILES = 6
 RES_LEAD = 40
 TAP_ROWS = 48
+OWN_FIRST = 3
 BATCH = 4
 SLOTS = 8
 CHUNK = 9
 CHUNK_ROWS = 352
 SHIFT = 4
-VMEM_ALL = 60 << 20
 SMALL = pl.CostEstimate(flops=1000, bytes_accessed=1000, transcendentals=0)
 F32 = jnp.float32
 BF16 = jnp.bfloat16
+
+
+def whole_vmem():
+    return pl.BlockSpec(memory_space=pltpu.VMEM)
+
+
+def on_chip(x):
+    return pltpu.with_memory_space_constraint(x, pltpu.VMEM)
 
 
 def from_behind(x, axis, by):
@@ -51,15 +58,14 @@
     return x
 
 
-def regroup_kernel(data_ref, keep_ref, out_ref, scratch):
+def regroup_kernel(data_ref, keep_ref, out_ref):
     def per_piece(p, carry):
         known = jnp.where(keep_ref[p] != 0, data_ref[p].astype(F32), jnp.inf)
-        blocks = swap_groups(known.reshape(2 * OUT, 8, LANES))
-        scratch[...] = jnp.full_like(scratch, jnp.inf)
-        for row in range(2 * OUT):
-            half = row % 2
-            scratch[pl.ds(EXT * (row // 2), 8), half * LANES : (half + 1) * LANES] = blocks[row]
-        out_ref[p] = scratch[...].astype(BF16)
+        blocks = swap_groups(known.reshape(2 * OUT, 8, LANES)).reshape(OUT, 2, 8, LANES)
+        for half in range(2):
+            out_ref[p, :, half * LANES : (half + 1) * LANES] = (
+                blocks[:, half].reshape(BLOCKS, LANES).astype(BF16)
+            )
         return carry
 
     lax.fori_loop(0, data_ref.shape[0], per_piece, 0)
@@ -72,9 +78,8 @@
         regroup_kernel,
         grid=(pieces // BATCH,),
         in_specs=[block, block],
-        out_specs=pl.BlockSpec((BATCH, BLK_ROWS, 2 * LANES), lambda p: (p, 0, 0)),
-        out_shape=jax.ShapeDtypeStruct((pieces, BLK_ROWS, 2 * LANES), BF16),
-        scratch_shapes=[pltpu.VMEM((BLK_ROWS, 2 * LANES), F32)],
+        out_specs=pl.BlockSpec((BATCH, BLOCKS, 2 * LANES), lambda p: (p, 0, 0)),
+        out_shape=jax.ShapeDtypeStruct((pieces, BLOCKS, 2 * LANES), BF16),
         cost_estimate=SMALL,
         name="regroup",
     )(exposure_data, pixel_mask)
@@ -140,39 +145,64 @@
             pltpu.VMEM((TAP_ROWS, LANES), F32),
             pltpu.VMEM((REACH, 2, 8, LANES), F32),
         ],
-        compiler_params=pltpu.CompilerParams(vmem_limit_bytes=VMEM_ALL),
         cost_estimate=SMALL,
         name="taps",
     )(kernels)
 
 
-def blocks_kernel(stripe_ref, out_ref):
-    def per_row(r, carry):
-        start = pl.multiple_of(r * G, G)
-        for tile in range(PITCH // 8):
-            part = stripe_ref[pl.ds(start, G), tile * LANES : (tile + 1) * LANES].astype(F32)
-            out_ref[pl.ds(2 * r, 2), tile * 8 : (tile + 1) * 8, :] = swap_groups(
-                part.reshape(2, 8, LANES)
-            )
-        return carry
-
-    lax.fori_loop(0, stripe_ref.shape[0] // G, per_row, 0)
-
-
-def stripe_blocks(stripe):
-    rows = stripe.shape[0] // 8
-    return pl.pallas_call(
-        blocks_kernel,
-        out_shape=jax.ShapeDtypeStruct((rows, PITCH, LANES), F32),
+def row_blocks(pixels):
+    far = lax.broadcasted_iota(jnp.int32, (8, LANES), 1) >= HALO
+    tiles = pixels.shape[1] // LANES
+    empty = jnp.zeros((8, LANES), F32)
+    turned = [
+        pltpu.roll(pixels[:, tile * LANES : (tile + 1) * LANES], HALO, 1) for tile in range(tiles)
+    ]
+    before, after = [empty] + turned, turned + [empty]
+    moved = [jnp.where(far, now, old) for old, now in zip(before, after)]
+    return swap_groups(jnp.stack(moved, 0)).reshape((tiles + 1) * 8, LANES)
+
+
+def own_kernel(stripe_ref, out_ref, pixels):
+    skip = 8 * OWN_FIRST - HALO
+    pixels[...] = stripe_ref[...].astype(F32)
+
+    for row in range(out_ref.shape[0]):
+        out_ref[row] = row_blocks(pixels[skip + 8 * row : skip + 8 * row + 8, :])
+
+
+def own_blocks(stripe):
+    rows, columns = stripe.shape
+    count = (rows + HALO) // 8 - OWN_FIRST
+    return pl.pallas_call(
+        own_kernel,
         in_specs=[pl.BlockSpec(memory_space=pltpu.VMEM)],
         out_specs=pl.BlockSpec(memory_space=pltpu.VMEM),
-        cost_estimate=SMALL,
-        name="blocks",
+        out_shape=pltpu.VMEM((count, PITCH, LANES), F32),
+        scratch_shapes=[pltpu.VMEM((rows, columns), F32)],
+        cost_estimate=SMALL,
+        name="own",
     )(stripe)
 
 
-def cut_kernel(per_row, ids_ref, blocks_ref, out_ref, scratch):
+def cut_kernel(
+    per_row, ids_ref, own_ref, above_ref, top_ref, bottom_ref, below_ref, out_ref, blocks, upper, lower, scratch
+):
     step = pl.program_id(0)
+
+    @pl.when(step == 0)
+    def _():
+        own = own_ref.shape[0]
+        blocks[OWN_FIRST : OWN_FIRST + own] = own_ref[...]
+        missing = 8 * OWN_FIRST - HALO
+        upper[:HALO, :] = above_ref[...].astype(F32)
+        upper[HALO:, :] = top_ref[...].astype(F32)[:missing]
+        for row in range(OWN_FIRST):
+            blocks[row] = row_blocks(upper[8 * row : 8 * row + 8, :])
+        lower[...] = jnp.zeros_like(lower)
+        lower[:missing, :] = bottom_ref[...].astype(F32)[G - missing :]
+        lower[missing : missing + HALO, :] = below_ref[...].astype(F32)
+        for row in range(lower.shape[0] // 8):
+            blocks[OWN_FIRST + own + row] = row_blocks(lower[8 * row : 8 * row + 8, :])
 
     def per_slot(n, carry):
         wanted = ids_ref[step * SLOTS + n]
@@ -183,7 +213,7 @@
             first_col = pl.multiple_of(wanted % per_row * OUT, 8)
             for row in range(EXT):
                 for half in range(2):
-                    part = blocks_ref[first_row + 2 * row + half, pl.ds(first_col, G), :]
+                    part = blocks[first_row + 2 * row + half, pl.ds(first_col, G), :]
                     scratch[pl.ds(EXT * row, G), half * LANES : (half + 1) * LANES] = part
             out_ref[n] = scratch[...].astype(BF16)
 
@@ -192,21 +222,34 @@
     lax.fori_loop(0, SLOTS, per_slot, 0)
 
 
-def cut_patches(ids, blocks, per_row):
+def cut_patches(ids, own, stripe, above, below, half_rows):
     slots = ids.shape[0]
-    return pl.pallas_call(
-        lambda *refs: cut_kernel(per_row, *refs),
+    rows, columns = stripe.shape
+    last = rows // G - 1
+    return pl.pallas_call(
+        lambda *refs: cut_kernel(columns // B, *refs),
         grid_spec=pltpu.PrefetchScalarGridSpec(
             num_scalar_prefetch=1,
             grid=(slots // SLOTS,),
-            in_specs=[pl.BlockSpec(blocks.shape, lambda n, ids: (0, 0, 0))],
+            in_specs=[
+                whole_vmem(),
+                whole_vmem(),
+                pl.BlockSpec((G, columns), lambda n, ids: (0, 0)),
+                pl.BlockSpec((G, columns), lambda n, ids: (last, 0)),
+                whole_vmem(),
+            ],
             out_specs=pl.BlockSpec((SLOTS, SLOT_ROWS, 2 * LANES), lambda n, ids: (n, 0, 0)),
-            scratch_shapes=[pltpu.VMEM((SLOT_ROWS, 2 * LANES), F32)],
+            scratch_shapes=[
+                pltpu.VMEM((half_rows, PITCH, LANES), F32),
+                pltpu.VMEM((8 * OWN_FIRST, columns), F32),
+                pltpu.VMEM((8 * (half_rows - OWN_FIRST - own.shape[0]), columns), F32),
+                pltpu.VMEM((SLOT_ROWS, 2 * LANES), F32),
+            ],
         ),
         out_shape=jax.ShapeDtypeStruct((slots, SLOT_ROWS, 2 * LANES), BF16),
         cost_estimate=SMALL,
         name="cut",
-    )(ids, blocks)
+    )(ids, on_chip(own), on_chip(above), stripe, stripe, on_chip(below))
 
 
 def block_taps(taps_ref, s, t):
@@ -265,23 +308,27 @@
     return jnp.concatenate([total[:, :LANES] + last, total[:, LANES:]], axis=1)
 
 
-def piece_kernel(
-    slot_ref, cell_ref, patch_ref, taps_ref, data_ref, adj_out, res_out, field, resid
-):
-    @pl.when(pl.program_id(0) == 0)
+def piece_kernel(slot_ref, cell_ref, patch_ref, taps_ref, data_ref, adj_out, res_out, field, resid):
+    piece = pl.program_id(0)
+
+    @pl.when(piece == 0)
     def _():
         resid[...] = jnp.zeros_like(resid)
 
-    field[...] = patch_ref[0].astype(F32)
+    field[...] = patch_ref[slot_ref[piece]].astype(F32)
 
     def read_patch(s, t):
-        return field[pl.ds(EXT * s + t, FWD_ROWS), :].astype(BF16)
-
-    predicted = correlate(read_patch, taps_ref, FWD_ROWS)
-    observed = data_ref[0, :FWD_ROWS].astype(F32)
+        starts = [EXT * (row + s) + t for row in range(OUT)]
+        return jnp.concatenate([field[at : at + OUT, :] for at in starts], axis=0).astype(BF16)
+
+    predicted = correlate(read_patch, taps_ref, BLOCKS)
+    observed = data_ref[0].astype(F32)
     residual = jnp.where(observed < jnp.inf, predicted - observed, 0.0).astype(BF16)
-    res_out[0, :FWD_ROWS] = residual
-    resid[RES_LEAD : RES_LEAD + FWD_ROWS, :] = residual.astype(F32)
+    res_out[0] = residual
+    wide = residual.astype(F32)
+    for row in range(OUT):
+        first = RES_LEAD + EXT * row
+        resid[first : first + OUT, :] = wide[OUT * row : OUT * (row + 1)]
 
     def read_residual(s, t):
         return resid[pl.ds(RES_LEAD - EXT * s - t, SLOT_ROWS), :].astype(BF16)
@@ -295,13 +342,13 @@
     cell = pl.BlockSpec(
         (1, REACH * LANES, TILES * LANES), lambda p, slots, cells: (cells[p], 0, 0)
     )
-    block = pl.BlockSpec((1, BLK_ROWS, 2 * LANES), lambda p, slots, cells: (p, 0, 0))
+    block = pl.BlockSpec((1, BLOCKS, 2 * LANES), lambda p, slots, cells: (p, 0, 0))
     return pl.pallas_call(
         piece_kernel,
         grid_spec=pltpu.PrefetchScalarGridSpec(
             num_scalar_prefetch=2,
             grid=(count,),
-            in_specs=[slot, cell, block],
+            in_specs=[whole_vmem(), cell, block],
             out_specs=[slot, block],
             scratch_shapes=[
                 pltpu.VMEM((SLOT_ROWS, 2 * LANES), F32),
@@ -314,18 +361,17 @@
         ],
         cost_estimate=SMALL,
         name="pieces",
-    )(slots, cells, patches, taps, data)
-
-
-def ungroup_kernel(res_ref, out_ref, scratch):
+    )(slots, cells, on_chip(patches), taps, data)
+
+
+def ungroup_kernel(res_ref, out_ref):
     def per_piece(p, carry):
-        scratch[...] = res_ref[p].astype(F32)
-        for row in range(OUT):
-            halves = [
-                scratch[pl.ds(EXT * row, 8), half * LANES : (half + 1) * LANES] for half in range(2)
-            ]
-            rows = swap_groups(jnp.stack(halves, 0)).reshape(G, LANES)
-            out_ref[p, row * G : (row + 1) * G, :] = rows.astype(BF16)
+        halves = [
+            res_ref[p, :, half * LANES : (half + 1) * LANES].astype(F32).reshape(OUT, 8, LANES)
+            for half in range(2)
+        ]
+        pixels = swap_groups(jnp.stack(halves, 1).reshape(2 * OUT, 8, LANES))
+        out_ref[p] = pixels.reshape(B, LANES).astype(BF16)
         return carry
 
     lax.fori_loop(0, res_ref.shape[0], per_piece, 0)
@@ -336,11 +382,9 @@
     return pl.pallas_call(
         ungroup_kernel,
         grid=(count // BATCH,),
-        in_specs=[pl.BlockSpec((BATCH, BLK_ROWS, 2 * LANES), lambda p: (p, 0, 0))],
+        in_specs=[pl.BlockSpec((BATCH, BLOCKS, 2 * LANES), lambda p: (p, 0, 0))],
         out_specs=pl.BlockSpec((BATCH, B, B), lambda p: (p, 0, 0)),
         out_shape=jax.ShapeDtypeStruct((count, B, B), BF16),
-        scratch_shapes=[pltpu.VMEM((BLK_ROWS, 2 * LANES), F32)],
-        compiler_params=pltpu.CompilerParams(vmem_limit_bytes=VMEM_ALL),
         cost_estimate=SMALL,
         name="ungroup",
     )(residual)
@@ -391,7 +435,7 @@
         out_shape=jax.ShapeDtypeStruct((per_row, CHUNK_ROWS, LANES), BF16),
         cost_estimate=SMALL,
         name="fold",
-    )(ids, received)
+    )(ids, on_chip(received))
 
 
 def finish_kernel(half_rows, terms_ref, up_out, middle_out, down_out, summed, canvas):
@@ -459,24 +503,22 @@
 
     above = from_behind(sky_model[stripe_rows - HALO :], "sky", 1)
     below = from_behind(sky_model[:HALO], "sky", -1)
-    stripe = jnp.concatenate([above, sky_model, below], axis=0)
-    stripe = jnp.pad(stripe, ((0, TAIL), (HALO, PITCH * G - HALO - stripe_cols)))
-    blocks = stripe_blocks(stripe)
+    half_rows = (stripe_rows + 2 * HALO + TAIL) // 8
+    own = own_blocks(sky_model)
+    asked, own = lax.optimization_barrier((asked, own))
+    outgoing = cut_patches(asked, own, sky_model, above, below, half_rows)
+    exposure_data, pixel_mask, psf_table, code, _ = lax.optimization_barrier(
+        (exposure_data, pixel_mask, psf_table, code, outgoing)
+    )
     second = jnp.any(mine & (first[:, None] < code[None, :]), axis=0)
     slot_index = owner_sky * CAP + second.astype(jnp.int32)
-    asked, blocks, slot_index = lax.optimization_barrier((asked, blocks, slot_index))
-    outgoing = cut_patches(asked, blocks, per_row)
-    exposure_data, pixel_mask, psf_table, _ = lax.optimization_barrier(
-        (exposure_data, pixel_mask, psf_table, outgoing)
-    )
     patches = lax.all_to_all(outgoing, "sky", split_axis=0, concat_axis=0, tiled=True)
+    data = regroup(exposure_data, pixel_mask)
     taps = build_taps(psf_table)
-    data = regroup(exposure_data, pixel_mask)
     adjoints, residuals = pieces(slot_index, psf_cell, patches, taps, data)
     received = lax.all_to_all(adjoints, "sky", split_axis=0, concat_axis=0, tiled=True)
     received, residual = lax.optimization_barrier((received, ungroup(residuals)))
 
-    half_rows = (stripe_rows + 2 * HALO + TAIL) // 8
     partial = fold(asked, received, per_row, half_rows)
     terms = lax.all_to_all(partial, "exp", split_axis=0, concat_axis=0, tiled=True)
     up, middle, down = finish(terms, half_rows, stripe_rows)

time: 169 us -> 164 us (0.970)
  other arithmetic: 7.98 us -> 4.31 us
  starting transfers between devices: 36.5 us -> 39.7 us
  local copies, waits for them, and re-layouts: 6.27 us -> 3.59 us
    unnamed x6 -> x4, local copies, waits for them, and re-layouts: 2.69 us -> 0.01 us
    ppermute x4, starting transfers between devices: 13.9 us -> 16.5 us  [from_behind(): return lax.ppermute(x, axis, pairs)]
    ppermute x4, waiting for transfers between devices: 8.38 us -> 5.91 us  [from_behind(): return lax.ppermute(x, axis, pairs)]
    concatenate x1 -> x0, other arithmetic: 2.34 us -> none  [shards(): stripe = jnp.concatenate([above, sky_model, below], axis=0)]
  transfers between devices with their start and end apart: 7 -> 7, of which waited for: 3 -> 3; matrix products, arithmetic and copies ran while one was open for 3% -> 3% of each run, Pallas kernels for 17% -> 22%
where the time goes in v3:
time: 164 us
  Pallas kernels  71.1 us (43%)
  starting transfers between devices  39.7 us (24%)
  waiting for transfers between devices  27.1 us (17%)
  blocking collectives  17.1 us (10%)
  other arithmetic  4.31 us (3%)
  local copies, waits for them, and re-layouts  3.59 us (2%)
    pallas_call x1, Pallas kernels, pieces(): pl.pallas_call(piece_kernel, grid_spec=pltpu.PrefetchScalarGridSpec(num_s...  26.1 us
    all_to_all x1, waiting for transfers between devices, shards(): lax.all_to_all(adjoints, 'sky', split_axis=0, concat_axis=0, tiled=True)  20.4 us
    all_to_all x1, blocking collectives, shards(): lax.all_to_all(partial, 'exp', split_axis=0, concat_axis=0, tiled=True)  17.1 us
    pallas_call x1, Pallas kernels, build_taps(): pl.pallas_call(taps_kernel, grid=(cells,), in_specs=[pl.BlockSpec((1, TAP...  16.9 us
    ppermute x4, starting transfers between devices, from_behind(): return lax.ppermute(x, axis, pairs)  16.5 us
    all_to_all x1, starting transfers between devices, shards(): lax.all_to_all(adjoints, 'sky', split_axis=0, concat_axis=0, tiled=True)  7.99 us
    all_to_all x1, starting transfers between devices, shards(): lax.all_to_all(requests, 'sky', split_axis=0, concat_axis=0, tiled=True)  7.84 us
    pallas_call x1, Pallas kernels, own_blocks(): pl.pallas_call(own_kernel, in_specs=[pl.BlockSpec(memory_space=pltpu.VMEM...  7.52 us
  transfers between devices with their start and end apart: 7, of which 3 were waited for; matrix products, arithmetic and copies ran while one was open for 3% of the time, Pallas kernels for 22%

profile of v3, /device:TPU:24, one launch (start us, length us, event | category | flops | bytes accessed | tf_op | source)
XLA Modules:
  0.0 163.6 jit_solution(16499481617698342238)
XLA Ops:
  0.6 0.8 fusion.4
  1.5 2.7 %collective-permute-start.1 = (bf16[20,1024]{1,0:T(8,128)(2,1)S(1)}, bf16[20,1024]{1,0:T(8,128)(2,1)S(1)}, u32[]{:S(2)}, u32[]{:S(2)}) collective-permute-start(bf16[20,1024]{1,0:T(8,128)(2,1)S(1)} %get-tuple-element.30), channel_id=1, source_target_pairs={{8,0},{16,8},{24,16},{32,24},{40,32},{48,40},{56,48},{64,56},{72,6... | collective-permute-start | bytes 122888 | tf_op jit(solution)/shard_map/ppermute | solution.py:47
  4.1 5.3 %collective-permute-start = (bf16[20,1024]{1,0:T(8,128)(2,1)S(1)}, bf16[20,1024]{1,0:T(8,128)(2,1)S(1)}, u32[]{:S(2)}, u32[]{:S(2)}) collective-permute-start(bf16[20,1024]{1,0:T(8,128)(2,1)S(1)} %get-tuple-element.31), channel_id=1, source_target_pairs={{0,8},{8,16},{16,24},{24,32},{32,40},{40,48},{48,56},{56,64},{64,7... | collective-permute-start | bytes 122888 | tf_op jit(solution)/shard_map/ppermute | solution.py:47
  9.4 0.7 multiply_add_fusion
  10.1 0.8 select_reduce_fusion.1
  10.9 0.7 copy.12
  11.6 7.8 %all-to-all-start = ((s32[16,1,2]{2,1,0:T(1,128)}), s32[16,1,2]{2,1,0:T(1,128)S(1)}, u32[]{:S(2)}, u32[]{:S(2)}) async-start(s32[16,1,2]{2,1,0:T(1,128)} %copy.12), calls=%async_computation | async-start | bytes 16384 | tf_op jit(solution)/shard_map/all_to_all | solution.py:501
  19.4 7.5 %own.1.refs_1_ = f32[31,72,128]{2,1,0:T(8,128)S(1)} custom-call(bf16[256,1024]{1,0:T(8,128)(2,1)} %refs_4_.1), custom_call_target="tpu_custom_call" | custom-call | flops 1000 | bytes 1000 | tf_op jit(solution)/shard_map/own/pallas_call | solution.py:176
  26.9 0.0 all-to-all-done
  27.0 0.5 broadcast.122
  27.5 0.7 reduce.3
  28.1 0.6 reshape.109.refs_0_
  28.8 0.0 collective-permute-done.1.refs_5_
  28.8 0.0 collective-permute-done.refs_2_
  28.8 4.2 %cut.1 = bf16[32,128,256]{2,1,0:T(8,128)(2,1)} custom-call(s32[32]{0:T(128)} %reshape.109.refs_0_, f32[31,72,128]{2,1,0:T(8,128)S(1)} %own.1.refs_1_, bf16[20,1024]{1,0:T(8,128)(2,1)S(1)} %collective-permute-done.refs_2_, bf16[256,1024]{1,0:T(8,128)(2,1)} %refs_4_.1, bf16[256,1024]{1,0:T(8,128)(2,1)} %refs_4_.1, ...), custom_call_target="tpu_custom_call" | custom-call | flops 1000 | bytes 1000 | tf_op jit(solution)/shard_map/cut/pallas_call | solution.py:229
  32.9 0.0 copy-start
  32.9 7.4 %all-to-all-start.1 = ((bf16[32,128,256]{2,1,0:T(8,128)(2,1)}), bf16[32,128,256]{2,1,0:T(8,128)(2,1)S(1)}, u32[]{:S(2)}, u32[]{:S(2)}) async-start(bf16[32,128,256]{2,1,0:T(8,128)(2,1)} %cut.1), calls=%async_computation.1 | async-start | bytes 4194304 | tf_op jit(solution)/shard_map/all_to_all | solution.py:515
  40.3 0.0 copy-done
  40.3 0.2 reshape.110
  40.5 0.7 pad.18.kernel_ref
  41.2 16.9 %taps.1.taps_ref = bf16[16,512,768]{2,1,0:T(8,128)(2,1)} custom-call(bf16[16,48,128]{2,1,0:T(8,128)(2,1)} %pad.18.kernel_ref), custom_call_target="tpu_custom_call" | custom-call | flops 1000 | bytes 1000 | tf_op jit(solution)/shard_map/taps/pallas_call | solution.py:138
  58.2 0.0 copy-start.1
  58.2 5.7 %regroup.1.data_ref = bf16[16,64,256]{2,1,0:T(8,128)(2,1)} custom-call(bf16[16,128,128]{2,1,0:T(8,128)(2,1)} %data_ref, s32[16,128,128]{2,1,0:T(8,128)} %keep_ref), custom_call_target="tpu_custom_call" | custom-call | flops 1000 | bytes 1000 | tf_op jit(solution)/shard_map/regroup/pallas_call | solution.py:77
  63.9 0.0 copy-done.1
  63.9 0.1 fusion.1
  64.0 0.5 convert_add_fusion.1.slot_ref
  64.5 0.8 all-to-all-done.1.patch_ref
  65.3 26.1 %pieces.1 = (bf16[32,128,256]{2,1,0:T(8,128)(2,1)}, bf16[16,64,256]{2,1,0:T(8,128)(2,1)}) custom-call(s32[16]{0:T(128)} %convert_add_fusion.1.slot_ref, s32[16]{0:T(128)} %cell_ref.1, bf16[32,128,256]{2,1,0:T(8,128)(2,1)S(1)} %all-to-all-done.1.patch_ref, bf16[16,512,768]{2,1,0:T(8,128)(2,1)} %taps.1.taps_ref, bf16[16,64,256]{2,1,0:T(8,128)(2,1)} %regroup.1.data_ref), custom_call_target="tpu_custom_call" | custom-call | flops 1000 | bytes 1000 | tf_op jit(solution)/shard_map/pieces/pallas_call | solution.py:346
  91.4 8.0 %all-to-all-start.2 = ((bf16[32,128,256]{2,1,0:T(8,128)(2,1)}), bf16[32,128,256]{2,1,0:T(8,128)(2,1)S(1)}, u32[]{:S(2)}, u32[]{:S(2)}) async-start(bf16[32,128,256]{2,1,0:T(8,128)(2,1)} %get-tuple-element.21), calls=%async_computation.2 | async-start | bytes 4194304 | tf_op jit(solution)/shard_map/all_to_all | solution.py:519
  99.4 5.5 %ungroup.1 = bf16[16,128,128]{2,1,0:T(8,128)(2,1)} custom-call(bf16[16,64,256]{2,1,0:T(8,128)(2,1)} %get-tuple-element.22.res_ref), custom_call_target="tpu_custom_call" | custom-call | flops 1000 | bytes 1000 | tf_op jit(solution)/shard_map/ungroup/pallas_call | solution.py:382
  104.9 20.4 %all-to-all-done.2.refs_1_ = bf16[32,128,256]{2,1,0:T(8,128)(2,1)S(1)} async-done(((bf16[32,128,256]{2,1,0:T(8,128)(2,1)}), bf16[32,128,256]{2,1,0:T(8,128)(2,1)S(1)}, u32[]{:S(2)}, u32[]{:S(2)}) %all-to-all-start.2) | async-done | bytes 2097184 | tf_op jit(solution)/shard_map/all_to_all | solution.py:519
  125.3 2.8 %fold.1 = bf16[8,352,128]{2,1,0:T(8,128)(2,1)} custom-call(s32[32]{0:T(128)} %reshape.109.refs_0_, bf16[32,128,256]{2,1,0:T(8,128)(2,1)S(1)} %all-to-all-done.2.refs_1_), custom_call_target="tpu_custom_call" | custom-call | flops 1000 | bytes 1000 | tf_op jit(solution)/shard_map/fold/pallas_call | solution.py:423
  128.1 17.1 %all_to_all.24.refs_0_ = bf16[8,352,128]{2,1,0:T(8,128)(2,1)} all-to-all(bf16[8,352,128]{2,1,0:T(8,128)(2,1)} %fold.1), channel_id=1, replica_groups=mesh['sky'=16,'exp'=8] {'exp'}, dimensions={0} | all-to-all | bytes 1441792 | tf_op jit(solution)/shard_map/all_to_all | solution.py:523
  145.2 2.3 %finish.1 = (bf16[20,128]{1,0:T(8,128)(2,1)}, f32[256,128]{1,0:T(8,128)}, bf16[20,128]{1,0:T(8,128)(2,1)}) custom-call(bf16[8,352,128]{2,1,0:T(8,128)(2,1)} %all_to_all.24.refs_0_), custom_call_target="tpu_custom_call" | custom-call | flops 1000 | bytes 1000 | tf_op jit(solution)/shard_map/finish/pallas_call | solution.py:469
  147.5 6.6 %collective-permute-start.2 = (bf16[20,128]{1,0:T(8,128)(2,1)}, bf16[20,128]{1,0:T(8,128)(2,1)S(1)}, u32[]{:S(2)}, u32[]{:S(2)}) collective-permute-start(bf16[20,128]{1,0:T(8,128)(2,1)} %get-tuple-element.25), channel_id=1, source_target_pairs={{0,8},{8,16},{16,24},{24,32},{32,40},{40,48},{48,56},{56,64},{64,7... | collective-permute-start | bytes 15368 | tf_op jit(solution)/shard_map/ppermute | solution.py:47
  154.2 1.9 %collective-permute-start.3 = (bf16[20,128]{1,0:T(8,128)(2,1)}, bf16[20,128]{1,0:T(8,128)(2,1)S(1)}, u32[]{:S(2)}, u32[]{:S(2)}) collective-permute-start(bf16[20,128]{1,0:T(8,128)(2,1)} %get-tuple-element.26), channel_id=1, source_target_pairs={{8,0},{16,8},{24,16},{32,24},{40,32},{48,40},{56,48},{64,56},{72,6... | collective-permute-start | bytes 15368 | tf_op jit(solution)/shard_map/ppermute | solution.py:47
  156.1 0.0 collective-permute-done.2
  156.1 5.9 %collective-permute-done.3 = bf16[20,128]{1,0:T(8,128)(2,1)S(1)} collective-permute-done((bf16[20,128]{1,0:T(8,128)(2,1)}, bf16[20,128]{1,0:T(8,128)(2,1)S(1)}, u32[]{:S(2)}, u32[]{:S(2)}) %collective-permute-start.3) | collective-permute-done | bytes 5152 | tf_op jit(solution)/shard_map/ppermute | solution.py:47
  162.0 1.6 convert_add_fusion
  (2 shorter events, 0.0 us)
Async XLA Ops:
  1.5 27.3 %collective-permute-start.1 = (bf16[20,1024]{1,0:T(8,128)(2,1)S(1)}, bf16[20,1024]{1,0:T(8,128)(2,1)S(1)}, u32[]{:S(2)}, u32[]{:S(2)}) collective-permute-start(bf16[20,1024]{1,0:T(8,128)(2,1)S(1)} %get-tuple-element.30), channel_id=1, source_target_pairs={{8,0},{16,8},{24,16},{32,24},{40,32},{48,40},{56,48},{64,56},{72,6... | collective-permute-start | bytes 122888 | tf_op jit(solution)/shard_map/ppermute | solution.py:47
  4.1 24.6 %collective-permute-start = (bf16[20,1024]{1,0:T(8,128)(2,1)S(1)}, bf16[20,1024]{1,0:T(8,128)(2,1)S(1)}, u32[]{:S(2)}, u32[]{:S(2)}) collective-permute-start(bf16[20,1024]{1,0:T(8,128)(2,1)S(1)} %get-tuple-element.31), channel_id=1, source_target_pairs={{0,8},{8,16},{16,24},{24,32},{32,40},{40,48},{48,56},{56,64},{64,7... | collective-permute-start | bytes 122888 | tf_op jit(solution)/shard_map/ppermute | solution.py:47
  11.6 15.4 %all-to-all-start = ((s32[16,1,2]{2,1,0:T(1,128)}), s32[16,1,2]{2,1,0:T(1,128)S(1)}, u32[]{:S(2)}, u32[]{:S(2)}) async-start(s32[16,1,2]{2,1,0:T(1,128)} %copy.12), calls=%async_computation | async-start | bytes 16384 | tf_op jit(solution)/shard_map/all_to_all | solution.py:501
  32.9 7.4 %copy-start = (bf16[16,1681]{1,0:T(8,128)(2,1)S(1)}, bf16[16,1681]{1,0:T(8,128)(2,1)}, u32[]{:S(2)}) copy-start(bf16[16,1681]{1,0:T(8,128)(2,1)} %param.13) | copy-start | bytes 161380
  32.9 32.4 %all-to-all-start.1 = ((bf16[32,128,256]{2,1,0:T(8,128)(2,1)}), bf16[32,128,256]{2,1,0:T(8,128)(2,1)S(1)}, u32[]{:S(2)}, u32[]{:S(2)}) async-start(bf16[32,128,256]{2,1,0:T(8,128)(2,1)} %cut.1), calls=%async_computation.1 | async-start | bytes 4194304 | tf_op jit(solution)/shard_map/all_to_all | solution.py:515
  58.2 5.7 %copy-start.1 = (s32[16,1]{0,1:T(1,128)S(1)}, s32[16,1]{0,1:T(1,128)}, u32[]{:S(2)}) copy-start(s32[16,1]{0,1:T(1,128)} %param.10) | copy-start | bytes 196
  91.4 33.9 %all-to-all-start.2 = ((bf16[32,128,256]{2,1,0:T(8,128)(2,1)}), bf16[32,128,256]{2,1,0:T(8,128)(2,1)S(1)}, u32[]{:S(2)}, u32[]{:S(2)}) async-start(bf16[32,128,256]{2,1,0:T(8,128)(2,1)} %get-tuple-element.21), calls=%async_computation.2 | async-start | bytes 4194304 | tf_op jit(solution)/shard_map/all_to_all | solution.py:519
  147.5 8.5 %collective-permute-start.2 = (bf16[20,128]{1,0:T(8,128)(2,1)}, bf16[20,128]{1,0:T(8,128)(2,1)S(1)}, u32[]{:S(2)}, u32[]{:S(2)}) collective-permute-start(bf16[20,128]{1,0:T(8,128)(2,1)} %get-tuple-element.25), channel_id=1, source_target_pairs={{0,8},{8,16},{16,24},{24,32},{32,40},{40,48},{48,56},{56,64},{64,7... | collective-permute-start | bytes 15368 | tf_op jit(solution)/shard_map/ppermute | solution.py:47
  154.2 7.8 %collective-permute-start.3 = (bf16[20,128]{1,0:T(8,128)(2,1)}, bf16[20,128]{1,0:T(8,128)(2,1)S(1)}, u32[]{:S(2)}, u32[]{:S(2)}) collective-permute-start(bf16[20,128]{1,0:T(8,128)(2,1)} %get-tuple-element.26), channel_id=1, source_target_pairs={{8,0},{16,8},{24,16},{32,24},{40,32},{48,40},{56,48},{64,56},{72,6... | collective-permute-start | bytes 15368 | tf_op jit(solution)/shard_map/ppermute | solution.py:47

commit v4 on v3

--- a/solution.py
+++ b/solution.py
@@ -268,25 +268,16 @@
     return taps_ref[0, t * LANES : (t + 1) * LANES, (TILES - 1) * LANES :]
 
 
-def correlate(read, taps_ref, rows):
+def correlate(read, taps_ref):
     across = (((1,), (1,)), ((), ()))
-    total = jnp.zeros((rows, 2 * LANES), F32)
+    total = jnp.zeros((2 * BLOCKS, LANES), F32)
     for t in range(REACH):
-        for s in range(REACH - 1):
+        for d in range(TILES // 2):
+            taps = taps_ref[0, t * LANES : (t + 1) * LANES, 2 * d * LANES : (2 * d + 2) * LANES]
             total = total + lax.dot_general(
-                read(s, t), block_taps(taps_ref, s, t), across, preferred_element_type=F32
+                read(d, t), taps, across, preferred_element_type=F32
             )
-    last = jnp.zeros((rows, LANES), F32)
-    for t in range(0, REACH, 2):
-        field = [read(REACH - 1, t + i)[:, :LANES] for i in range(2)]
-        taps = [last_taps(taps_ref, t + i) for i in range(2)]
-        last = last + lax.dot_general(
-            jnp.concatenate(field, axis=1),
-            jnp.concatenate(taps, axis=1),
-            across,
-            preferred_element_type=F32,
-        )
-    return jnp.concatenate([total[:, :LANES], total[:, LANES:] + last], axis=1)
+    return jnp.concatenate([total[:BLOCKS], total[BLOCKS:]], axis=1)
 
 
 def convolve(read, taps_ref, rows):
@@ -317,11 +308,18 @@
 
     field[...] = patch_ref[slot_ref[piece]].astype(F32)
 
-    def read_patch(s, t):
-        starts = [EXT * (row + s) + t for row in range(OUT)]
-        return jnp.concatenate([field[at : at + OUT, :] for at in starts], axis=0).astype(BF16)
-
-    predicted = correlate(read_patch, taps_ref, BLOCKS)
+    def read_patch(d, t):
+        starts = [EXT * (row + d) + t for row in range(OUT)]
+        upper = [field[at : at + OUT, :] for at in starts]
+        lower = [
+            jnp.concatenate(
+                [field[at : at + OUT, LANES:], field[at + EXT : at + EXT + OUT, :LANES]], axis=1
+            )
+            for at in starts
+        ]
+        return jnp.concatenate(upper + lower, axis=0).astype(BF16)
+
+    predicted = correlate(read_patch, taps_ref)
     observed = data_ref[0].astype(F32)
     residual = jnp.where(observed < jnp.inf, predicted - observed, 0.0).astype(BF16)
     res_out[0] = residual

time: 164 us -> 159 us (0.970)
  Pallas kernels: 71.1 us -> 66.1 us
    pallas_call x1, Pallas kernels: 26.1 us -> 21.2 us  [pieces(): pl.pallas_call(piece_kernel, grid_spec=pltpu.PrefetchScalarGridSpec(num_s...]
  transfers between devices with their start and end apart: 7 -> 7, of which waited for: 3 -> 3; matrix products, arithmetic and copies ran while one was open for 3% -> 3% of each run, Pallas kernels for 22% -> 23%
where the time goes in v4:
time: 159 us; the launch traced here: 158 us
  Pallas kernels  66.1 us (42%)
  starting transfers between devices  39.6 us (25%)
  waiting for transfers between devices  27.1 us (17%)
  blocking collectives  17 us (11%)
  other arithmetic  4.31 us (3%)
  local copies, waits for them, and re-layouts  3.59 us (2%)
    pallas_call x1, Pallas kernels, pieces(): pl.pallas_call(piece_kernel, grid_spec=pltpu.PrefetchScalarGridSpec(num_s...  21.2 us
    all_to_all x1, waiting for transfers between devices, shards(): lax.all_to_all(adjoints, 'sky', split_axis=0, concat_axis=0, tiled=True)  20.4 us
    all_to_all x1, blocking collectives, shards(): lax.all_to_all(partial, 'exp', split_axis=0, concat_axis=0, tiled=True)  17 us
    pallas_call x1, Pallas kernels, build_taps(): pl.pallas_call(taps_kernel, grid=(cells,), in_specs=[pl.BlockSpec((1, TAP...  16.9 us
    ppermute x4, starting transfers between devices, from_behind(): return lax.ppermute(x, axis, pairs)  16.4 us
    all_to_all x1, starting transfers between devices, shards(): lax.all_to_all(adjoints, 'sky', split_axis=0, concat_axis=0, tiled=True)  7.99 us
    all_to_all x1, starting transfers between devices, shards(): lax.all_to_all(requests, 'sky', split_axis=0, concat_axis=0, tiled=True)  7.84 us
    pallas_call x1, Pallas kernels, own_blocks(): pl.pallas_call(own_kernel, in_specs=[pl.BlockSpec(memory_space=pltpu.VMEM...  7.52 us
  transfers between devices with their start and end apart: 7, of which 3 were waited for; matrix products, arithmetic and copies ran while one was open for 3% of the time, Pallas kernels for 23%

profile of v4, /device:TPU:24, one launch (start us, length us, event | category | flops | bytes accessed | tf_op | source)
XLA Modules:
  0.0 158.5 jit_solution(9084877916015124486)
XLA Ops:
  0.6 0.8 fusion.4
  1.5 2.7 %collective-permute-start.1 = (bf16[20,1024]{1,0:T(8,128)(2,1)S(1)}, bf16[20,1024]{1,0:T(8,128)(2,1)S(1)}, u32[]{:S(2)}, u32[]{:S(2)}) collective-permute-start(bf16[20,1024]{1,0:T(8,128)(2,1)S(1)} %get-tuple-element.30), channel_id=1, source_target_pairs={{8,0},{16,8},{24,16},{32,24},{40,32},{48,40},{56,48},{64,56},{72,6... | collective-permute-start | bytes 122888 | tf_op jit(solution)/shard_map/ppermute | solution.py:47
  4.1 5.3 %collective-permute-start = (bf16[20,1024]{1,0:T(8,128)(2,1)S(1)}, bf16[20,1024]{1,0:T(8,128)(2,1)S(1)}, u32[]{:S(2)}, u32[]{:S(2)}) collective-permute-start(bf16[20,1024]{1,0:T(8,128)(2,1)S(1)} %get-tuple-element.31), channel_id=1, source_target_pairs={{0,8},{8,16},{16,24},{24,32},{32,40},{40,48},{48,56},{56,64},{64,7... | collective-permute-start | bytes 122888 | tf_op jit(solution)/shard_map/ppermute | solution.py:47
  9.4 0.7 multiply_add_fusion
  10.1 0.8 select_reduce_fusion.1
  10.9 0.7 copy.12
  11.6 7.8 %all-to-all-start = ((s32[16,1,2]{2,1,0:T(1,128)}), s32[16,1,2]{2,1,0:T(1,128)S(1)}, u32[]{:S(2)}, u32[]{:S(2)}) async-start(s32[16,1,2]{2,1,0:T(1,128)} %copy.12), calls=%async_computation | async-start | bytes 16384 | tf_op jit(solution)/shard_map/all_to_all | solution.py:499
  19.4 7.5 %own.1.refs_1_ = f32[31,72,128]{2,1,0:T(8,128)S(1)} custom-call(bf16[256,1024]{1,0:T(8,128)(2,1)} %refs_4_.1), custom_call_target="tpu_custom_call" | custom-call | flops 1000 | bytes 1000 | tf_op jit(solution)/shard_map/own/pallas_call | solution.py:176
  26.9 0.0 all-to-all-done
  27.0 0.5 broadcast.122
  27.5 0.7 reduce.3
  28.1 0.6 reshape.109.refs_0_
  28.8 0.0 collective-permute-done.1.refs_5_
  28.8 0.0 collective-permute-done.refs_2_
  28.8 4.1 %cut.1 = bf16[32,128,256]{2,1,0:T(8,128)(2,1)} custom-call(s32[32]{0:T(128)} %reshape.109.refs_0_, f32[31,72,128]{2,1,0:T(8,128)S(1)} %own.1.refs_1_, bf16[20,1024]{1,0:T(8,128)(2,1)S(1)} %collective-permute-done.refs_2_, bf16[256,1024]{1,0:T(8,128)(2,1)} %refs_4_.1, bf16[256,1024]{1,0:T(8,128)(2,1)} %refs_4_.1, ...), custom_call_target="tpu_custom_call" | custom-call | flops 1000 | bytes 1000 | tf_op jit(solution)/shard_map/cut/pallas_call | solution.py:229
  32.9 0.0 copy-start
  32.9 7.4 %all-to-all-start.1 = ((bf16[32,128,256]{2,1,0:T(8,128)(2,1)}), bf16[32,128,256]{2,1,0:T(8,128)(2,1)S(1)}, u32[]{:S(2)}, u32[]{:S(2)}) async-start(bf16[32,128,256]{2,1,0:T(8,128)(2,1)} %cut.1), calls=%async_computation.1 | async-start | bytes 4194304 | tf_op jit(solution)/shard_map/all_to_all | solution.py:513
  40.3 0.0 copy-done
  40.3 0.2 reshape.110
  40.5 0.7 pad.18.kernel_ref
  41.2 16.9 %taps.1.taps_ref = bf16[16,512,768]{2,1,0:T(8,128)(2,1)} custom-call(bf16[16,48,128]{2,1,0:T(8,128)(2,1)} %pad.18.kernel_ref), custom_call_target="tpu_custom_call" | custom-call | flops 1000 | bytes 1000 | tf_op jit(solution)/shard_map/taps/pallas_call | solution.py:138
  58.2 0.0 copy-start.1
  58.2 5.7 %regroup.1.data_ref = bf16[16,64,256]{2,1,0:T(8,128)(2,1)} custom-call(bf16[16,128,128]{2,1,0:T(8,128)(2,1)} %data_ref, s32[16,128,128]{2,1,0:T(8,128)} %keep_ref), custom_call_target="tpu_custom_call" | custom-call | flops 1000 | bytes 1000 | tf_op jit(solution)/shard_map/regroup/pallas_call | solution.py:77
  63.9 0.0 copy-done.1
  63.9 0.1 fusion.1
  64.0 0.5 convert_add_fusion.1.slot_ref
  64.5 0.7 all-to-all-done.1.patch_ref
  65.3 21.2 %pieces.1 = (bf16[32,128,256]{2,1,0:T(8,128)(2,1)}, bf16[16,64,256]{2,1,0:T(8,128)(2,1)}) custom-call(s32[16]{0:T(128)} %convert_add_fusion.1.slot_ref, s32[16]{0:T(128)} %cell_ref.1, bf16[32,128,256]{2,1,0:T(8,128)(2,1)S(1)} %all-to-all-done.1.patch_ref, bf16[16,512,768]{2,1,0:T(8,128)(2,1)} %taps.1.taps_ref, bf16[16,64,256]{2,1,0:T(8,128)(2,1)} %regroup.1.data_ref), custom_call_target="tpu_custom_call" | custom-call | flops 1000 | bytes 1000 | tf_op jit(solution)/shard_map/pieces/pallas_call | solution.py:344
  86.4 8.0 %all-to-all-start.2 = ((bf16[32,128,256]{2,1,0:T(8,128)(2,1)}), bf16[32,128,256]{2,1,0:T(8,128)(2,1)S(1)}, u32[]{:S(2)}, u32[]{:S(2)}) async-start(bf16[32,128,256]{2,1,0:T(8,128)(2,1)} %get-tuple-element.21), calls=%async_computation.2 | async-start | bytes 4194304 | tf_op jit(solution)/shard_map/all_to_all | solution.py:517
  94.4 5.5 %ungroup.1 = bf16[16,128,128]{2,1,0:T(8,128)(2,1)} custom-call(bf16[16,64,256]{2,1,0:T(8,128)(2,1)} %get-tuple-element.22.res_ref), custom_call_target="tpu_custom_call" | custom-call | flops 1000 | bytes 1000 | tf_op jit(solution)/shard_map/ungroup/pallas_call | solution.py:380
  100.0 20.4 %all-to-all-done.2.refs_1_ = bf16[32,128,256]{2,1,0:T(8,128)(2,1)S(1)} async-done(((bf16[32,128,256]{2,1,0:T(8,128)(2,1)}), bf16[32,128,256]{2,1,0:T(8,128)(2,1)S(1)}, u32[]{:S(2)}, u32[]{:S(2)}) %all-to-all-start.2) | async-done | bytes 2097184 | tf_op jit(solution)/shard_map/all_to_all | solution.py:517
  120.4 2.8 %fold.1 = bf16[8,352,128]{2,1,0:T(8,128)(2,1)} custom-call(s32[32]{0:T(128)} %reshape.109.refs_0_, bf16[32,128,256]{2,1,0:T(8,128)(2,1)S(1)} %all-to-all-done.2.refs_1_), custom_call_target="tpu_custom_call" | custom-call | flops 1000 | bytes 1000 | tf_op jit(solution)/shard_map/fold/pallas_call | solution.py:421
  123.2 17.0 %all_to_all.24.refs_0_ = bf16[8,352,128]{2,1,0:T(8,128)(2,1)} all-to-all(bf16[8,352,128]{2,1,0:T(8,128)(2,1)} %fold.1), channel_id=1, replica_groups=mesh['sky'=16,'exp'=8] {'exp'}, dimensions={0} | all-to-all | bytes 1441792 | tf_op jit(solution)/shard_map/all_to_all | solution.py:521
  140.2 2.3 %finish.1 = (bf16[20,128]{1,0:T(8,128)(2,1)}, f32[256,128]{1,0:T(8,128)}, bf16[20,128]{1,0:T(8,128)(2,1)}) custom-call(bf16[8,352,128]{2,1,0:T(8,128)(2,1)} %all_to_all.24.refs_0_), custom_call_target="tpu_custom_call" | custom-call | flops 1000 | bytes 1000 | tf_op jit(solution)/shard_map/finish/pallas_call | solution.py:467
  142.5 6.5 %collective-permute-start.2 = (bf16[20,128]{1,0:T(8,128)(2,1)}, bf16[20,128]{1,0:T(8,128)(2,1)S(1)}, u32[]{:S(2)}, u32[]{:S(2)}) collective-permute-start(bf16[20,128]{1,0:T(8,128)(2,1)} %get-tuple-element.25), channel_id=1, source_target_pairs={{0,8},{8,16},{16,24},{24,32},{32,40},{40,48},{48,56},{56,64},{64,7... | collective-permute-start | bytes 15368 | tf_op jit(solution)/shard_map/ppermute | solution.py:47
  149.1 1.9 %collective-permute-start.3 = (bf16[20,128]{1,0:T(8,128)(2,1)}, bf16[20,128]{1,0:T(8,128)(2,1)S(1)}, u32[]{:S(2)}, u32[]{:S(2)}) collective-permute-start(bf16[20,128]{1,0:T(8,128)(2,1)} %get-tuple-element.26), channel_id=1, source_target_pairs={{8,0},{16,8},{24,16},{32,24},{40,32},{48,40},{56,48},{64,56},{72,6... | collective-permute-start | bytes 15368 | tf_op jit(solution)/shard_map/ppermute | solution.py:47
  151.0 0.0 collective-permute-done.2
  151.0 5.9 %collective-permute-done.3 = bf16[20,128]{1,0:T(8,128)(2,1)S(1)} collective-permute-done((bf16[20,128]{1,0:T(8,128)(2,1)}, bf16[20,128]{1,0:T(8,128)(2,1)S(1)}, u32[]{:S(2)}, u32[]{:S(2)}) %collective-permute-start.3) | collective-permute-done | bytes 5152 | tf_op jit(solution)/shard_map/ppermute | solution.py:47
  156.9 1.6 convert_add_fusion
  (2 shorter events, 0.0 us)
Async XLA Ops:
  1.5 27.3 %collective-permute-start.1 = (bf16[20,1024]{1,0:T(8,128)(2,1)S(1)}, bf16[20,1024]{1,0:T(8,128)(2,1)S(1)}, u32[]{:S(2)}, u32[]{:S(2)}) collective-permute-start(bf16[20,1024]{1,0:T(8,128)(2,1)S(1)} %get-tuple-element.30), channel_id=1, source_target_pairs={{8,0},{16,8},{24,16},{32,24},{40,32},{48,40},{56,48},{64,56},{72,6... | collective-permute-start | bytes 122888 | tf_op jit(solution)/shard_map/ppermute | solution.py:47
  4.1 24.6 %collective-permute-start = (bf16[20,1024]{1,0:T(8,128)(2,1)S(1)}, bf16[20,1024]{1,0:T(8,128)(2,1)S(1)}, u32[]{:S(2)}, u32[]{:S(2)}) collective-permute-start(bf16[20,1024]{1,0:T(8,128)(2,1)S(1)} %get-tuple-element.31), channel_id=1, source_target_pairs={{0,8},{8,16},{16,24},{24,32},{32,40},{40,48},{48,56},{56,64},{64,7... | collective-permute-start | bytes 122888 | tf_op jit(solution)/shard_map/ppermute | solution.py:47
  11.6 15.4 %all-to-all-start = ((s32[16,1,2]{2,1,0:T(1,128)}), s32[16,1,2]{2,1,0:T(1,128)S(1)}, u32[]{:S(2)}, u32[]{:S(2)}) async-start(s32[16,1,2]{2,1,0:T(1,128)} %copy.12), calls=%async_computation | async-start | bytes 16384 | tf_op jit(solution)/shard_map/all_to_all | solution.py:499
  32.9 7.4 %copy-start = (bf16[16,1681]{1,0:T(8,128)(2,1)S(1)}, bf16[16,1681]{1,0:T(8,128)(2,1)}, u32[]{:S(2)}) copy-start(bf16[16,1681]{1,0:T(8,128)(2,1)} %param.13) | copy-start | bytes 161380
  32.9 32.4 %all-to-all-start.1 = ((bf16[32,128,256]{2,1,0:T(8,128)(2,1)}), bf16[32,128,256]{2,1,0:T(8,128)(2,1)S(1)}, u32[]{:S(2)}, u32[]{:S(2)}) async-start(bf16[32,128,256]{2,1,0:T(8,128)(2,1)} %cut.1), calls=%async_computation.1 | async-start | bytes 4194304 | tf_op jit(solution)/shard_map/all_to_all | solution.py:513
  58.2 5.7 %copy-start.1 = (s32[16,1]{0,1:T(1,128)S(1)}, s32[16,1]{0,1:T(1,128)}, u32[]{:S(2)}) copy-start(s32[16,1]{0,1:T(1,128)} %param.10) | copy-start | bytes 196
  86.4 34.0 %all-to-all-start.2 = ((bf16[32,128,256]{2,1,0:T(8,128)(2,1)}), bf16[32,128,256]{2,1,0:T(8,128)(2,1)S(1)}, u32[]{:S(2)}, u32[]{:S(2)}) async-start(bf16[32,128,256]{2,1,0:T(8,128)(2,1)} %get-tuple-element.21), calls=%async_computation.2 | async-start | bytes 4194304 | tf_op jit(solution)/shard_map/all_to_all | solution.py:517
  142.5 8.5 %collective-permute-start.2 = (bf16[20,128]{1,0:T(8,128)(2,1)}, bf16[20,128]{1,0:T(8,128)(2,1)S(1)}, u32[]{:S(2)}, u32[]{:S(2)}) collective-permute-start(bf16[20,128]{1,0:T(8,128)(2,1)} %get-tuple-element.25), channel_id=1, source_target_pairs={{0,8},{8,16},{16,24},{24,32},{32,40},{40,48},{48,56},{56,64},{64,7... | collective-permute-start | bytes 15368 | tf_op jit(solution)/shard_map/ppermute | solution.py:47
  149.1 7.8 %collective-permute-start.3 = (bf16[20,128]{1,0:T(8,128)(2,1)}, bf16[20,128]{1,0:T(8,128)(2,1)S(1)}, u32[]{:S(2)}, u32[]{:S(2)}) collective-permute-start(bf16[20,128]{1,0:T(8,128)(2,1)} %get-tuple-element.26), channel_id=1, source_target_pairs={{8,0},{16,8},{24,16},{32,24},{40,32},{48,40},{56,48},{64,56},{72,6... | collective-permute-start | bytes 15368 | tf_op jit(solution)/shard_map/ppermute | solution.py:47

commit v5 on v4

--- a/solution.py
+++ b/solution.py
@@ -17,6 +17,7 @@
 REACH = 4
 TAIL = 8
 BLOCKS = OUT * OUT
+PATCH_ROWS = 240
 SLOT_ROWS = 128
 PITCH = 72
 TILES = 6
@@ -28,6 +29,7 @@
 CHUNK = 9
 CHUNK_ROWS = 352
 SHIFT = 4
+UNKNOWN = 2.0**100
 SMALL = pl.CostEstimate(flops=1000, bytes_accessed=1000, transcendentals=0)
 F32 = jnp.float32
 BF16 = jnp.bfloat16
@@ -58,10 +60,29 @@
     return x
 
 
+def reversed_groups(shift=0):
+    source = lax.broadcasted_iota(jnp.int32, (2 * LANES, LANES), 0)
+    lane = lax.broadcasted_iota(jnp.int32, (2 * LANES, LANES), 1)
+    group = (8 - lane // G) % 8
+    return (source == LANES - shift + group * G + lane % G).astype(BF16)
+
+
+def swap_reversed(x):
+    group = lax.broadcasted_iota(jnp.int32, (8, LANES), 1) // G
+    tiles = []
+    for tile in range(x.shape[0]):
+        now = pltpu.roll(x[tile], 0, 1, stride=G, stride_axis=0)
+        for d in (1, 2, 4):
+            now = jnp.where((group & d) != 0, pltpu.roll(now, 8 - d, 0), now)
+        tiles.append(pltpu.roll(now, 0, 1, stride=G, stride_axis=0))
+    return jnp.stack(tiles, 0)
+
+
 def regroup_kernel(data_ref, keep_ref, out_ref):
     def per_piece(p, carry):
-        known = jnp.where(keep_ref[p] != 0, data_ref[p].astype(F32), jnp.inf)
-        blocks = swap_groups(known.reshape(2 * OUT, 8, LANES)).reshape(OUT, 2, 8, LANES)
+        known = jnp.where(keep_ref[p] != 0, data_ref[p].astype(F32), UNKNOWN).astype(BF16)
+        turned = jnp.dot(known, reversed_groups()[LANES:], preferred_element_type=F32)
+        blocks = swap_reversed(turned.reshape(2 * OUT, 8, LANES)).reshape(OUT, 2, 8, LANES)
         for half in range(2):
             out_ref[p, :, half * LANES : (half + 1) * LANES] = (
                 blocks[:, half].reshape(BLOCKS, LANES).astype(BF16)
@@ -150,24 +171,28 @@
     )(kernels)
 
 
-def row_blocks(pixels):
-    far = lax.broadcasted_iota(jnp.int32, (8, LANES), 1) >= HALO
-    tiles = pixels.shape[1] // LANES
-    empty = jnp.zeros((8, LANES), F32)
-    turned = [
-        pltpu.roll(pixels[:, tile * LANES : (tile + 1) * LANES], HALO, 1) for tile in range(tiles)
+def moved_tiles(pixels):
+    rows, columns = pixels.shape
+    turn = reversed_groups(HALO)
+    empty = jnp.zeros((rows, LANES), BF16)
+    tiles = [pixels[:, at : at + LANES] for at in range(0, columns, LANES)]
+    return [
+        jnp.dot(jnp.concatenate([old, now], axis=1), turn, preferred_element_type=F32)
+        for old, now in zip([empty] + tiles, tiles + [empty])
     ]
-    before, after = [empty] + turned, turned + [empty]
-    moved = [jnp.where(far, now, old) for old, now in zip(before, after)]
-    return swap_groups(jnp.stack(moved, 0)).reshape((tiles + 1) * 8, LANES)
 
 
 def own_kernel(stripe_ref, out_ref, pixels):
     skip = 8 * OWN_FIRST - HALO
-    pixels[...] = stripe_ref[...].astype(F32)
+    for tile, moved in enumerate(moved_tiles(stripe_ref[...])):
+        pixels[:, tile * LANES : (tile + 1) * LANES] = moved
 
     for row in range(out_ref.shape[0]):
-        out_ref[row] = row_blocks(pixels[skip + 8 * row : skip + 8 * row + 8, :])
+        first = skip + 8 * row
+        tiles = [
+            pixels[first : first + 8, at : at + LANES] for at in range(0, PITCH * G, LANES)
+        ]
+        out_ref[row] = swap_reversed(jnp.stack(tiles, 0)).reshape(PITCH, LANES)
 
 
 def own_blocks(stripe):
@@ -178,7 +203,7 @@
         in_specs=[pl.BlockSpec(memory_space=pltpu.VMEM)],
         out_specs=pl.BlockSpec(memory_space=pltpu.VMEM),
         out_shape=pltpu.VMEM((count, PITCH, LANES), F32),
-        scratch_shapes=[pltpu.VMEM((rows, columns), F32)],
+        scratch_shapes=[pltpu.VMEM((rows, PITCH * G), F32)],
         cost_estimate=SMALL,
         name="own",
     )(stripe)
@@ -194,15 +219,22 @@
         own = own_ref.shape[0]
         blocks[OWN_FIRST : OWN_FIRST + own] = own_ref[...]
         missing = 8 * OWN_FIRST - HALO
-        upper[:HALO, :] = above_ref[...].astype(F32)
-        upper[HALO:, :] = top_ref[...].astype(F32)[:missing]
-        for row in range(OWN_FIRST):
-            blocks[row] = row_blocks(upper[8 * row : 8 * row + 8, :])
+        rims = ((above_ref, 0), (top_ref, 1), (bottom_ref, 2), (below_ref, 3))
+        tiles = {at: moved_tiles(ref[...]) for ref, at in rims}
         lower[...] = jnp.zeros_like(lower)
-        lower[:missing, :] = bottom_ref[...].astype(F32)[G - missing :]
-        lower[missing : missing + HALO, :] = below_ref[...].astype(F32)
-        for row in range(lower.shape[0] // 8):
-            blocks[OWN_FIRST + own + row] = row_blocks(lower[8 * row : 8 * row + 8, :])
+        for tile in range(PITCH // 8):
+            lanes = slice(tile * LANES, (tile + 1) * LANES)
+            upper[:HALO, lanes] = tiles[0][tile]
+            upper[HALO:, lanes] = tiles[1][tile][:missing]
+            lower[:missing, lanes] = tiles[2][tile][G - missing :]
+            lower[missing : missing + HALO, lanes] = tiles[3][tile]
+        for pixels, first in ((upper, 0), (lower, OWN_FIRST + own)):
+            for row in range(pixels.shape[0] // 8):
+                parts = [
+                    pixels[8 * row : 8 * row + 8, at : at + LANES]
+                    for at in range(0, PITCH * G, LANES)
+                ]
+                blocks[first + row] = swap_reversed(jnp.stack(parts, 0)).reshape(PITCH, LANES)
 
     def per_slot(n, carry):
         wanted = ids_ref[step * SLOTS + n]
@@ -211,10 +243,9 @@
         def _():
             first_row = wanted // per_row * (2 * OUT)
             first_col = pl.multiple_of(wanted % per_row * OUT, 8)
-            for row in range(EXT):
-                for half in range(2):
-                    part = blocks[first_row + 2 * row + half, pl.ds(first_col, G), :]
-                    scratch[pl.ds(EXT * row, G), half * LANES : (half + 1) * LANES] = part
+            for row in range(2 * EXT - 1):
+                part = blocks[first_row + row, pl.ds(first_col, G), :]
+                scratch[EXT * row : EXT * row + G, :] = part
             out_ref[n] = scratch[...].astype(BF16)
 
         return carry
@@ -238,15 +269,15 @@
                 pl.BlockSpec((G, columns), lambda n, ids: (last, 0)),
                 whole_vmem(),
             ],
-            out_specs=pl.BlockSpec((SLOTS, SLOT_ROWS, 2 * LANES), lambda n, ids: (n, 0, 0)),
+            out_specs=pl.BlockSpec((SLOTS, PATCH_ROWS, LANES), lambda n, ids: (n, 0, 0)),
             scratch_shapes=[
                 pltpu.VMEM((half_rows, PITCH, LANES), F32),
-                pltpu.VMEM((8 * OWN_FIRST, columns), F32),
-                pltpu.VMEM((8 * (half_rows - OWN_FIRST - own.shape[0]), columns), F32),
-                pltpu.VMEM((SLOT_ROWS, 2 * LANES), F32),
+                pltpu.VMEM((8 * OWN_FIRST, PITCH * G), F32),
+                pltpu.VMEM((8 * (half_rows - OWN_FIRST - own.shape[0]), PITCH * G), F32),
+                pltpu.VMEM((PATCH_ROWS, LANES), F32),
             ],
         ),
-        out_shape=jax.ShapeDtypeStruct((slots, SLOT_ROWS, 2 * LANES), BF16),
+        out_shape=jax.ShapeDtypeStruct((slots, PATCH_ROWS, LANES), BF16),
         cost_estimate=SMALL,
         name="cut",
     )(ids, on_chip(own), on_chip(above), stripe, stripe, on_chip(below))
@@ -309,19 +340,17 @@
     field[...] = patch_ref[slot_ref[piece]].astype(F32)
 
     def read_patch(d, t):
-        starts = [EXT * (row + d) + t for row in range(OUT)]
-        upper = [field[at : at + OUT, :] for at in starts]
-        lower = [
-            jnp.concatenate(
-                [field[at : at + OUT, LANES:], field[at + EXT : at + EXT + OUT, :LANES]], axis=1
-            )
-            for at in starts
-        ]
-        return jnp.concatenate(upper + lower, axis=0).astype(BF16)
+        parts = []
+        for half in range(2):
+            for row in range(OUT):
+                at = EXT * (2 * (row + d) + half) + t
+                pair = [field[at : at + OUT, :], field[at + EXT : at + EXT + OUT, :]]
+                parts.append(jnp.concatenate(pair, axis=1))
+        return jnp.concatenate(parts, axis=0).astype(BF16)
 
     predicted = correlate(read_patch, taps_ref)
     observed = data_ref[0].astype(F32)
-    residual = jnp.where(observed < jnp.inf, predicted - observed, 0.0).astype(BF16)
+    residual = jnp.where(observed < UNKNOWN, predicted - observed, 0.0).astype(BF16)
     res_out[0] = residual
     wide = residual.astype(F32)
     for row in range(OUT):
@@ -349,12 +378,12 @@
             in_specs=[whole_vmem(), cell, block],
             out_specs=[slot, block],
             scratch_shapes=[
-                pltpu.VMEM((SLOT_ROWS, 2 * LANES), F32),
+                pltpu.VMEM((PATCH_ROWS, LANES), F32),
                 pltpu.VMEM((RES_LEAD + SLOT_ROWS, 2 * LANES), F32),
             ],
         ),
         out_shape=[
-            jax.ShapeDtypeStruct(patches.shape, BF16),
+            jax.ShapeDtypeStruct((patches.shape[0], SLOT_ROWS, 2 * LANES), BF16),
             jax.ShapeDtypeStruct(data.shape, BF16),
         ],
         cost_estimate=SMALL,
@@ -363,12 +392,16 @@
 
 
 def ungroup_kernel(res_ref, out_ref):
+    turn = reversed_groups()[LANES:]
+
     def per_piece(p, carry):
         halves = [
-            res_ref[p, :, half * LANES : (half + 1) * LANES].astype(F32).reshape(OUT, 8, LANES)
+            jnp.dot(
+                res_ref[p, :, half * LANES : (half + 1) * LANES], turn, preferred_element_type=F32
+            ).reshape(OUT, 8, LANES)
             for half in range(2)
         ]
-        pixels = swap_groups(jnp.stack(halves, 1).reshape(2 * OUT, 8, LANES))
+        pixels = swap_reversed(jnp.stack(halves, 1).reshape(2 * OUT, 8, LANES))
         out_ref[p] = pixels.reshape(B, LANES).astype(BF16)
         return carry
 
@@ -478,6 +511,35 @@
     )(terms)
 
 
+def rims_kernel(middle_ref, above_ref, below_ref, out_ref):
+    rows = out_ref.shape[0]
+    out_ref[...] = middle_ref[...]
+
+    @pl.when(pl.program_id(0) == 0)
+    def _():
+        out_ref[:HALO, :] = out_ref[:HALO, :] + above_ref[...].astype(F32)
+
+    @pl.when(pl.program_id(0) == 1)
+    def _():
+        out_ref[rows - HALO :, :] = out_ref[rows - HALO :, :] + below_ref[...].astype(F32)
+
+
+def add_rims(middle, above, below):
+    rows = 32
+    last = middle.shape[0] // rows - 1
+    block = pl.BlockSpec((rows, LANES), lambda i: (i * last, 0))
+    return pl.pallas_call(
+        rims_kernel,
+        grid=(2,),
+        in_specs=[block, whole_vmem(), whole_vmem()],
+        out_specs=block,
+        out_shape=jax.ShapeDtypeStruct(middle.shape, F32),
+        input_output_aliases={0: 0},
+        cost_estimate=SMALL,
+        name="rims",
+    )(middle, on_chip(above), on_chip(below))
+
+
 def shards(sky_model, exposure_data, pixel_mask, block_owner, block_local, psf_cell, psf_table):
     sky_count = lax.axis_size("sky")
     stripe_rows, stripe_cols = sky_model.shape
@@ -496,6 +558,7 @@
         ],
         axis=1,
     )
+    requests, sky_model = lax.optimization_barrier((requests, sky_model))
     asked = lax.all_to_all(requests, "sky", split_axis=0, concat_axis=0, tiled=True)
     asked = asked.reshape(sky_count * CAP)
 
@@ -520,13 +583,9 @@
     partial = fold(asked, received, per_row, half_rows)
     terms = lax.all_to_all(partial, "exp", split_axis=0, concat_axis=0, tiled=True)
     up, middle, down = finish(terms, half_rows, stripe_rows)
-    from_below = from_behind(up, "sky", -1).astype(F32)
-    from_above = from_behind(down, "sky", 1).astype(F32)
-    gradient = (
-        middle
-        + jnp.pad(from_above, ((0, stripe_rows - HALO), (0, 0)))
-        + jnp.pad(from_below, ((stripe_rows - HALO, 0), (0, 0)))
-    )
+    from_below = from_behind(up, "sky", -1)
+    from_above = from_behind(down, "sky", 1)
+    gradient = add_rims(middle, from_above, from_below)
     return (gradient, residual)
 
 

time: 159 us -> 151 us (0.950)
  starting transfers between devices: 39.6 us -> 35.1 us
  Pallas kernels: 66.1 us -> 63.8 us
    pallas_call x1, Pallas kernels: 7.52 us -> 2.11 us  [own_blocks(): pl.pallas_call(own_kernel, in_specs=[pl.BlockSpec(memory_space=pltpu.VMEM...]
    all_to_all x1, waiting for transfers between devices: 0.01 us -> 3.41 us  [shards(): lax.all_to_all(requests, 'sky', split_axis=0, concat_axis=0, tiled=True)]
    all_to_all x1, waiting for transfers between devices: 20.4 us -> 17.3 us  [shards(): lax.all_to_all(adjoints, 'sky', split_axis=0, concat_axis=0, tiled=True)]
    ppermute x4, starting transfers between devices: 16.4 us -> 14.3 us  [from_behind(): return lax.ppermute(x, axis, pairs)]
    all_to_all x1, starting transfers between devices: 7.38 us -> 5.73 us  [shards(): lax.all_to_all(outgoing, 'sky', split_axis=0, concat_axis=0, tiled=True)]
  transfers between devices with their start and end apart: 7 -> 7, of which waited for: 3 -> 3; matrix products, arithmetic and copies ran while one was open for 3% -> 3% of each run, Pallas kernels for 23% -> 21%
where the time goes in v5:
time: 151 us; the launch traced here: 149 us
  Pallas kernels  63.8 us (42%)
  starting transfers between devices  35.1 us (23%)
  waiting for transfers between devices  26.6 us (18%)
  blocking collectives  16.9 us (11%)
  local copies, waits for them, and re-layouts  3.59 us (2%)
  other arithmetic  2.74 us (2%)
    pallas_call x1, Pallas kernels, pieces(): pl.pallas_call(piece_kernel, grid_spec=pltpu.PrefetchScalarGridSpec(num_s...  21.1 us
    all_to_all x1, waiting for transfers between devices, shards(): lax.all_to_all(adjoints, 'sky', split_axis=0, concat_axis=0, tiled=True)  17.3 us
    pallas_call x1, Pallas kernels, build_taps(): pl.pallas_call(taps_kernel, grid=(cells,), in_specs=[pl.BlockSpec((1, TAP...  16.9 us
    all_to_all x1, blocking collectives, shards(): lax.all_to_all(partial, 'exp', split_axis=0, concat_axis=0, tiled=True)  16.9 us
    ppermute x4, starting transfers between devices, from_behind(): return lax.ppermute(x, axis, pairs)  14.3 us
    all_to_all x1, starting transfers between devices, shards(): lax.all_to_all(requests, 'sky', split_axis=0, concat_axis=0, tiled=True)  7.84 us
    all_to_all x1, starting transfers between devices, shards(): lax.all_to_all(adjoints, 'sky', split_axis=0, concat_axis=0, tiled=True)  7.27 us
    pallas_call x1, Pallas kernels, regroup(): pl.pallas_call(regroup_kernel, grid=(pieces // BATCH,), in_specs=[block,...  6.64 us
  transfers between devices with their start and end apart: 7, of which 3 were waited for; matrix products, arithmetic and copies ran while one was open for 3% of the time, Pallas kernels for 21%

profile of v5, /device:TPU:24, one launch (start us, length us, event | category | flops | bytes accessed | tf_op | source)
XLA Modules:
  0.0 149.5 jit_solution(2571346093386560456)
XLA Ops:
  0.6 0.7 multiply_add_fusion
  1.3 0.8 select_reduce_fusion.1
  2.1 0.8 fusion.4
  2.9 2.7 %collective-permute-start.1 = (bf16[20,1024]{1,0:T(8,128)(2,1)S(1)}, bf16[20,1024]{1,0:T(8,128)(2,1)S(1)}, u32[]{:S(2)}, u32[]{:S(2)}) collective-permute-start(bf16[20,1024]{1,0:T(8,128)(2,1)S(1)} %get-tuple-element.34), channel_id=1, source_target_pairs={{8,0},{16,8},{24,16},{32,24},{40,32},{48,40},{56,48},{64,56},{72,6... | collective-permute-start | bytes 122888 | tf_op jit(solution)/shard_map/ppermute | solution.py:49
  5.6 5.3 %collective-permute-start = (bf16[20,1024]{1,0:T(8,128)(2,1)S(1)}, bf16[20,1024]{1,0:T(8,128)(2,1)S(1)}, u32[]{:S(2)}, u32[]{:S(2)}) collective-permute-start(bf16[20,1024]{1,0:T(8,128)(2,1)S(1)} %get-tuple-element.35), channel_id=1, source_target_pairs={{0,8},{8,16},{16,24},{24,32},{32,40},{40,48},{48,56},{56,64},{64,7... | collective-permute-start | bytes 122888 | tf_op jit(solution)/shard_map/ppermute | solution.py:49
  10.9 0.7 copy.13
  11.6 7.8 %all-to-all-start = ((s32[16,1,2]{2,1,0:T(1,128)}), s32[16,1,2]{2,1,0:T(1,128)S(1)}, u32[]{:S(2)}, u32[]{:S(2)}) async-start(s32[16,1,2]{2,1,0:T(1,128)} %copy.13), calls=%async_computation | async-start | bytes 16384 | tf_op jit(solution)/shard_map/all_to_all | solution.py:562
  19.4 2.1 %own.1.refs_1_ = f32[31,72,128]{2,1,0:T(8,128)S(1)} custom-call(bf16[256,1024]{1,0:T(8,128)(2,1)} %refs_4_), custom_call_target="tpu_custom_call" | custom-call | flops 1000 | bytes 1000 | tf_op jit(solution)/shard_map/own/pallas_call | solution.py:201
  21.5 3.4 %all-to-all-done = s32[16,1,2]{2,1,0:T(1,128)S(1)} async-done(((s32[16,1,2]{2,1,0:T(1,128)}), s32[16,1,2]{2,1,0:T(1,128)S(1)}, u32[]{:S(2)}, u32[]{:S(2)}) %all-to-all-start) | async-done | bytes 160 | tf_op jit(solution)/shard_map/all_to_all | solution.py:562
  24.9 0.5 broadcast.118
  25.5 0.7 reduce.3
  26.1 0.6 reshape.109.refs_0_
  26.7 0.0 collective-permute-done.1.refs_5_
  26.7 0.0 collective-permute-done.refs_2_
  26.7 4.3 %cut.1 = bf16[32,240,128]{2,1,0:T(8,128)(2,1)} custom-call(s32[32]{0:T(128)} %reshape.109.refs_0_, f32[31,72,128]{2,1,0:T(8,128)S(1)} %own.1.refs_1_, bf16[20,1024]{1,0:T(8,128)(2,1)S(1)} %collective-permute-done.refs_2_, bf16[256,1024]{1,0:T(8,128)(2,1)} %refs_4_, bf16[256,1024]{1,0:T(8,128)(2,1)} %refs_4_, bf16[20,1024]{1,0:T(8,128)(2,1)S(1)} %collective-permute-done.1.refs_5_), custom_call_target="tpu_custom_call" | custom-call | flops 1000 | bytes 1000 | tf_op jit(solution)/shard_map/cut/pallas_call | solution.py:260
  31.0 0.0 copy-start
  31.0 5.7 %all-to-all-start.1 = ((bf16[32,240,128]{2,1,0:T(8,128)(2,1)}), bf16[32,240,128]{2,1,0:T(8,128)(2,1)S(1)}, u32[]{:S(2)}, u32[]{:S(2)}) async-start(bf16[32,240,128]{2,1,0:T(8,128)(2,1)} %cut.1), calls=%async_computation.1 | async-start | bytes 3932160 | tf_op jit(solution)/shard_map/all_to_all | solution.py:576
  36.8 0.0 copy-done
  36.8 0.2 reshape.110
  37.0 0.7 pad.4.kernel_ref
  37.7 16.9 %taps.1.taps_ref = bf16[16,512,768]{2,1,0:T(8,128)(2,1)} custom-call(bf16[16,48,128]{2,1,0:T(8,128)(2,1)} %pad.4.kernel_ref), custom_call_target="tpu_custom_call" | custom-call | flops 1000 | bytes 1000 | tf_op jit(solution)/shard_map/taps/pallas_call | solution.py:159
  54.6 0.0 copy-start.1
  54.6 6.6 %regroup.1.data_ref = bf16[16,64,256]{2,1,0:T(8,128)(2,1)} custom-call(bf16[16,128,128]{2,1,0:T(8,128)(2,1)} %data_ref, s32[16,128,128]{2,1,0:T(8,128)} %keep_ref), custom_call_target="tpu_custom_call" | custom-call | flops 1000 | bytes 1000 | tf_op jit(solution)/shard_map/regroup/pallas_call | solution.py:98
  61.3 0.0 copy-done.1
  61.3 0.1 fusion.1
  61.4 0.5 convert_add_fusion.slot_ref
  61.9 0.0 all-to-all-done.1.patch_ref
  61.9 21.1 %pieces.1 = (bf16[32,128,256]{2,1,0:T(8,128)(2,1)}, bf16[16,64,256]{2,1,0:T(8,128)(2,1)}) custom-call(s32[16]{0:T(128)} %convert_add_fusion.slot_ref, s32[16]{0:T(128)} %cell_ref.1, bf16[32,240,128]{2,1,0:T(8,128)(2,1)S(1)} %all-to-all-done.1.patch_ref, bf16[16,512,768]{2,1,0:T(8,128)(2,1)} %taps.1.taps_ref, bf16[16,64,256]{2,1,0:T(8,128)(2,1)} %regroup.1.data_ref), custom_call_target="tpu_custom_call" | custom-call | flops 1000 | bytes 1000 | tf_op jit(solution)/shard_map/pieces/pallas_call | solution.py:373
  83.1 7.3 %all-to-all-start.2 = ((bf16[32,128,256]{2,1,0:T(8,128)(2,1)}), bf16[32,128,256]{2,1,0:T(8,128)(2,1)S(1)}, u32[]{:S(2)}, u32[]{:S(2)}) async-start(bf16[32,128,256]{2,1,0:T(8,128)(2,1)} %get-tuple-element.25), calls=%async_computation.2 | async-start | bytes 4194304 | tf_op jit(solution)/shard_map/all_to_all | solution.py:580
  90.3 6.3 %ungroup.1 = bf16[16,128,128]{2,1,0:T(8,128)(2,1)} custom-call(bf16[16,64,256]{2,1,0:T(8,128)(2,1)} %get-tuple-element.26.res_ref), custom_call_target="tpu_custom_call" | custom-call | flops 1000 | bytes 1000 | tf_op jit(solution)/shard_map/ungroup/pallas_call | solution.py:413
  96.6 17.3 %all-to-all-done.2.refs_1_ = bf16[32,128,256]{2,1,0:T(8,128)(2,1)S(1)} async-done(((bf16[32,128,256]{2,1,0:T(8,128)(2,1)}), bf16[32,128,256]{2,1,0:T(8,128)(2,1)S(1)}, u32[]{:S(2)}, u32[]{:S(2)}) %all-to-all-start.2) | async-done | bytes 2097184 | tf_op jit(solution)/shard_map/all_to_all | solution.py:580
  113.9 2.7 %fold.1 = bf16[8,352,128]{2,1,0:T(8,128)(2,1)} custom-call(s32[32]{0:T(128)} %reshape.109.refs_0_, bf16[32,128,256]{2,1,0:T(8,128)(2,1)S(1)} %all-to-all-done.2.refs_1_), custom_call_target="tpu_custom_call" | custom-call | flops 1000 | bytes 1000 | tf_op jit(solution)/shard_map/fold/pallas_call | solution.py:454
  116.6 16.9 %all_to_all.24.refs_0_ = bf16[8,352,128]{2,1,0:T(8,128)(2,1)} all-to-all(bf16[8,352,128]{2,1,0:T(8,128)(2,1)} %fold.1), channel_id=1, replica_groups=mesh['sky'=16,'exp'=8] {'exp'}, dimensions={0} | all-to-all | bytes 1441792 | tf_op jit(solution)/shard_map/all_to_all | solution.py:584
  133.5 2.3 %finish.1 = (bf16[20,128]{1,0:T(8,128)(2,1)}, f32[256,128]{1,0:T(8,128)}, bf16[20,128]{1,0:T(8,128)(2,1)}) custom-call(bf16[8,352,128]{2,1,0:T(8,128)(2,1)} %all_to_all.24.refs_0_), custom_call_target="tpu_custom_call" | custom-call | flops 1000 | bytes 1000 | tf_op jit(solution)/shard_map/finish/pallas_call | solution.py:500
  135.8 4.4 %collective-permute-start.2 = (bf16[20,128]{1,0:T(8,128)(2,1)}, bf16[20,128]{1,0:T(8,128)(2,1)S(1)}, u32[]{:S(2)}, u32[]{:S(2)}) collective-permute-start(bf16[20,128]{1,0:T(8,128)(2,1)} %get-tuple-element.29), channel_id=1, source_target_pairs={{0,8},{8,16},{16,24},{24,32},{32,40},{40,48},{48,56},{56,64},{64,7... | collective-permute-start | bytes 15368 | tf_op jit(solution)/shard_map/ppermute | solution.py:49
  140.3 1.9 %collective-permute-start.3 = (bf16[20,128]{1,0:T(8,128)(2,1)}, bf16[20,128]{1,0:T(8,128)(2,1)S(1)}, u32[]{:S(2)}, u32[]{:S(2)}) collective-permute-start(bf16[20,128]{1,0:T(8,128)(2,1)} %get-tuple-element.30), channel_id=1, source_target_pairs={{8,0},{16,8},{24,16},{32,24},{40,32},{48,40},{56,48},{64,56},{72,6... | collective-permute-start | bytes 15368 | tf_op jit(solution)/shard_map/ppermute | solution.py:49
  142.2 0.0 collective-permute-done.2.above_ref
  142.2 5.9 %collective-permute-done.3.below_ref = bf16[20,128]{1,0:T(8,128)(2,1)S(1)} collective-permute-done((bf16[20,128]{1,0:T(8,128)(2,1)}, bf16[20,128]{1,0:T(8,128)(2,1)S(1)}, u32[]{:S(2)}, u32[]{:S(2)}) %collective-permute-start.3) | collective-permute-done | bytes 5152 | tf_op jit(solution)/shard_map/ppermute | solution.py:49
  148.1 1.4 rims.1
  (2 shorter events, 0.0 us)
Async XLA Ops:
  2.9 23.8 %collective-permute-start.1 = (bf16[20,1024]{1,0:T(8,128)(2,1)S(1)}, bf16[20,1024]{1,0:T(8,128)(2,1)S(1)}, u32[]{:S(2)}, u32[]{:S(2)}) collective-permute-start(bf16[20,1024]{1,0:T(8,128)(2,1)S(1)} %get-tuple-element.34), channel_id=1, source_target_pairs={{8,0},{16,8},{24,16},{32,24},{40,32},{48,40},{56,48},{64,56},{72,6... | collective-permute-start | bytes 122888 | tf_op jit(solution)/shard_map/ppermute | solution.py:49
  5.6 21.1 %collective-permute-start = (bf16[20,1024]{1,0:T(8,128)(2,1)S(1)}, bf16[20,1024]{1,0:T(8,128)(2,1)S(1)}, u32[]{:S(2)}, u32[]{:S(2)}) collective-permute-start(bf16[20,1024]{1,0:T(8,128)(2,1)S(1)} %get-tuple-element.35), channel_id=1, source_target_pairs={{0,8},{8,16},{16,24},{24,32},{32,40},{40,48},{48,56},{56,64},{64,7... | collective-permute-start | bytes 122888 | tf_op jit(solution)/shard_map/ppermute | solution.py:49
  11.6 13.4 %all-to-all-start = ((s32[16,1,2]{2,1,0:T(1,128)}), s32[16,1,2]{2,1,0:T(1,128)S(1)}, u32[]{:S(2)}, u32[]{:S(2)}) async-start(s32[16,1,2]{2,1,0:T(1,128)} %copy.13), calls=%async_computation | async-start | bytes 16384 | tf_op jit(solution)/shard_map/all_to_all | solution.py:562
  31.0 5.7 %copy-start = (bf16[16,1681]{1,0:T(8,128)(2,1)S(1)}, bf16[16,1681]{1,0:T(8,128)(2,1)}, u32[]{:S(2)}) copy-start(bf16[16,1681]{1,0:T(8,128)(2,1)} %param.13) | copy-start | bytes 161380
  31.0 30.9 %all-to-all-start.1 = ((bf16[32,240,128]{2,1,0:T(8,128)(2,1)}), bf16[32,240,128]{2,1,0:T(8,128)(2,1)S(1)}, u32[]{:S(2)}, u32[]{:S(2)}) async-start(bf16[32,240,128]{2,1,0:T(8,128)(2,1)} %cut.1), calls=%async_computation.1 | async-start | bytes 3932160 | tf_op jit(solution)/shard_map/all_to_all | solution.py:576
  54.6 6.6 %copy-start.1 = (s32[16,1]{0,1:T(1,128)S(1)}, s32[16,1]{0,1:T(1,128)}, u32[]{:S(2)}) copy-start(s32[16,1]{0,1:T(1,128)} %param.10) | copy-start | bytes 196
  83.1 30.9 %all-to-all-start.2 = ((bf16[32,128,256]{2,1,0:T(8,128)(2,1)}), bf16[32,128,256]{2,1,0:T(8,128)(2,1)S(1)}, u32[]{:S(2)}, u32[]{:S(2)}) async-start(bf16[32,128,256]{2,1,0:T(8,128)(2,1)} %get-tuple-element.25), calls=%async_computation.2 | async-start | bytes 4194304 | tf_op jit(solution)/shard_map/all_to_all | solution.py:580
  135.8 6.3 %collective-permute-start.2 = (bf16[20,128]{1,0:T(8,128)(2,1)}, bf16[20,128]{1,0:T(8,128)(2,1)S(1)}, u32[]{:S(2)}, u32[]{:S(2)}) collective-permute-start(bf16[20,128]{1,0:T(8,128)(2,1)} %get-tuple-element.29), channel_id=1, source_target_pairs={{0,8},{8,16},{16,24},{24,32},{32,40},{40,48},{48,56},{56,64},{64,7... | collective-permute-start | bytes 15368 | tf_op jit(solution)/shard_map/ppermute | solution.py:49
  140.3 7.8 %collective-permute-start.3 = (bf16[20,128]{1,0:T(8,128)(2,1)}, bf16[20,128]{1,0:T(8,128)(2,1)S(1)}, u32[]{:S(2)}, u32[]{:S(2)}) collective-permute-start(bf16[20,128]{1,0:T(8,128)(2,1)} %get-tuple-element.30), channel_id=1, source_target_pairs={{8,0},{16,8},{24,16},{32,24},{40,32},{48,40},{56,48},{64,56},{72,6... | collective-permute-start | bytes 15368 | tf_op jit(solution)/shard_map/ppermute | solution.py:49

commit v6 on v5

--- a/solution.py
+++ b/solution.py
@@ -23,7 +23,7 @@
 TILES = 6
 RES_LEAD = 40
 TAP_ROWS = 48
-OWN_FIRST = 3
+GROUP = 2
 BATCH = 4
 SLOTS = 8
 CHUNK = 9
@@ -182,69 +182,46 @@
     ]
 
 
-def own_kernel(stripe_ref, out_ref, pixels):
-    skip = 8 * OWN_FIRST - HALO
-    for tile, moved in enumerate(moved_tiles(stripe_ref[...])):
-        pixels[:, tile * LANES : (tile + 1) * LANES] = moved
-
+def blocks_kernel(stripe_ref, above_ref, below_ref, out_ref, pixels):
+    first = 0
+    for ref in (above_ref, stripe_ref, below_ref):
+        rows = ref.shape[0]
+        for tile, moved in enumerate(moved_tiles(ref[...])):
+            pixels[first : first + rows, tile * LANES : (tile + 1) * LANES] = moved
+        first += rows
+    pixels[first:, :] = jnp.zeros((TAIL, PITCH * G), F32)
     for row in range(out_ref.shape[0]):
-        first = skip + 8 * row
         tiles = [
-            pixels[first : first + 8, at : at + LANES] for at in range(0, PITCH * G, LANES)
+            pixels[8 * row : 8 * row + 8, at : at + LANES] for at in range(0, PITCH * G, LANES)
         ]
         out_ref[row] = swap_reversed(jnp.stack(tiles, 0)).reshape(PITCH, LANES)
 
 
-def own_blocks(stripe):
-    rows, columns = stripe.shape
-    count = (rows + HALO) // 8 - OWN_FIRST
-    return pl.pallas_call(
-        own_kernel,
-        in_specs=[pl.BlockSpec(memory_space=pltpu.VMEM)],
-        out_specs=pl.BlockSpec(memory_space=pltpu.VMEM),
-        out_shape=pltpu.VMEM((count, PITCH, LANES), F32),
-        scratch_shapes=[pltpu.VMEM((rows, PITCH * G), F32)],
-        cost_estimate=SMALL,
-        name="own",
-    )(stripe)
-
-
-def cut_kernel(
-    per_row, ids_ref, own_ref, above_ref, top_ref, bottom_ref, below_ref, out_ref, blocks, upper, lower, scratch
-):
+def stripe_blocks(stripe, above, below, half_rows):
+    return pl.pallas_call(
+        blocks_kernel,
+        in_specs=[whole_vmem(), whole_vmem(), whole_vmem()],
+        out_specs=whole_vmem(),
+        out_shape=pltpu.VMEM((half_rows, PITCH, LANES), F32),
+        scratch_shapes=[pltpu.VMEM((8 * half_rows, PITCH * G), F32)],
+        cost_estimate=SMALL,
+        name="blocks",
+    )(stripe, on_chip(above), on_chip(below))
+
+
+def cut_kernel(per_row, ids_ref, blocks_ref, out_ref, scratch):
     step = pl.program_id(0)
 
-    @pl.when(step == 0)
-    def _():
-        own = own_ref.shape[0]
-        blocks[OWN_FIRST : OWN_FIRST + own] = own_ref[...]
-        missing = 8 * OWN_FIRST - HALO
-        rims = ((above_ref, 0), (top_ref, 1), (bottom_ref, 2), (below_ref, 3))
-        tiles = {at: moved_tiles(ref[...]) for ref, at in rims}
-        lower[...] = jnp.zeros_like(lower)
-        for tile in range(PITCH // 8):
-            lanes = slice(tile * LANES, (tile + 1) * LANES)
-            upper[:HALO, lanes] = tiles[0][tile]
-            upper[HALO:, lanes] = tiles[1][tile][:missing]
-            lower[:missing, lanes] = tiles[2][tile][G - missing :]
-            lower[missing : missing + HALO, lanes] = tiles[3][tile]
-        for pixels, first in ((upper, 0), (lower, OWN_FIRST + own)):
-            for row in range(pixels.shape[0] // 8):
-                parts = [
-                    pixels[8 * row : 8 * row + 8, at : at + LANES]
-                    for at in range(0, PITCH * G, LANES)
-                ]
-                blocks[first + row] = swap_reversed(jnp.stack(parts, 0)).reshape(PITCH, LANES)
-
     def per_slot(n, carry):
-        wanted = ids_ref[step * SLOTS + n]
+        at = step * SLOTS + n
+        wanted = ids_ref[at // CAP, 0, at % CAP]
 
         @pl.when(wanted >= 0)
         def _():
             first_row = wanted // per_row * (2 * OUT)
             first_col = pl.multiple_of(wanted % per_row * OUT, 8)
             for row in range(2 * EXT - 1):
-                part = blocks[first_row + row, pl.ds(first_col, G), :]
+                part = blocks_ref[first_row + row, pl.ds(first_col, G), :]
                 scratch[EXT * row : EXT * row + G, :] = part
             out_ref[n] = scratch[...].astype(BF16)
 
@@ -253,34 +230,21 @@
     lax.fori_loop(0, SLOTS, per_slot, 0)
 
 
-def cut_patches(ids, own, stripe, above, below, half_rows):
-    slots = ids.shape[0]
-    rows, columns = stripe.shape
-    last = rows // G - 1
-    return pl.pallas_call(
-        lambda *refs: cut_kernel(columns // B, *refs),
+def cut_patches(ids, blocks, per_row):
+    slots = ids.shape[0] * CAP
+    return pl.pallas_call(
+        lambda *refs: cut_kernel(per_row, *refs),
         grid_spec=pltpu.PrefetchScalarGridSpec(
             num_scalar_prefetch=1,
             grid=(slots // SLOTS,),
-            in_specs=[
-                whole_vmem(),
-                whole_vmem(),
-                pl.BlockSpec((G, columns), lambda n, ids: (0, 0)),
-                pl.BlockSpec((G, columns), lambda n, ids: (last, 0)),
-                whole_vmem(),
-            ],
+            in_specs=[whole_vmem()],
             out_specs=pl.BlockSpec((SLOTS, PATCH_ROWS, LANES), lambda n, ids: (n, 0, 0)),
-            scratch_shapes=[
-                pltpu.VMEM((half_rows, PITCH, LANES), F32),
-                pltpu.VMEM((8 * OWN_FIRST, PITCH * G), F32),
-                pltpu.VMEM((8 * (half_rows - OWN_FIRST - own.shape[0]), PITCH * G), F32),
-                pltpu.VMEM((PATCH_ROWS, LANES), F32),
-            ],
+            scratch_shapes=[pltpu.VMEM((PATCH_ROWS, LANES), F32)],
         ),
         out_shape=jax.ShapeDtypeStruct((slots, PATCH_ROWS, LANES), BF16),
         cost_estimate=SMALL,
         name="cut",
-    )(ids, on_chip(own), on_chip(above), stripe, stripe, on_chip(below))
+    )(ids, on_chip(blocks))
 
 
 def block_taps(taps_ref, s, t):
@@ -330,56 +294,89 @@
     return jnp.concatenate([total[:, :LANES] + last, total[:, LANES:]], axis=1)
 
 
-def piece_kernel(slot_ref, cell_ref, patch_ref, taps_ref, data_ref, adj_out, res_out, field, resid):
-    piece = pl.program_id(0)
-
-    @pl.when(piece == 0)
+def pieces_kernel(slot_ref, cell_ref, patch_ref, *refs):
+    taps, refs = refs[:GROUP], refs[GROUP:]
+    data_ref, adjoints, res_out, field, resid, adj_slots, sems = refs
+    step = pl.program_id(0)
+    slots = lax.rem(step, 2)
+
+    @pl.when(step == 0)
     def _():
         resid[...] = jnp.zeros_like(resid)
 
-    field[...] = patch_ref[slot_ref[piece]].astype(F32)
-
-    def read_patch(d, t):
-        parts = []
-        for half in range(2):
-            for row in range(OUT):
-                at = EXT * (2 * (row + d) + half) + t
-                pair = [field[at : at + OUT, :], field[at + EXT : at + EXT + OUT, :]]
-                parts.append(jnp.concatenate(pair, axis=1))
-        return jnp.concatenate(parts, axis=0).astype(BF16)
-
-    predicted = correlate(read_patch, taps_ref)
-    observed = data_ref[0].astype(F32)
-    residual = jnp.where(observed < UNKNOWN, predicted - observed, 0.0).astype(BF16)
-    res_out[0] = residual
-    wide = residual.astype(F32)
-    for row in range(OUT):
-        first = RES_LEAD + EXT * row
-        resid[first : first + OUT, :] = wide[OUT * row : OUT * (row + 1)]
-
-    def read_residual(s, t):
-        return resid[pl.ds(RES_LEAD - EXT * s - t, SLOT_ROWS), :].astype(BF16)
-
-    adj_out[0] = convolve(read_residual, taps_ref, SLOT_ROWS).astype(BF16)
+    def sent(step):
+        at = lax.rem(step, 2)
+        return [
+            pltpu.make_async_copy(
+                adj_slots.at[at, i], adjoints.at[slot_ref[GROUP * step + i]], sems.at[at, i]
+            )
+            for i in range(GROUP)
+        ]
+
+    @pl.when(step >= 2)
+    def _():
+        for copy in sent(step - 2):
+            copy.wait()
+
+    def per_piece(i, taps_ref, field, resid):
+        field[...] = patch_ref[slot_ref[GROUP * step + i]].astype(F32)
+
+        def read_patch(d, t):
+            parts = []
+            for half in range(2):
+                for row in range(OUT):
+                    at = EXT * (2 * (row + d) + half) + t
+                    pair = [field[at : at + OUT, :], field[at + EXT : at + EXT + OUT, :]]
+                    parts.append(jnp.concatenate(pair, axis=1))
+            return jnp.concatenate(parts, axis=0).astype(BF16)
+
+        predicted = correlate(read_patch, taps_ref)
+        observed = data_ref[i].astype(F32)
+        residual = jnp.where(observed < UNKNOWN, predicted - observed, 0.0).astype(BF16)
+        res_out[i] = residual
+        wide = residual.astype(F32)
+        for row in range(OUT):
+            first = RES_LEAD + EXT * row
+            resid[first : first + OUT, :] = wide[OUT * row : OUT * (row + 1)]
+
+        def read_residual(s, t):
+            return resid[pl.ds(RES_LEAD - EXT * s - t, SLOT_ROWS), :].astype(BF16)
+
+        adj_slots[slots, i] = convolve(read_residual, taps_ref, SLOT_ROWS).astype(BF16)
+
+    for i in range(GROUP):
+        per_piece(i, taps[i], field.at[i], resid.at[i])
+    for copy in sent(step):
+        copy.start()
+
+    @pl.when(step == pl.num_programs(0) - 1)
+    def _():
+        for copy in sent(step - 1) + sent(step):
+            copy.wait()
 
 
 def pieces(slots, cells, patches, taps, data):
     count = data.shape[0]
-    slot = pl.BlockSpec((1, SLOT_ROWS, 2 * LANES), lambda p, slots, cells: (slots[p], 0, 0))
-    cell = pl.BlockSpec(
-        (1, REACH * LANES, TILES * LANES), lambda p, slots, cells: (cells[p], 0, 0)
-    )
-    block = pl.BlockSpec((1, BLOCKS, 2 * LANES), lambda p, slots, cells: (p, 0, 0))
-    return pl.pallas_call(
-        piece_kernel,
+    cell = [
+        pl.BlockSpec(
+            (1, REACH * LANES, TILES * LANES),
+            lambda p, slots, cells, i=i: (cells[GROUP * p + i], 0, 0),
+        )
+        for i in range(GROUP)
+    ]
+    block = pl.BlockSpec((GROUP, BLOCKS, 2 * LANES), lambda p, slots, cells: (p, 0, 0))
+    return pl.pallas_call(
+        pieces_kernel,
         grid_spec=pltpu.PrefetchScalarGridSpec(
             num_scalar_prefetch=2,
-            grid=(count,),
-            in_specs=[whole_vmem(), cell, block],
-            out_specs=[slot, block],
+            grid=(count // GROUP,),
+            in_specs=[whole_vmem(), *cell, block],
+            out_specs=[pl.BlockSpec(memory_space=pltpu.HBM), block],
             scratch_shapes=[
-                pltpu.VMEM((PATCH_ROWS, LANES), F32),
-                pltpu.VMEM((RES_LEAD + SLOT_ROWS, 2 * LANES), F32),
+                pltpu.VMEM((GROUP, PATCH_ROWS, LANES), F32),
+                pltpu.VMEM((GROUP, RES_LEAD + SLOT_ROWS, 2 * LANES), F32),
+                pltpu.VMEM((2, GROUP, SLOT_ROWS, 2 * LANES), BF16),
+                pltpu.SemaphoreType.DMA((2, GROUP)),
             ],
         ),
         out_shape=[
@@ -388,7 +385,7 @@
         ],
         cost_estimate=SMALL,
         name="pieces",
-    )(slots, cells, on_chip(patches), taps, data)
+    )(slots, cells, on_chip(patches), *[taps] * GROUP, data)
 
 
 def ungroup_kernel(res_ref, out_ref):
@@ -426,7 +423,7 @@
     inside = lax.broadcasted_iota(jnp.int32, (G, LANES), 0) < EXT
 
     def per_slot(n, carry):
-        named = ids_ref[n]
+        named = ids_ref[n // CAP, 0, n % CAP]
 
         @pl.when(named >= 0)
         def _():
@@ -558,21 +555,20 @@
         ],
         axis=1,
     )
-    requests, sky_model = lax.optimization_barrier((requests, sky_model))
-    asked = lax.all_to_all(requests, "sky", split_axis=0, concat_axis=0, tiled=True)
-    asked = asked.reshape(sky_count * CAP)
-
+    asked = lax.all_to_all(
+        requests[:, None, :], "sky", split_axis=0, concat_axis=0, tiled=True
+    )
     above = from_behind(sky_model[stripe_rows - HALO :], "sky", 1)
     below = from_behind(sky_model[:HALO], "sky", -1)
     half_rows = (stripe_rows + 2 * HALO + TAIL) // 8
-    own = own_blocks(sky_model)
-    asked, own = lax.optimization_barrier((asked, own))
-    outgoing = cut_patches(asked, own, sky_model, above, below, half_rows)
-    exposure_data, pixel_mask, psf_table, code, _ = lax.optimization_barrier(
-        (exposure_data, pixel_mask, psf_table, code, outgoing)
-    )
     second = jnp.any(mine & (first[:, None] < code[None, :]), axis=0)
     slot_index = owner_sky * CAP + second.astype(jnp.int32)
+    asked, above, below, slot_index = lax.optimization_barrier((asked, above, below, slot_index))
+    blocks = stripe_blocks(sky_model, above, below, half_rows)
+    outgoing = cut_patches(asked, blocks, per_row)
+    exposure_data, pixel_mask, psf_table, _ = lax.optimization_barrier(
+        (exposure_data, pixel_mask, psf_table, outgoing)
+    )
     patches = lax.all_to_all(outgoing, "sky", split_axis=0, concat_axis=0, tiled=True)
     data = regroup(exposure_data, pixel_mask)
     taps = build_taps(psf_table)

time: 151 us -> 145 us (0.960)
  Pallas kernels: 63.8 us -> 59.4 us
  waiting for transfers between devices: 26.6 us -> 23.1 us
  starting transfers between devices: 35.1 us -> 38 us
    pallas_call x3, Pallas kernels: 27.5 us -> 22.8 us  [the longest x1 17.4 us: pieces(): pl.pallas_call(pieces_kernel, grid_spec=pltpu.PrefetchScalarGridSpec(num_...]
    all_to_all x1, waiting for transfers between devices: 3.41 us -> 0.01 us  [shards(): lax.all_to_all(requests[:, None, :], 'sky', split_axis=0, concat_axis=0,...]
    all_to_all x1, starting transfers between devices: 5.73 us -> 7.77 us  [shards(): lax.all_to_all(outgoing, 'sky', split_axis=0, concat_axis=0, tiled=True)]
  transfers between devices with their start and end apart: 7 -> 7, of which waited for: 3 -> 2; matrix products, arithmetic and copies ran while one was open for 3% -> 3% of each run, Pallas kernels for 21% -> 21%
where the time goes in v6:
time: 145 us; the launch traced here: 144 us
  Pallas kernels  59.4 us (41%)
  starting transfers between devices  38 us (26%)
  waiting for transfers between devices  23.1 us (16%)
  blocking collectives  16.9 us (12%)
  other arithmetic  3.39 us (2%)
  local copies, waits for them, and re-layouts  2.47 us (2%)
    pallas_call x1, Pallas kernels, pieces(): pl.pallas_call(pieces_kernel, grid_spec=pltpu.PrefetchScalarGridSpec(num_...  17.4 us
    all_to_all x1, waiting for transfers between devices, shards(): lax.all_to_all(adjoints, 'sky', split_axis=0, concat_axis=0, tiled=True)  17.2 us
    all_to_all x1, blocking collectives, shards(): lax.all_to_all(partial, 'exp', split_axis=0, concat_axis=0, tiled=True)  16.9 us
    pallas_call x1, Pallas kernels, build_taps(): pl.pallas_call(taps_kernel, grid=(cells,), in_specs=[pl.BlockSpec((1, TAP...  16.9 us
    ppermute x4, starting transfers between devices, from_behind(): return lax.ppermute(x, axis, pairs)  14.8 us
    all_to_all x1, starting transfers between devices, shards(): lax.all_to_all(requests[:, None, :], 'sky', split_axis=0, concat_axis=0,...  8.18 us
    all_to_all x1, starting transfers between devices, shards(): lax.all_to_all(outgoing, 'sky', split_axis=0, concat_axis=0, tiled=True)  7.77 us
    all_to_all x1, starting transfers between devices, shards(): lax.all_to_all(adjoints, 'sky', split_axis=0, concat_axis=0, tiled=True)  7.23 us
  transfers between devices with their start and end apart: 7, of which 2 were waited for; matrix products, arithmetic and copies ran while one was open for 3% of the time, Pallas kernels for 21%

profile of v6, /device:TPU:24, one launch (start us, length us, event | category | flops | bytes accessed | tf_op | source)
XLA Modules:
  0.0 144.0 jit_solution(16226900671338009102)
XLA Ops:
  0.6 0.7 multiply_add_fusion
  1.3 0.8 select_reduce_fusion.1
  2.1 0.7 copy.12
  2.8 8.2 %all-to-all-start = ((s32[16,1,2]{2,1,0:T(1,128)}), s32[16,1,2]{2,1,0:T(1,128)S(1)}, u32[]{:S(2)}, u32[]{:S(2)}) async-start(s32[16,1,2]{2,1,0:T(1,128)} %copy.12), calls=%async_computation | async-start | bytes 16384 | tf_op jit(solution)/shard_map/all_to_all | solution.py:558
  11.0 0.8 fusion.4
  11.8 2.8 %collective-permute-start.1 = (bf16[20,1024]{1,0:T(8,128)(2,1)S(1)}, bf16[20,1024]{1,0:T(8,128)(2,1)S(1)}, u32[]{:S(2)}, u32[]{:S(2)}) collective-permute-start(bf16[20,1024]{1,0:T(8,128)(2,1)S(1)} %get-tuple-element.32), channel_id=1, source_target_pairs={{8,0},{16,8},{24,16},{32,24},{40,32},{48,40},{56,48},{64,56},{72,6... | collective-permute-start | bytes 122888 | tf_op jit(solution)/shard_map/ppermute | solution.py:49
  14.6 5.2 %collective-permute-start = (bf16[20,1024]{1,0:T(8,128)(2,1)S(1)}, bf16[20,1024]{1,0:T(8,128)(2,1)S(1)}, u32[]{:S(2)}, u32[]{:S(2)}) collective-permute-start(bf16[20,1024]{1,0:T(8,128)(2,1)S(1)} %get-tuple-element.33), channel_id=1, source_target_pairs={{0,8},{8,16},{16,24},{24,32},{32,40},{40,48},{48,56},{56,64},{64,7... | collective-permute-start | bytes 122888 | tf_op jit(solution)/shard_map/ppermute | solution.py:49
  19.8 0.7 fusion.1
  20.5 1.2 convert_add_fusion.slot_ref
  21.7 0.0 all-to-all-done.refs_0_
  21.7 0.0 copy-start
  21.7 0.0 collective-permute-done.1.below_ref
  21.7 0.0 collective-permute-done.above_ref
  21.7 2.2 %blocks.1.refs_1_ = f32[38,72,128]{2,1,0:T(8,128)S(1)} custom-call(bf16[256,1024]{1,0:T(8,128)(2,1)} %stripe_ref.1, bf16[20,1024]{1,0:T(8,128)(2,1)S(1)} %collective-permute-done.above_ref, bf16[20,1024]{1,0:T(8,128)(2,1)S(1)} %collective-permute-done.1.below_ref), custom_call_target="tpu_custom_call" | custom-call | flops 1000 | bytes 1000 | tf_op jit(solution)/shard_map/blocks/pallas_call | solution.py:201
  24.0 0.0 copy-done
  24.0 3.1 %cut.1 = bf16[32,240,128]{2,1,0:T(8,128)(2,1)} custom-call(s32[16,1,2]{2,1,0:T(1,128)} %copy-done, f32[38,72,128]{2,1,0:T(8,128)S(1)} %blocks.1.refs_1_), custom_call_target="tpu_custom_call" | custom-call | flops 1000 | bytes 1000 | tf_op jit(solution)/shard_map/cut/pallas_call | solution.py:235
  27.1 0.0 copy-start.1
  27.1 7.8 %all-to-all-start.1 = ((bf16[32,240,128]{2,1,0:T(8,128)(2,1)}), bf16[32,240,128]{2,1,0:T(8,128)(2,1)S(1)}, u32[]{:S(2)}, u32[]{:S(2)}) async-start(bf16[32,240,128]{2,1,0:T(8,128)(2,1)} %cut.1), calls=%async_computation.1 | async-start | bytes 3932160 | tf_op jit(solution)/shard_map/all_to_all | solution.py:572
  34.9 0.0 copy-done.1
  34.9 0.2 reshape.102
  35.1 0.7 pad.4.kernel_ref
  35.9 16.9 %taps.1.refs_0_.refs_1_ = bf16[16,512,768]{2,1,0:T(8,128)(2,1)} custom-call(bf16[16,48,128]{2,1,0:T(8,128)(2,1)} %pad.4.kernel_ref), custom_call_target="tpu_custom_call" | custom-call | flops 1000 | bytes 1000 | tf_op jit(solution)/shard_map/taps/pallas_call | solution.py:159
  52.8 6.6 %regroup.1.refs_2_ = bf16[16,64,256]{2,1,0:T(8,128)(2,1)} custom-call(bf16[16,128,128]{2,1,0:T(8,128)(2,1)} %data_ref, s32[16,128,128]{2,1,0:T(8,128)} %keep_ref), custom_call_target="tpu_custom_call" | custom-call | flops 1000 | bytes 1000 | tf_op jit(solution)/shard_map/regroup/pallas_call | solution.py:98
  59.4 0.0 all-to-all-done.1.patch_ref
  59.4 17.4 %pieces.1 = (bf16[32,128,256]{2,1,0:T(8,128)(2,1)}, bf16[16,64,256]{2,1,0:T(8,128)(2,1)}) custom-call(s32[16]{0:T(128)} %convert_add_fusion.slot_ref, s32[16]{0:T(128)} %cell_ref.1, bf16[32,240,128]{2,1,0:T(8,128)(2,1)S(1)} %all-to-all-done.1.patch_ref, bf16[16,512,768]{2,1,0:T(8,128)(2,1)} %taps.1.refs_0_.refs_1_, ...), custom_call_target="tpu_custom_call" | custom-call | flops 1000 | bytes 1000 | tf_op jit(solution)/shard_map/pieces/pallas_call | solution.py:368
  76.8 7.2 %all-to-all-start.2 = ((bf16[32,128,256]{2,1,0:T(8,128)(2,1)}), bf16[32,128,256]{2,1,0:T(8,128)(2,1)S(1)}, u32[]{:S(2)}, u32[]{:S(2)}) async-start(bf16[32,128,256]{2,1,0:T(8,128)(2,1)} %get-tuple-element.23), calls=%async_computation.2 | async-start | bytes 4194304 | tf_op jit(solution)/shard_map/all_to_all | solution.py:576
  84.0 6.3 %ungroup.1 = bf16[16,128,128]{2,1,0:T(8,128)(2,1)} custom-call(bf16[16,64,256]{2,1,0:T(8,128)(2,1)} %get-tuple-element.24.res_ref), custom_call_target="tpu_custom_call" | custom-call | flops 1000 | bytes 1000 | tf_op jit(solution)/shard_map/ungroup/pallas_call | solution.py:410
  90.4 17.2 %all-to-all-done.2.refs_1_ = bf16[32,128,256]{2,1,0:T(8,128)(2,1)S(1)} async-done(((bf16[32,128,256]{2,1,0:T(8,128)(2,1)}), bf16[32,128,256]{2,1,0:T(8,128)(2,1)S(1)}, u32[]{:S(2)}, u32[]{:S(2)}) %all-to-all-start.2) | async-done | bytes 2097184 | tf_op jit(solution)/shard_map/all_to_all | solution.py:576
  107.5 3.1 %fold.1 = bf16[8,352,128]{2,1,0:T(8,128)(2,1)} custom-call(s32[16,1,2]{2,1,0:T(1,128)} %copy-done, bf16[32,128,256]{2,1,0:T(8,128)(2,1)S(1)} %all-to-all-done.2.refs_1_), custom_call_target="tpu_custom_call" | custom-call | flops 1000 | bytes 1000 | tf_op jit(solution)/shard_map/fold/pallas_call | solution.py:451
  110.6 16.9 %all_to_all.20.refs_0_ = bf16[8,352,128]{2,1,0:T(8,128)(2,1)} all-to-all(bf16[8,352,128]{2,1,0:T(8,128)(2,1)} %fold.1), channel_id=1, replica_groups=mesh['sky'=16,'exp'=8] {'exp'}, dimensions={0} | all-to-all | bytes 1441792 | tf_op jit(solution)/shard_map/all_to_all | solution.py:580
  127.6 2.3 %finish.1 = (bf16[20,128]{1,0:T(8,128)(2,1)}, f32[256,128]{1,0:T(8,128)}, bf16[20,128]{1,0:T(8,128)(2,1)}) custom-call(bf16[8,352,128]{2,1,0:T(8,128)(2,1)} %all_to_all.20.refs_0_), custom_call_target="tpu_custom_call" | custom-call | flops 1000 | bytes 1000 | tf_op jit(solution)/shard_map/finish/pallas_call | solution.py:497
  129.9 5.0 %collective-permute-start.2 = (bf16[20,128]{1,0:T(8,128)(2,1)}, bf16[20,128]{1,0:T(8,128)(2,1)S(1)}, u32[]{:S(2)}, u32[]{:S(2)}) collective-permute-start(bf16[20,128]{1,0:T(8,128)(2,1)} %get-tuple-element.27), channel_id=1, source_target_pairs={{0,8},{8,16},{16,24},{24,32},{32,40},{40,48},{48,56},{56,64},{64,7... | collective-permute-start | bytes 15368 | tf_op jit(solution)/shard_map/ppermute | solution.py:49
  134.8 1.9 %collective-permute-start.3 = (bf16[20,128]{1,0:T(8,128)(2,1)}, bf16[20,128]{1,0:T(8,128)(2,1)S(1)}, u32[]{:S(2)}, u32[]{:S(2)}) collective-permute-start(bf16[20,128]{1,0:T(8,128)(2,1)} %get-tuple-element.28), channel_id=1, source_target_pairs={{8,0},{16,8},{24,16},{32,24},{40,32},{48,40},{56,48},{64,56},{72,6... | collective-permute-start | bytes 15368 | tf_op jit(solution)/shard_map/ppermute | solution.py:49
  136.8 0.0 collective-permute-done.2.above_ref
  136.8 5.9 %collective-permute-done.3.below_ref = bf16[20,128]{1,0:T(8,128)(2,1)S(1)} collective-permute-done((bf16[20,128]{1,0:T(8,128)(2,1)}, bf16[20,128]{1,0:T(8,128)(2,1)S(1)}, u32[]{:S(2)}, u32[]{:S(2)}) %collective-permute-start.3) | collective-permute-done | bytes 5152 | tf_op jit(solution)/shard_map/ppermute | solution.py:49
  142.7 1.4 rims.1
  (2 shorter events, 0.0 us)
Async XLA Ops:
  2.8 18.9 %all-to-all-start = ((s32[16,1,2]{2,1,0:T(1,128)}), s32[16,1,2]{2,1,0:T(1,128)S(1)}, u32[]{:S(2)}, u32[]{:S(2)}) async-start(s32[16,1,2]{2,1,0:T(1,128)} %copy.12), calls=%async_computation | async-start | bytes 16384 | tf_op jit(solution)/shard_map/all_to_all | solution.py:558
  11.8 9.9 %collective-permute-start.1 = (bf16[20,1024]{1,0:T(8,128)(2,1)S(1)}, bf16[20,1024]{1,0:T(8,128)(2,1)S(1)}, u32[]{:S(2)}, u32[]{:S(2)}) collective-permute-start(bf16[20,1024]{1,0:T(8,128)(2,1)S(1)} %get-tuple-element.32), channel_id=1, source_target_pairs={{8,0},{16,8},{24,16},{32,24},{40,32},{48,40},{56,48},{64,56},{72,6... | collective-permute-start | bytes 122888 | tf_op jit(solution)/shard_map/ppermute | solution.py:49
  14.6 7.1 %collective-permute-start = (bf16[20,1024]{1,0:T(8,128)(2,1)S(1)}, bf16[20,1024]{1,0:T(8,128)(2,1)S(1)}, u32[]{:S(2)}, u32[]{:S(2)}) collective-permute-start(bf16[20,1024]{1,0:T(8,128)(2,1)S(1)} %get-tuple-element.33), channel_id=1, source_target_pairs={{0,8},{8,16},{16,24},{24,32},{32,40},{40,48},{48,56},{56,64},{64,7... | collective-permute-start | bytes 122888 | tf_op jit(solution)/shard_map/ppermute | solution.py:49
  21.7 2.3 %copy-start = (s32[16,1,2]{2,1,0:T(1,128)}, s32[16,1,2]{2,1,0:T(1,128)S(1)}, u32[]{:S(2)}) copy-start(s32[16,1,2]{2,1,0:T(1,128)S(1)} %all-to-all-done.refs_0_) | copy-start | bytes 388
  27.1 7.8 %copy-start.1 = (bf16[16,1681]{1,0:T(8,128)(2,1)S(1)}, bf16[16,1681]{1,0:T(8,128)(2,1)}, u32[]{:S(2)}) copy-start(bf16[16,1681]{1,0:T(8,128)(2,1)} %param.13) | copy-start | bytes 161380
  27.1 32.3 %all-to-all-start.1 = ((bf16[32,240,128]{2,1,0:T(8,128)(2,1)}), bf16[32,240,128]{2,1,0:T(8,128)(2,1)S(1)}, u32[]{:S(2)}, u32[]{:S(2)}) async-start(bf16[32,240,128]{2,1,0:T(8,128)(2,1)} %cut.1), calls=%async_computation.1 | async-start | bytes 3932160 | tf_op jit(solution)/shard_map/all_to_all | solution.py:572
  76.8 30.7 %all-to-all-start.2 = ((bf16[32,128,256]{2,1,0:T(8,128)(2,1)}), bf16[32,128,256]{2,1,0:T(8,128)(2,1)S(1)}, u32[]{:S(2)}, u32[]{:S(2)}) async-start(bf16[32,128,256]{2,1,0:T(8,128)(2,1)} %get-tuple-element.23), calls=%async_computation.2 | async-start | bytes 4194304 | tf_op jit(solution)/shard_map/all_to_all | solution.py:576
  129.9 6.9 %collective-permute-start.2 = (bf16[20,128]{1,0:T(8,128)(2,1)}, bf16[20,128]{1,0:T(8,128)(2,1)S(1)}, u32[]{:S(2)}, u32[]{:S(2)}) collective-permute-start(bf16[20,128]{1,0:T(8,128)(2,1)} %get-tuple-element.27), channel_id=1, source_target_pairs={{0,8},{8,16},{16,24},{24,32},{32,40},{40,48},{48,56},{56,64},{64,7... | collective-permute-start | bytes 15368 | tf_op jit(solution)/shard_map/ppermute | solution.py:49
  134.8 7.8 %collective-permute-start.3 = (bf16[20,128]{1,0:T(8,128)(2,1)}, bf16[20,128]{1,0:T(8,128)(2,1)S(1)}, u32[]{:S(2)}, u32[]{:S(2)}) collective-permute-start(bf16[20,128]{1,0:T(8,128)(2,1)} %get-tuple-element.28), channel_id=1, source_target_pairs={{8,0},{16,8},{24,16},{32,24},{40,32},{48,40},{56,48},{64,56},{72,6... | collective-permute-start | bytes 15368 | tf_op jit(solution)/shard_map/ppermute | solution.py:49

commit v7 on v6

--- a/solution.py
+++ b/solution.py
@@ -17,7 +17,8 @@
 REACH = 4
 TAIL = 8
 BLOCKS = OUT * OUT
-PATCH_ROWS = 240
+PATCH_ROWS = 232
+ADJ_ROWS = 240
 SLOT_ROWS = 128
 PITCH = 72
 TILES = 6
@@ -151,11 +152,13 @@
     lax.fori_loop(0, REACH, per_shift, 0)
 
 
-def build_taps(table):
-    cells = table.shape[0]
-    kernels = jnp.pad(
-        table.reshape(cells, PSF, PSF), ((0, 0), (0, TAP_ROWS - PSF), (0, LANES - PSF))
-    )
+def padded_kernels(table):
+    kernels = table.reshape(table.shape[0], PSF, PSF)
+    return jnp.pad(kernels, ((0, 0), (0, TAP_ROWS - PSF), (0, LANES - PSF)))
+
+
+def build_taps(kernels):
+    cells = kernels.shape[0]
     return pl.pallas_call(
         taps_kernel,
         grid=(cells,),
@@ -223,7 +226,7 @@
             for row in range(2 * EXT - 1):
                 part = blocks_ref[first_row + row, pl.ds(first_col, G), :]
                 scratch[EXT * row : EXT * row + G, :] = part
-            out_ref[n] = scratch[...].astype(BF16)
+            out_ref[n] = scratch[:PATCH_ROWS, :].astype(BF16)
 
         return carry
 
@@ -239,7 +242,7 @@
             grid=(slots // SLOTS,),
             in_specs=[whole_vmem()],
             out_specs=pl.BlockSpec((SLOTS, PATCH_ROWS, LANES), lambda n, ids: (n, 0, 0)),
-            scratch_shapes=[pltpu.VMEM((PATCH_ROWS, LANES), F32)],
+            scratch_shapes=[pltpu.VMEM((PATCH_ROWS + 8, LANES), F32)],
         ),
         out_shape=jax.ShapeDtypeStruct((slots, PATCH_ROWS, LANES), BF16),
         cost_estimate=SMALL,
@@ -342,7 +345,9 @@
         def read_residual(s, t):
             return resid[pl.ds(RES_LEAD - EXT * s - t, SLOT_ROWS), :].astype(BF16)
 
-        adj_slots[slots, i] = convolve(read_residual, taps_ref, SLOT_ROWS).astype(BF16)
+        adjoint = convolve(read_residual, taps_ref, SLOT_ROWS).astype(BF16)
+        adj_slots[slots, i, :SLOT_ROWS] = adjoint[:, :LANES]
+        adj_slots[slots, i, SLOT_ROWS:] = adjoint[: ADJ_ROWS - SLOT_ROWS, LANES:]
 
     for i in range(GROUP):
         per_piece(i, taps[i], field.at[i], resid.at[i])
@@ -375,12 +380,12 @@
             scratch_shapes=[
                 pltpu.VMEM((GROUP, PATCH_ROWS, LANES), F32),
                 pltpu.VMEM((GROUP, RES_LEAD + SLOT_ROWS, 2 * LANES), F32),
-                pltpu.VMEM((2, GROUP, SLOT_ROWS, 2 * LANES), BF16),
+                pltpu.VMEM((2, GROUP, ADJ_ROWS, LANES), BF16),
                 pltpu.SemaphoreType.DMA((2, GROUP)),
             ],
         ),
         out_shape=[
-            jax.ShapeDtypeStruct((patches.shape[0], SLOT_ROWS, 2 * LANES), BF16),
+            jax.ShapeDtypeStruct((patches.shape[0], ADJ_ROWS, LANES), BF16),
             jax.ShapeDtypeStruct(data.shape, BF16),
         ],
         cost_estimate=SMALL,
@@ -429,11 +434,11 @@
         def _():
             first_row = named // per_row * (2 * OUT)
             first_col = pl.multiple_of(named % per_row * OUT, 8)
-            scratch[...] = slot_ref[n].astype(F32)
+            scratch[:ADJ_ROWS, :] = slot_ref[n].astype(F32)
             for row in range(EXT):
-                for half in range(2):
-                    part = scratch[pl.ds(EXT * row, G), half * LANES : (half + 1) * LANES]
-                    part = jnp.where(inside, part, 0.0)
+                for half in range(2 if row < EXT - 1 else 1):
+                    first = SLOT_ROWS * half + EXT * row
+                    part = jnp.where(inside, scratch[first : first + G, :], 0.0)
                     at = (first_row + 2 * row + half, pl.ds(first_col, G), slice(None))
                     canvas[at] = canvas[at] + part
 
@@ -457,10 +462,10 @@
         out_specs=pl.BlockSpec(memory_space=pltpu.VMEM),
         scratch_shapes=[
             pltpu.VMEM((half_rows, PITCH + 8, LANES), F32),
-            pltpu.VMEM((SLOT_ROWS, 2 * LANES), F32),
+            pltpu.VMEM((ADJ_ROWS + 8, LANES), F32),
             pltpu.VMEM((CHUNK_ROWS, LANES), F32),
         ],
-        out_shape=jax.ShapeDtypeStruct((per_row, CHUNK_ROWS, LANES), BF16),
+        out_shape=pltpu.VMEM((per_row, CHUNK_ROWS, LANES), BF16),
         cost_estimate=SMALL,
         name="fold",
     )(ids, on_chip(received))
@@ -492,7 +497,7 @@
 
 
 def finish(terms, half_rows, rows):
-    rim = jax.ShapeDtypeStruct((HALO, LANES), BF16)
+    rim = pltpu.VMEM((HALO, LANES), BF16)
     vmem = pl.BlockSpec(memory_space=pltpu.VMEM)
     return pl.pallas_call(
         lambda *refs: finish_kernel(half_rows, *refs),
@@ -505,7 +510,7 @@
         ],
         cost_estimate=SMALL,
         name="finish",
-    )(terms)
+    )(on_chip(terms))
 
 
 def rims_kernel(middle_ref, above_ref, below_ref, out_ref):
@@ -563,15 +568,16 @@
     half_rows = (stripe_rows + 2 * HALO + TAIL) // 8
     second = jnp.any(mine & (first[:, None] < code[None, :]), axis=0)
     slot_index = owner_sky * CAP + second.astype(jnp.int32)
+    kernels = padded_kernels(psf_table)
     asked, above, below, slot_index = lax.optimization_barrier((asked, above, below, slot_index))
     blocks = stripe_blocks(sky_model, above, below, half_rows)
     outgoing = cut_patches(asked, blocks, per_row)
-    exposure_data, pixel_mask, psf_table, _ = lax.optimization_barrier(
-        (exposure_data, pixel_mask, psf_table, outgoing)
+    exposure_data, pixel_mask, kernels, _ = lax.optimization_barrier(
+        (exposure_data, pixel_mask, kernels, outgoing)
     )
     patches = lax.all_to_all(outgoing, "sky", split_axis=0, concat_axis=0, tiled=True)
     data = regroup(exposure_data, pixel_mask)
-    taps = build_taps(psf_table)
+    taps = build_taps(kernels)
     adjoints, residuals = pieces(slot_index, psf_cell, patches, taps, data)
     received = lax.all_to_all(adjoints, "sky", split_axis=0, concat_axis=0, tiled=True)
     received, residual = lax.optimization_barrier((received, ungroup(residuals)))

time: 145 us -> 141 us (0.972)
  Pallas kernels: 59.4 us -> 57.9 us
where the time goes in v7:
time: 141 us; the launch traced here: 140 us
  Pallas kernels  57.9 us (41%)
  starting transfers between devices  37.2 us (26%)
  waiting for transfers between devices  21.7 us (15%)
  blocking collectives  16.7 us (12%)
  other arithmetic  3.44 us (2%)
  local copies, waits for them, and re-layouts  2.47 us (2%)
    pallas_call x1, Pallas kernels, pieces(): pl.pallas_call(pieces_kernel, grid_spec=pltpu.PrefetchScalarGridSpec(num_...  17.9 us
    pallas_call x1, Pallas kernels, build_taps(): pl.pallas_call(taps_kernel, grid=(cells,), in_specs=[pl.BlockSpec((1, TAP...  16.9 us
    all_to_all x1, blocking collectives, shards(): lax.all_to_all(partial, 'exp', split_axis=0, concat_axis=0, tiled=True)  16.7 us
    all_to_all x1, waiting for transfers between devices, shards(): lax.all_to_all(adjoints, 'sky', split_axis=0, concat_axis=0, tiled=True)  16 us
    ppermute x4, starting transfers between devices, from_behind(): return lax.ppermute(x, axis, pairs)  14.4 us
    all_to_all x1, starting transfers between devices, shards(): lax.all_to_all(requests[:, None, :], 'sky', split_axis=0, concat_axis=0,...  8.18 us
    all_to_all x1, starting transfers between devices, shards(): lax.all_to_all(outgoing, 'sky', split_axis=0, concat_axis=0, tiled=True)  7.68 us
    all_to_all x1, starting transfers between devices, shards(): lax.all_to_all(adjoints, 'sky', split_axis=0, concat_axis=0, tiled=True)  6.86 us
  transfers between devices with their start and end apart: 7, of which 2 were waited for; matrix products, arithmetic and copies ran while one was open for 3% of the time, Pallas kernels for 21%

profile of v7, /device:TPU:24, one launch (start us, length us, event | category | flops | bytes accessed | tf_op | source)
XLA Modules:
  0.0 140.1 jit_solution(2471730624844786378)
XLA Ops:
  0.6 0.7 multiply_add_fusion
  1.3 0.8 select_reduce_fusion.1
  2.1 0.7 copy.12
  2.8 8.2 %all-to-all-start = ((s32[16,1,2]{2,1,0:T(1,128)}), s32[16,1,2]{2,1,0:T(1,128)S(1)}, u32[]{:S(2)}, u32[]{:S(2)}) async-start(s32[16,1,2]{2,1,0:T(1,128)} %copy.12), calls=%async_computation | async-start | bytes 16384 | tf_op jit(solution)/shard_map/all_to_all | solution.py:563
  11.0 0.8 fusion.4
  11.8 2.8 %collective-permute-start.1 = (bf16[20,1024]{1,0:T(8,128)(2,1)S(1)}, bf16[20,1024]{1,0:T(8,128)(2,1)S(1)}, u32[]{:S(2)}, u32[]{:S(2)}) collective-permute-start(bf16[20,1024]{1,0:T(8,128)(2,1)S(1)} %get-tuple-element.32), channel_id=1, source_target_pairs={{8,0},{16,8},{24,16},{32,24},{40,32},{48,40},{56,48},{64,56},{72,6... | collective-permute-start | bytes 122888 | tf_op jit(solution)/shard_map/ppermute | solution.py:50
  14.6 5.2 %collective-permute-start = (bf16[20,1024]{1,0:T(8,128)(2,1)S(1)}, bf16[20,1024]{1,0:T(8,128)(2,1)S(1)}, u32[]{:S(2)}, u32[]{:S(2)}) collective-permute-start(bf16[20,1024]{1,0:T(8,128)(2,1)S(1)} %get-tuple-element.33), channel_id=1, source_target_pairs={{0,8},{8,16},{16,24},{24,32},{32,40},{40,48},{48,56},{56,64},{64,7... | collective-permute-start | bytes 122888 | tf_op jit(solution)/shard_map/ppermute | solution.py:50
  19.8 0.7 fusion.1
  20.5 1.2 convert_add_fusion.slot_ref
  21.7 0.0 all-to-all-done.refs_0_
  21.8 0.0 copy-start
  21.8 0.0 collective-permute-done.1.below_ref
  21.8 0.0 collective-permute-done.above_ref
  21.8 2.2 %blocks.1.refs_1_ = f32[38,72,128]{2,1,0:T(8,128)S(1)} custom-call(bf16[256,1024]{1,0:T(8,128)(2,1)} %stripe_ref.1, bf16[20,1024]{1,0:T(8,128)(2,1)S(1)} %collective-permute-done.above_ref, bf16[20,1024]{1,0:T(8,128)(2,1)S(1)} %collective-permute-done.1.below_ref), custom_call_target="tpu_custom_call" | custom-call | flops 1000 | bytes 1000 | tf_op jit(solution)/shard_map/blocks/pallas_call | solution.py:204
  24.0 0.0 copy-done
  24.0 3.2 %cut.1 = bf16[32,232,128]{2,1,0:T(8,128)(2,1)} custom-call(s32[16,1,2]{2,1,0:T(1,128)} %copy-done, f32[38,72,128]{2,1,0:T(8,128)S(1)} %blocks.1.refs_1_), custom_call_target="tpu_custom_call" | custom-call | flops 1000 | bytes 1000 | tf_op jit(solution)/shard_map/cut/pallas_call | solution.py:238
  27.2 0.0 copy-start.1
  27.2 7.7 %all-to-all-start.1 = ((bf16[32,232,128]{2,1,0:T(8,128)(2,1)}), bf16[32,232,128]{2,1,0:T(8,128)(2,1)S(1)}, u32[]{:S(2)}, u32[]{:S(2)}) async-start(bf16[32,232,128]{2,1,0:T(8,128)(2,1)} %cut.1), calls=%async_computation.1 | async-start | bytes 3801088 | tf_op jit(solution)/shard_map/all_to_all | solution.py:578
  34.9 0.0 copy-done.1
  34.9 0.2 reshape.102
  35.1 0.7 pad.4.kernel_ref
  35.8 16.9 %taps.1.refs_0_.refs_1_ = bf16[16,512,768]{2,1,0:T(8,128)(2,1)} custom-call(bf16[16,48,128]{2,1,0:T(8,128)(2,1)} %pad.4.kernel_ref), custom_call_target="tpu_custom_call" | custom-call | flops 1000 | bytes 1000 | tf_op jit(solution)/shard_map/taps/pallas_call | solution.py:162
  52.7 6.6 %regroup.1.refs_2_ = bf16[16,64,256]{2,1,0:T(8,128)(2,1)} custom-call(bf16[16,128,128]{2,1,0:T(8,128)(2,1)} %data_ref, s32[16,128,128]{2,1,0:T(8,128)} %keep_ref), custom_call_target="tpu_custom_call" | custom-call | flops 1000 | bytes 1000 | tf_op jit(solution)/shard_map/regroup/pallas_call | solution.py:99
  59.4 0.0 all-to-all-done.1.patch_ref
  59.4 17.9 %pieces.1 = (bf16[32,240,128]{2,1,0:T(8,128)(2,1)}, bf16[16,64,256]{2,1,0:T(8,128)(2,1)}) custom-call(s32[16]{0:T(128)} %convert_add_fusion.slot_ref, s32[16]{0:T(128)} %cell_ref.1, bf16[32,232,128]{2,1,0:T(8,128)(2,1)S(1)} %all-to-all-done.1.patch_ref, bf16[16,512,768]{2,1,0:T(8,128)(2,1)} %taps.1.refs_0_.refs_1_, ...), custom_call_target="tpu_custom_call" | custom-call | flops 1000 | bytes 1000 | tf_op jit(solution)/shard_map/pieces/pallas_call | solution.py:373
  77.3 6.9 %all-to-all-start.2 = ((bf16[32,240,128]{2,1,0:T(8,128)(2,1)}), bf16[32,240,128]{2,1,0:T(8,128)(2,1)S(1)}, u32[]{:S(2)}, u32[]{:S(2)}) async-start(bf16[32,240,128]{2,1,0:T(8,128)(2,1)} %get-tuple-element.23), calls=%async_computation.2 | async-start | bytes 3932160 | tf_op jit(solution)/shard_map/all_to_all | solution.py:582
  84.2 6.3 %ungroup.1 = bf16[16,128,128]{2,1,0:T(8,128)(2,1)} custom-call(bf16[16,64,256]{2,1,0:T(8,128)(2,1)} %get-tuple-element.24.res_ref), custom_call_target="tpu_custom_call" | custom-call | flops 1000 | bytes 1000 | tf_op jit(solution)/shard_map/ungroup/pallas_call | solution.py:415
  90.5 16.0 %all-to-all-done.2.refs_1_ = bf16[32,240,128]{2,1,0:T(8,128)(2,1)S(1)} async-done(((bf16[32,240,128]{2,1,0:T(8,128)(2,1)}), bf16[32,240,128]{2,1,0:T(8,128)(2,1)S(1)}, u32[]{:S(2)}, u32[]{:S(2)}) %all-to-all-start.2) | async-done | bytes 1966112 | tf_op jit(solution)/shard_map/all_to_all | solution.py:582
  106.5 2.1 %fold.1 = bf16[8,352,128]{2,1,0:T(8,128)(2,1)S(1)} custom-call(s32[16,1,2]{2,1,0:T(1,128)} %copy-done, bf16[32,240,128]{2,1,0:T(8,128)(2,1)S(1)} %all-to-all-done.2.refs_1_), custom_call_target="tpu_custom_call" | custom-call | flops 1000 | bytes 1000 | tf_op jit(solution)/shard_map/fold/pallas_call | solution.py:456
  108.6 16.7 %all_to_all.20.refs_0_ = bf16[8,352,128]{2,1,0:T(8,128)(2,1)S(1)} all-to-all(bf16[8,352,128]{2,1,0:T(8,128)(2,1)S(1)} %fold.1), channel_id=1, replica_groups=mesh['sky'=16,'exp'=8] {'exp'}, dimensions={0} | all-to-all | bytes 1441792 | tf_op jit(solution)/shard_map/all_to_all | solution.py:586
  125.3 1.3 finish.1
  126.6 4.6 %collective-permute-start.2 = (bf16[20,128]{1,0:T(8,128)(2,1)S(1)}, bf16[20,128]{1,0:T(8,128)(2,1)S(1)}, u32[]{:S(2)}, u32[]{:S(2)}) collective-permute-start(bf16[20,128]{1,0:T(8,128)(2,1)S(1)} %get-tuple-element.27), channel_id=1, source_target_pairs={{0,8},{8,16},{16,24},{24,32},{32,40},{40,48},{48,56},{56,64},{64,7... | collective-permute-start | bytes 15368 | tf_op jit(solution)/shard_map/ppermute | solution.py:50
  131.2 1.9 %collective-permute-start.3 = (bf16[20,128]{1,0:T(8,128)(2,1)S(1)}, bf16[20,128]{1,0:T(8,128)(2,1)S(1)}, u32[]{:S(2)}, u32[]{:S(2)}) collective-permute-start(bf16[20,128]{1,0:T(8,128)(2,1)S(1)} %get-tuple-element.28), channel_id=1, source_target_pairs={{8,0},{16,8},{24,16},{32,24},{40,32},{48,40},{56,48},{64,56},{72,6... | collective-permute-start | bytes 15368 | tf_op jit(solution)/shard_map/ppermute | solution.py:50
  133.1 0.0 collective-permute-done.2.above_ref
  133.1 5.7 %collective-permute-done.3.below_ref = bf16[20,128]{1,0:T(8,128)(2,1)S(1)} collective-permute-done((bf16[20,128]{1,0:T(8,128)(2,1)S(1)}, bf16[20,128]{1,0:T(8,128)(2,1)S(1)}, u32[]{:S(2)}, u32[]{:S(2)}) %collective-permute-start.3) | collective-permute-done | bytes 5152 | tf_op jit(solution)/shard_map/ppermute | solution.py:50
  138.8 1.4 rims.1
  (2 shorter events, 0.0 us)
Async XLA Ops:
  2.8 19.0 %all-to-all-start = ((s32[16,1,2]{2,1,0:T(1,128)}), s32[16,1,2]{2,1,0:T(1,128)S(1)}, u32[]{:S(2)}, u32[]{:S(2)}) async-start(s32[16,1,2]{2,1,0:T(1,128)} %copy.12), calls=%async_computation | async-start | bytes 16384 | tf_op jit(solution)/shard_map/all_to_all | solution.py:563
  11.8 10.0 %collective-permute-start.1 = (bf16[20,1024]{1,0:T(8,128)(2,1)S(1)}, bf16[20,1024]{1,0:T(8,128)(2,1)S(1)}, u32[]{:S(2)}, u32[]{:S(2)}) collective-permute-start(bf16[20,1024]{1,0:T(8,128)(2,1)S(1)} %get-tuple-element.32), channel_id=1, source_target_pairs={{8,0},{16,8},{24,16},{32,24},{40,32},{48,40},{56,48},{64,56},{72,6... | collective-permute-start | bytes 122888 | tf_op jit(solution)/shard_map/ppermute | solution.py:50
  14.6 7.2 %collective-permute-start = (bf16[20,1024]{1,0:T(8,128)(2,1)S(1)}, bf16[20,1024]{1,0:T(8,128)(2,1)S(1)}, u32[]{:S(2)}, u32[]{:S(2)}) collective-permute-start(bf16[20,1024]{1,0:T(8,128)(2,1)S(1)} %get-tuple-element.33), channel_id=1, source_target_pairs={{0,8},{8,16},{16,24},{24,32},{32,40},{40,48},{48,56},{56,64},{64,7... | collective-permute-start | bytes 122888 | tf_op jit(solution)/shard_map/ppermute | solution.py:50
  21.8 2.3 %copy-start = (s32[16,1,2]{2,1,0:T(1,128)}, s32[16,1,2]{2,1,0:T(1,128)S(1)}, u32[]{:S(2)}) copy-start(s32[16,1,2]{2,1,0:T(1,128)S(1)} %all-to-all-done.refs_0_) | copy-start | bytes 388
  27.2 7.7 %copy-start.1 = (bf16[16,1681]{1,0:T(8,128)(2,1)S(1)}, bf16[16,1681]{1,0:T(8,128)(2,1)}, u32[]{:S(2)}) copy-start(bf16[16,1681]{1,0:T(8,128)(2,1)} %param.13) | copy-start | bytes 161380
  27.2 32.2 %all-to-all-start.1 = ((bf16[32,232,128]{2,1,0:T(8,128)(2,1)}), bf16[32,232,128]{2,1,0:T(8,128)(2,1)S(1)}, u32[]{:S(2)}, u32[]{:S(2)}) async-start(bf16[32,232,128]{2,1,0:T(8,128)(2,1)} %cut.1), calls=%async_computation.1 | async-start | bytes 3801088 | tf_op jit(solution)/shard_map/all_to_all | solution.py:578
  77.3 29.2 %all-to-all-start.2 = ((bf16[32,240,128]{2,1,0:T(8,128)(2,1)}), bf16[32,240,128]{2,1,0:T(8,128)(2,1)S(1)}, u32[]{:S(2)}, u32[]{:S(2)}) async-start(bf16[32,240,128]{2,1,0:T(8,128)(2,1)} %get-tuple-element.23), calls=%async_computation.2 | async-start | bytes 3932160 | tf_op jit(solution)/shard_map/all_to_all | solution.py:582
  126.6 6.5 %collective-permute-start.2 = (bf16[20,128]{1,0:T(8,128)(2,1)S(1)}, bf16[20,128]{1,0:T(8,128)(2,1)S(1)}, u32[]{:S(2)}, u32[]{:S(2)}) collective-permute-start(bf16[20,128]{1,0:T(8,128)(2,1)S(1)} %get-tuple-element.27), channel_id=1, source_target_pairs={{0,8},{8,16},{16,24},{24,32},{32,40},{40,48},{48,56},{56,64},{64,7... | collective-permute-start | bytes 15368 | tf_op jit(solution)/shard_map/ppermute | solution.py:50
  131.2 7.6 %collective-permute-start.3 = (bf16[20,128]{1,0:T(8,128)(2,1)S(1)}, bf16[20,128]{1,0:T(8,128)(2,1)S(1)}, u32[]{:S(2)}, u32[]{:S(2)}) collective-permute-start(bf16[20,128]{1,0:T(8,128)(2,1)S(1)} %get-tuple-element.28), channel_id=1, source_target_pairs={{8,0},{16,8},{24,16},{32,24},{40,32},{48,40},{56,48},{64,56},{72,6... | collective-permute-start | bytes 15368 | tf_op jit(solution)/shard_map/ppermute | solution.py:50

commit v8 on v7

--- a/solution.py
+++ b/solution.py
@@ -24,7 +24,7 @@
 TILES = 6
 RES_LEAD = 40
 TAP_ROWS = 48
-GROUP = 2
+GROUP = 4
 BATCH = 4
 SLOTS = 8
 CHUNK = 9
@@ -90,7 +90,7 @@
             )
         return carry
 
-    lax.fori_loop(0, data_ref.shape[0], per_piece, 0)
+    lax.fori_loop(0, data_ref.shape[0], per_piece, 0, unroll=2)
 
 
 def regroup(exposure_data, pixel_mask):
@@ -321,7 +321,7 @@
         for copy in sent(step - 2):
             copy.wait()
 
-    def per_piece(i, taps_ref, field, resid):
+    def forward(i, taps_ref, field):
         field[...] = patch_ref[slot_ref[GROUP * step + i]].astype(F32)
 
         def read_patch(d, t):
@@ -333,7 +333,9 @@
                     parts.append(jnp.concatenate(pair, axis=1))
             return jnp.concatenate(parts, axis=0).astype(BF16)
 
-        predicted = correlate(read_patch, taps_ref)
+        return correlate(read_patch, taps_ref)
+
+    def compare(i, predicted, resid):
         observed = data_ref[i].astype(F32)
         residual = jnp.where(observed < UNKNOWN, predicted - observed, 0.0).astype(BF16)
         res_out[i] = residual
@@ -342,6 +344,7 @@
             first = RES_LEAD + EXT * row
             resid[first : first + OUT, :] = wide[OUT * row : OUT * (row + 1)]
 
+    def backward(i, taps_ref, resid):
         def read_residual(s, t):
             return resid[pl.ds(RES_LEAD - EXT * s - t, SLOT_ROWS), :].astype(BF16)
 
@@ -350,7 +353,9 @@
         adj_slots[slots, i, SLOT_ROWS:] = adjoint[: ADJ_ROWS - SLOT_ROWS, LANES:]
 
     for i in range(GROUP):
-        per_piece(i, taps[i], field.at[i], resid.at[i])
+        compare(i, forward(i, taps[i], field.at[i]), resid.at[i])
+    for i in range(GROUP):
+        backward(i, taps[i], resid.at[i])
     for copy in sent(step):
         copy.start()
 

time: 141 us -> 135 us (0.957)
  Pallas kernels: 57.9 us -> 50.7 us
    pallas_call x1, Pallas kernels: 17.9 us -> 12.4 us  [pieces(): pl.pallas_call(pieces_kernel, grid_spec=pltpu.PrefetchScalarGridSpec(num_...]
    pallas_call x1, Pallas kernels: 6.63 us -> 4.77 us  [regroup(): pl.pallas_call(regroup_kernel, grid=(pieces // BATCH,), in_specs=[block,...]
where the time goes in v8:
time: 135 us; the launch traced here: 134 us
  Pallas kernels  50.7 us (38%)
  starting transfers between devices  37.8 us (28%)
  waiting for transfers between devices  22.9 us (17%)
  blocking collectives  16.2 us (12%)
  other arithmetic  3.44 us (3%)
  local copies, waits for them, and re-layouts  2.47 us (2%)
    all_to_all x1, waiting for transfers between devices, shards(): lax.all_to_all(adjoints, 'sky', split_axis=0, concat_axis=0, tiled=True)  17.1 us
    pallas_call x1, Pallas kernels, build_taps(): pl.pallas_call(taps_kernel, grid=(cells,), in_specs=[pl.BlockSpec((1, TAP...  16.9 us
    all_to_all x1, blocking collectives, shards(): lax.all_to_all(partial, 'exp', split_axis=0, concat_axis=0, tiled=True)  16.2 us
    ppermute x4, starting transfers between devices, from_behind(): return lax.ppermute(x, axis, pairs)  14.9 us
    pallas_call x1, Pallas kernels, pieces(): pl.pallas_call(pieces_kernel, grid_spec=pltpu.PrefetchScalarGridSpec(num_...  12.4 us
    all_to_all x1, starting transfers between devices, shards(): lax.all_to_all(requests[:, None, :], 'sky', split_axis=0, concat_axis=0,...  8.18 us
    all_to_all x1, starting transfers between devices, shards(): lax.all_to_all(outgoing, 'sky', split_axis=0, concat_axis=0, tiled=True)  7.65 us
    all_to_all x1, starting transfers between devices, shards(): lax.all_to_all(adjoints, 'sky', split_axis=0, concat_axis=0, tiled=True)  7.11 us
  transfers between devices with their start and end apart: 7, of which 2 were waited for; matrix products, arithmetic and copies ran while one was open for 3% of the time, Pallas kernels for 21%

profile of v8, /device:TPU:24, one launch (start us, length us, event | category | flops | bytes accessed | tf_op | source)
XLA Modules:
  0.0 134.2 jit_solution(12624406414696238673)
XLA Ops:
  0.6 0.7 multiply_add_fusion
  1.3 0.8 select_reduce_fusion.1
  2.1 0.7 copy.12
  2.8 8.2 %all-to-all-start = ((s32[16,1,2]{2,1,0:T(1,128)}), s32[16,1,2]{2,1,0:T(1,128)S(1)}, u32[]{:S(2)}, u32[]{:S(2)}) async-start(s32[16,1,2]{2,1,0:T(1,128)} %copy.12), calls=%async_computation | async-start | bytes 16384 | tf_op jit(solution)/shard_map/all_to_all | solution.py:568
  11.0 0.8 fusion.4
  11.8 2.8 %collective-permute-start.1 = (bf16[20,1024]{1,0:T(8,128)(2,1)S(1)}, bf16[20,1024]{1,0:T(8,128)(2,1)S(1)}, u32[]{:S(2)}, u32[]{:S(2)}) collective-permute-start(bf16[20,1024]{1,0:T(8,128)(2,1)S(1)} %get-tuple-element.32), channel_id=1, source_target_pairs={{8,0},{16,8},{24,16},{32,24},{40,32},{48,40},{56,48},{64,56},{72,6... | collective-permute-start | bytes 122888 | tf_op jit(solution)/shard_map/ppermute | solution.py:50
  14.6 5.2 %collective-permute-start = (bf16[20,1024]{1,0:T(8,128)(2,1)S(1)}, bf16[20,1024]{1,0:T(8,128)(2,1)S(1)}, u32[]{:S(2)}, u32[]{:S(2)}) collective-permute-start(bf16[20,1024]{1,0:T(8,128)(2,1)S(1)} %get-tuple-element.33), channel_id=1, source_target_pairs={{0,8},{8,16},{16,24},{24,32},{32,40},{40,48},{48,56},{56,64},{64,7... | collective-permute-start | bytes 122888 | tf_op jit(solution)/shard_map/ppermute | solution.py:50
  19.8 0.7 fusion.1
  20.5 1.2 convert_add_fusion.slot_ref
  21.7 0.0 all-to-all-done.refs_0_
  21.8 0.0 copy-start
  21.8 0.0 collective-permute-done.1.below_ref
  21.8 0.0 collective-permute-done.above_ref
  21.8 2.2 %blocks.1.refs_1_ = f32[38,72,128]{2,1,0:T(8,128)S(1)} custom-call(bf16[256,1024]{1,0:T(8,128)(2,1)} %stripe_ref.1, bf16[20,1024]{1,0:T(8,128)(2,1)S(1)} %collective-permute-done.above_ref, bf16[20,1024]{1,0:T(8,128)(2,1)S(1)} %collective-permute-done.1.below_ref), custom_call_target="tpu_custom_call" | custom-call | flops 1000 | bytes 1000 | tf_op jit(solution)/shard_map/blocks/pallas_call | solution.py:204
  24.0 0.0 copy-done
  24.0 3.2 %cut.1 = bf16[32,232,128]{2,1,0:T(8,128)(2,1)} custom-call(s32[16,1,2]{2,1,0:T(1,128)} %copy-done, f32[38,72,128]{2,1,0:T(8,128)S(1)} %blocks.1.refs_1_), custom_call_target="tpu_custom_call" | custom-call | flops 1000 | bytes 1000 | tf_op jit(solution)/shard_map/cut/pallas_call | solution.py:238
  27.2 0.0 copy-start.1
  27.2 7.6 %all-to-all-start.1 = ((bf16[32,232,128]{2,1,0:T(8,128)(2,1)}), bf16[32,232,128]{2,1,0:T(8,128)(2,1)S(1)}, u32[]{:S(2)}, u32[]{:S(2)}) async-start(bf16[32,232,128]{2,1,0:T(8,128)(2,1)} %cut.1), calls=%async_computation.1 | async-start | bytes 3801088 | tf_op jit(solution)/shard_map/all_to_all | solution.py:583
  34.9 0.0 copy-done.1
  34.9 0.2 reshape.102
  35.1 0.7 pad.4.kernel_ref
  35.8 16.9 %taps.1.refs_0_.refs_1_.refs_2_.refs_3_ = bf16[16,512,768]{2,1,0:T(8,128)(2,1)} custom-call(bf16[16,48,128]{2,1,0:T(8,128)(2,1)} %pad.4.kernel_ref), custom_call_target="tpu_custom_call" | custom-call | flops 1000 | bytes 1000 | tf_op jit(solution)/shard_map/taps/pallas_call | solution.py:162
  52.8 4.8 %regroup.1.refs_4_ = bf16[16,64,256]{2,1,0:T(8,128)(2,1)} custom-call(bf16[16,128,128]{2,1,0:T(8,128)(2,1)} %data_ref, s32[16,128,128]{2,1,0:T(8,128)} %keep_ref), custom_call_target="tpu_custom_call" | custom-call | flops 1000 | bytes 1000 | tf_op jit(solution)/shard_map/regroup/pallas_call | solution.py:99
  57.5 0.0 all-to-all-done.1.patch_ref
  57.5 12.4 %pieces.1 = (bf16[32,240,128]{2,1,0:T(8,128)(2,1)}, bf16[16,64,256]{2,1,0:T(8,128)(2,1)}) custom-call(s32[16]{0:T(128)} %convert_add_fusion.slot_ref, s32[16]{0:T(128)} %cell_ref.1, bf16[32,232,128]{2,1,0:T(8,128)(2,1)S(1)} %all-to-all-done.1.patch_ref, bf16[16,512,768]{2,1,0:T(8,128)(2,1)} %taps.1.refs_0_.refs_1_.refs_2_.refs_3_, ...), custom_call_target="tpu_custom_call" | custom-call | flops 1000 | bytes 1000 | tf_op jit(solution)/shard_map/pieces/pallas_call | solution.py:378
  69.9 7.1 %all-to-all-start.2 = ((bf16[32,240,128]{2,1,0:T(8,128)(2,1)}), bf16[32,240,128]{2,1,0:T(8,128)(2,1)S(1)}, u32[]{:S(2)}, u32[]{:S(2)}) async-start(bf16[32,240,128]{2,1,0:T(8,128)(2,1)} %get-tuple-element.23), calls=%async_computation.2 | async-start | bytes 3932160 | tf_op jit(solution)/shard_map/all_to_all | solution.py:587
  77.1 6.3 %ungroup.1 = bf16[16,128,128]{2,1,0:T(8,128)(2,1)} custom-call(bf16[16,64,256]{2,1,0:T(8,128)(2,1)} %get-tuple-element.24.res_ref), custom_call_target="tpu_custom_call" | custom-call | flops 1000 | bytes 1000 | tf_op jit(solution)/shard_map/ungroup/pallas_call | solution.py:420
  83.4 17.1 %all-to-all-done.2.refs_1_ = bf16[32,240,128]{2,1,0:T(8,128)(2,1)S(1)} async-done(((bf16[32,240,128]{2,1,0:T(8,128)(2,1)}), bf16[32,240,128]{2,1,0:T(8,128)(2,1)S(1)}, u32[]{:S(2)}, u32[]{:S(2)}) %all-to-all-start.2) | async-done | bytes 1966112 | tf_op jit(solution)/shard_map/all_to_all | solution.py:587
  100.5 2.2 %fold.1 = bf16[8,352,128]{2,1,0:T(8,128)(2,1)S(1)} custom-call(s32[16,1,2]{2,1,0:T(1,128)} %copy-done, bf16[32,240,128]{2,1,0:T(8,128)(2,1)S(1)} %all-to-all-done.2.refs_1_), custom_call_target="tpu_custom_call" | custom-call | flops 1000 | bytes 1000 | tf_op jit(solution)/shard_map/fold/pallas_call | solution.py:461
  102.7 16.2 %all_to_all.20.refs_0_ = bf16[8,352,128]{2,1,0:T(8,128)(2,1)S(1)} all-to-all(bf16[8,352,128]{2,1,0:T(8,128)(2,1)S(1)} %fold.1), channel_id=1, replica_groups=mesh['sky'=16,'exp'=8] {'exp'}, dimensions={0} | all-to-all | bytes 1441792 | tf_op jit(solution)/shard_map/all_to_all | solution.py:591
  118.9 1.3 finish.1
  120.2 5.0 %collective-permute-start.2 = (bf16[20,128]{1,0:T(8,128)(2,1)S(1)}, bf16[20,128]{1,0:T(8,128)(2,1)S(1)}, u32[]{:S(2)}, u32[]{:S(2)}) collective-permute-start(bf16[20,128]{1,0:T(8,128)(2,1)S(1)} %get-tuple-element.27), channel_id=1, source_target_pairs={{0,8},{8,16},{16,24},{24,32},{32,40},{40,48},{48,56},{56,64},{64,7... | collective-permute-start | bytes 15368 | tf_op jit(solution)/shard_map/ppermute | solution.py:50
  125.2 1.9 %collective-permute-start.3 = (bf16[20,128]{1,0:T(8,128)(2,1)S(1)}, bf16[20,128]{1,0:T(8,128)(2,1)S(1)}, u32[]{:S(2)}, u32[]{:S(2)}) collective-permute-start(bf16[20,128]{1,0:T(8,128)(2,1)S(1)} %get-tuple-element.28), channel_id=1, source_target_pairs={{8,0},{16,8},{24,16},{32,24},{40,32},{48,40},{56,48},{64,56},{72,6... | collective-permute-start | bytes 15368 | tf_op jit(solution)/shard_map/ppermute | solution.py:50
  127.2 0.0 collective-permute-done.2.above_ref
  127.2 5.7 %collective-permute-done.3.below_ref = bf16[20,128]{1,0:T(8,128)(2,1)S(1)} collective-permute-done((bf16[20,128]{1,0:T(8,128)(2,1)S(1)}, bf16[20,128]{1,0:T(8,128)(2,1)S(1)}, u32[]{:S(2)}, u32[]{:S(2)}) %collective-permute-start.3) | collective-permute-done | bytes 5152 | tf_op jit(solution)/shard_map/ppermute | solution.py:50
  132.9 1.4 %rims.1 = f32[256,128]{1,0:T(8,128)} custom-call(f32[256,128]{1,0:T(8,128)} %get-tuple-element.26.middle_ref, bf16[20,128]{1,0:T(8,128)(2,1)S(1)} %collective-permute-done.2.above_ref, bf16[20,128]{1,0:T(8,128)(2,1)S(1)} %collective-permute-done.3.below_ref), custom_call_target="tpu_custom_call", output_to_operand_aliasing={{}: (0, {})} | custom-call | flops 1000 | bytes 1000 | tf_op jit(solution)/shard_map/rims/pallas_call | solution.py:538
  (2 shorter events, 0.0 us)
Async XLA Ops:
  2.8 19.0 %all-to-all-start = ((s32[16,1,2]{2,1,0:T(1,128)}), s32[16,1,2]{2,1,0:T(1,128)S(1)}, u32[]{:S(2)}, u32[]{:S(2)}) async-start(s32[16,1,2]{2,1,0:T(1,128)} %copy.12), calls=%async_computation | async-start | bytes 16384 | tf_op jit(solution)/shard_map/all_to_all | solution.py:568
  11.8 10.0 %collective-permute-start.1 = (bf16[20,1024]{1,0:T(8,128)(2,1)S(1)}, bf16[20,1024]{1,0:T(8,128)(2,1)S(1)}, u32[]{:S(2)}, u32[]{:S(2)}) collective-permute-start(bf16[20,1024]{1,0:T(8,128)(2,1)S(1)} %get-tuple-element.32), channel_id=1, source_target_pairs={{8,0},{16,8},{24,16},{32,24},{40,32},{48,40},{56,48},{64,56},{72,6... | collective-permute-start | bytes 122888 | tf_op jit(solution)/shard_map/ppermute | solution.py:50
  14.6 7.2 %collective-permute-start = (bf16[20,1024]{1,0:T(8,128)(2,1)S(1)}, bf16[20,1024]{1,0:T(8,128)(2,1)S(1)}, u32[]{:S(2)}, u32[]{:S(2)}) collective-permute-start(bf16[20,1024]{1,0:T(8,128)(2,1)S(1)} %get-tuple-element.33), channel_id=1, source_target_pairs={{0,8},{8,16},{16,24},{24,32},{32,40},{40,48},{48,56},{56,64},{64,7... | collective-permute-start | bytes 122888 | tf_op jit(solution)/shard_map/ppermute | solution.py:50
  21.8 2.3 %copy-start = (s32[16,1,2]{2,1,0:T(1,128)}, s32[16,1,2]{2,1,0:T(1,128)S(1)}, u32[]{:S(2)}) copy-start(s32[16,1,2]{2,1,0:T(1,128)S(1)} %all-to-all-done.refs_0_) | copy-start | bytes 388
  27.2 7.7 %copy-start.1 = (bf16[16,1681]{1,0:T(8,128)(2,1)S(1)}, bf16[16,1681]{1,0:T(8,128)(2,1)}, u32[]{:S(2)}) copy-start(bf16[16,1681]{1,0:T(8,128)(2,1)} %param.13) | copy-start | bytes 161380
  27.2 30.3 %all-to-all-start.1 = ((bf16[32,232,128]{2,1,0:T(8,128)(2,1)}), bf16[32,232,128]{2,1,0:T(8,128)(2,1)S(1)}, u32[]{:S(2)}, u32[]{:S(2)}) async-start(bf16[32,232,128]{2,1,0:T(8,128)(2,1)} %cut.1), calls=%async_computation.1 | async-start | bytes 3801088 | tf_op jit(solution)/shard_map/all_to_all | solution.py:583
  69.9 30.6 %all-to-all-start.2 = ((bf16[32,240,128]{2,1,0:T(8,128)(2,1)}), bf16[32,240,128]{2,1,0:T(8,128)(2,1)S(1)}, u32[]{:S(2)}, u32[]{:S(2)}) async-start(bf16[32,240,128]{2,1,0:T(8,128)(2,1)} %get-tuple-element.23), calls=%async_computation.2 | async-start | bytes 3932160 | tf_op jit(solution)/shard_map/all_to_all | solution.py:587
  120.2 7.0 %collective-permute-start.2 = (bf16[20,128]{1,0:T(8,128)(2,1)S(1)}, bf16[20,128]{1,0:T(8,128)(2,1)S(1)}, u32[]{:S(2)}, u32[]{:S(2)}) collective-permute-start(bf16[20,128]{1,0:T(8,128)(2,1)S(1)} %get-tuple-element.27), channel_id=1, source_target_pairs={{0,8},{8,16},{16,24},{24,32},{32,40},{40,48},{48,56},{56,64},{64,7... | collective-permute-start | bytes 15368 | tf_op jit(solution)/shard_map/ppermute | solution.py:50
  125.2 7.6 %collective-permute-start.3 = (bf16[20,128]{1,0:T(8,128)(2,1)S(1)}, bf16[20,128]{1,0:T(8,128)(2,1)S(1)}, u32[]{:S(2)}, u32[]{:S(2)}) collective-permute-start(bf16[20,128]{1,0:T(8,128)(2,1)S(1)} %get-tuple-element.28), channel_id=1, source_target_pairs={{8,0},{16,8},{24,16},{32,24},{40,32},{48,40},{56,48},{64,56},{72,6... | collective-permute-start | bytes 15368 | tf_op jit(solution)/shard_map/ppermute | solution.py:50

commit v9 on v8

--- a/solution.py
+++ b/solution.py
@@ -1,5 +1,6 @@
 import jax
 import jax.numpy as jnp
+import numpy as np
 from jax import lax
 from jax.experimental import pallas as pl
 from jax.experimental.pallas import tpu as pltpu
@@ -149,7 +150,7 @@
             before = turns
         return carry
 
-    lax.fori_loop(0, REACH, per_shift, 0)
+    lax.fori_loop(0, REACH, per_shift, 0, unroll=REACH)
 
 
 def padded_kernels(table):
@@ -558,28 +559,27 @@
     mine = owner_sky[None, :] == lax.broadcasted_iota(jnp.int32, (sky_count, 1), 0)
     first = jnp.min(jnp.where(mine, code[None, :], piece_count * block_total), axis=1)
     last = jnp.max(jnp.where(mine, code[None, :], -1), axis=1)
-    requests = jnp.stack(
-        [
-            jnp.where(last < 0, -1, first % block_total),
-            jnp.where(last > first, last % block_total, -1),
-        ],
-        axis=1,
+    turn = np.arange(CAP)[None, None, :]
+    earliest, latest = first[:, None, None], last[:, None, None]
+    requests = jnp.where(
+        turn == 0,
+        jnp.where(latest < 0, -1, earliest % block_total),
+        jnp.where(latest > earliest, latest % block_total, -1),
     )
-    asked = lax.all_to_all(
-        requests[:, None, :], "sky", split_axis=0, concat_axis=0, tiled=True
-    )
+    asked = lax.all_to_all(requests, "sky", split_axis=0, concat_axis=0, tiled=True)
+
     above = from_behind(sky_model[stripe_rows - HALO :], "sky", 1)
     below = from_behind(sky_model[:HALO], "sky", -1)
     half_rows = (stripe_rows + 2 * HALO + TAIL) // 8
     second = jnp.any(mine & (first[:, None] < code[None, :]), axis=0)
-    slot_index = owner_sky * CAP + second.astype(jnp.int32)
     kernels = padded_kernels(psf_table)
-    asked, above, below, slot_index = lax.optimization_barrier((asked, above, below, slot_index))
+    asked, above, below, second = lax.optimization_barrier((asked, above, below, second))
     blocks = stripe_blocks(sky_model, above, below, half_rows)
     outgoing = cut_patches(asked, blocks, per_row)
-    exposure_data, pixel_mask, kernels, _ = lax.optimization_barrier(
-        (exposure_data, pixel_mask, kernels, outgoing)
+    exposure_data, pixel_mask, kernels, second, _ = lax.optimization_barrier(
+        (exposure_data, pixel_mask, kernels, second, outgoing)
     )
+    slot_index = owner_sky * CAP + second.astype(jnp.int32)
     patches = lax.all_to_all(outgoing, "sky", split_axis=0, concat_axis=0, tiled=True)
     data = regroup(exposure_data, pixel_mask)
     taps = build_taps(kernels)

time: 135 us -> 137 us (1.015)
  Pallas kernels: 50.7 us -> 47.6 us
  waiting for transfers between devices: 22.9 us -> 25.5 us
    pallas_call x1, Pallas kernels: 16.9 us -> 13.7 us  [build_taps(): pl.pallas_call(taps_kernel, grid=(cells,), in_specs=[pl.BlockSpec((1, TAP...]
    all_to_all x1, waiting for transfers between devices: 0.01 us -> 1.6 us  [shards(): lax.all_to_all(outgoing, 'sky', split_axis=0, concat_axis=0, tiled=True)]
  transfers between devices with their start and end apart: 7 -> 7, of which waited for: 2 -> 4; matrix products, arithmetic and copies ran while one was open for 3% -> 2% of each run, Pallas kernels for 21% -> 18%
where the time goes in v9:
time: 137 us; the launch traced here: 135 us
  Pallas kernels  47.6 us (35%)
  starting transfers between devices  38.8 us (28%)
  waiting for transfers between devices  25.5 us (19%)
  blocking collectives  16.8 us (12%)
  other arithmetic  4.09 us (3%)
  local copies, waits for them, and re-layouts  1.8 us (1%)
    all_to_all x1, waiting for transfers between devices, shards(): lax.all_to_all(adjoints, 'sky', split_axis=0, concat_axis=0, tiled=True)  17.2 us
    all_to_all x1, blocking collectives, shards(): lax.all_to_all(partial, 'exp', split_axis=0, concat_axis=0, tiled=True)  16.8 us
    ppermute x4, starting transfers between devices, from_behind(): return lax.ppermute(x, axis, pairs)  15.7 us
    pallas_call x1, Pallas kernels, build_taps(): pl.pallas_call(taps_kernel, grid=(cells,), in_specs=[pl.BlockSpec((1, TAP...  13.7 us
    pallas_call x1, Pallas kernels, pieces(): pl.pallas_call(pieces_kernel, grid_spec=pltpu.PrefetchScalarGridSpec(num_...  12.6 us
    all_to_all x1, starting transfers between devices, shards(): lax.all_to_all(requests, 'sky', split_axis=0, concat_axis=0, tiled=True)  8.18 us
    all_to_all x1, starting transfers between devices, shards(): lax.all_to_all(outgoing, 'sky', split_axis=0, concat_axis=0, tiled=True)  7.96 us
    all_to_all x1, starting transfers between devices, shards(): lax.all_to_all(adjoints, 'sky', split_axis=0, concat_axis=0, tiled=True)  6.98 us
  transfers between devices with their start and end apart: 7, of which 4 were waited for; matrix products, arithmetic and copies ran while one was open for 2% of the time, Pallas kernels for 18%

profile of v9, /device:TPU:24, one launch (start us, length us, event | category | flops | bytes accessed | tf_op | source)
XLA Modules:
  0.0 135.3 jit_solution(4141336863279595542)
XLA Ops:
  0.6 0.7 multiply_add_fusion
  1.3 0.8 select_reduce_fusion
  2.1 1.4 %broadcast_select_fusion = s32[16,1,2]{2,1,0:T(1,128)} fusion(pred[2]{0:T(512)(128)(4,1)} %constant.47, s32[16]{0:T(128)S(1)} %get-tuple-element.37, s32[16]{0:T(128)S(1)} %get-tuple-element.36), kind=kLoop, calls=%fused_computation | loop fusion | flops 32 | bytes 258 | tf_op jit(solution)/shard_map/jit(_where)/select_n | solution.py:564
  3.4 8.2 %all-to-all-start = ((s32[16,1,2]{2,1,0:T(1,128)}), s32[16,1,2]{2,1,0:T(1,128)S(1)}, u32[]{:S(2)}, u32[]{:S(2)}) async-start(s32[16,1,2]{2,1,0:T(1,128)} %broadcast_select_fusion), calls=%async_computation | async-start | bytes 16384 | tf_op jit(solution)/shard_map/all_to_all | solution.py:569
  11.6 0.8 fusion.4
  12.5 2.8 %collective-permute-start.1 = (bf16[20,1024]{1,0:T(8,128)(2,1)S(1)}, bf16[20,1024]{1,0:T(8,128)(2,1)S(1)}, u32[]{:S(2)}, u32[]{:S(2)}) collective-permute-start(bf16[20,1024]{1,0:T(8,128)(2,1)S(1)} %get-tuple-element.34), channel_id=1, source_target_pairs={{8,0},{16,8},{24,16},{32,24},{40,32},{48,40},{56,48},{64,56},{72,6... | collective-permute-start | bytes 122888 | tf_op jit(solution)/shard_map/ppermute | solution.py:51
  15.2 5.2 %collective-permute-start = (bf16[20,1024]{1,0:T(8,128)(2,1)S(1)}, bf16[20,1024]{1,0:T(8,128)(2,1)S(1)}, u32[]{:S(2)}, u32[]{:S(2)}) collective-permute-start(bf16[20,1024]{1,0:T(8,128)(2,1)S(1)} %get-tuple-element.35), channel_id=1, source_target_pairs={{0,8},{8,16},{16,24},{24,32},{32,40},{40,48},{48,56},{56,64},{64,7... | collective-permute-start | bytes 122888 | tf_op jit(solution)/shard_map/ppermute | solution.py:51
  20.4 0.7 fusion.1
  21.2 0.0 all-to-all-done.refs_0_
  21.2 0.0 copy-start
  21.2 0.0 collective-permute-done.1.below_ref
  21.2 1.0 collective-permute-done.above_ref
  22.2 2.2 %blocks.1.refs_1_ = f32[38,72,128]{2,1,0:T(8,128)S(1)} custom-call(bf16[256,1024]{1,0:T(8,128)(2,1)} %stripe_ref.1, bf16[20,1024]{1,0:T(8,128)(2,1)S(1)} %collective-permute-done.above_ref, bf16[20,1024]{1,0:T(8,128)(2,1)S(1)} %collective-permute-done.1.below_ref), custom_call_target="tpu_custom_call" | custom-call | flops 1000 | bytes 1000 | tf_op jit(solution)/shard_map/blocks/pallas_call | solution.py:205
  24.4 0.0 copy-done
  24.4 3.2 %cut.1 = bf16[32,232,128]{2,1,0:T(8,128)(2,1)} custom-call(s32[16,1,2]{2,1,0:T(1,128)} %copy-done, f32[38,72,128]{2,1,0:T(8,128)S(1)} %blocks.1.refs_1_), custom_call_target="tpu_custom_call" | custom-call | flops 1000 | bytes 1000 | tf_op jit(solution)/shard_map/cut/pallas_call | solution.py:239
  27.6 0.0 copy-start.1
  27.6 8.0 %all-to-all-start.1 = ((bf16[32,232,128]{2,1,0:T(8,128)(2,1)}), bf16[32,232,128]{2,1,0:T(8,128)(2,1)S(1)}, u32[]{:S(2)}, u32[]{:S(2)}) async-start(bf16[32,232,128]{2,1,0:T(8,128)(2,1)} %cut.1), calls=%async_computation.1 | async-start | bytes 3801088 | tf_op jit(solution)/shard_map/all_to_all | solution.py:583
  35.5 0.0 copy-done.1
  35.5 0.2 reshape.136
  35.8 0.7 pad.4.kernel_ref
  36.5 13.7 %taps.1.refs_0_.refs_1_.refs_2_.refs_3_ = bf16[16,512,768]{2,1,0:T(8,128)(2,1)} custom-call(bf16[16,48,128]{2,1,0:T(8,128)(2,1)} %pad.4.kernel_ref), custom_call_target="tpu_custom_call" | custom-call | flops 1000 | bytes 1000 | tf_op jit(solution)/shard_map/taps/pallas_call | solution.py:163
  50.2 0.0 copy-start.2
  50.2 4.8 %regroup.1.refs_4_ = bf16[16,64,256]{2,1,0:T(8,128)(2,1)} custom-call(bf16[16,128,128]{2,1,0:T(8,128)(2,1)} %data_ref, s32[16,128,128]{2,1,0:T(8,128)} %keep_ref), custom_call_target="tpu_custom_call" | custom-call | flops 1000 | bytes 1000 | tf_op jit(solution)/shard_map/regroup/pallas_call | solution.py:100
  55.0 0.0 copy-done.2
  55.0 0.5 convert_add_fusion.slot_ref
  55.5 1.6 %all-to-all-done.1.patch_ref = bf16[32,232,128]{2,1,0:T(8,128)(2,1)S(1)} async-done(((bf16[32,232,128]{2,1,0:T(8,128)(2,1)}), bf16[32,232,128]{2,1,0:T(8,128)(2,1)S(1)}, u32[]{:S(2)}, u32[]{:S(2)}) %all-to-all-start.1) | async-done | bytes 1900576 | tf_op jit(solution)/shard_map/all_to_all | solution.py:583
  57.1 12.6 %pieces.1 = (bf16[32,240,128]{2,1,0:T(8,128)(2,1)}, bf16[16,64,256]{2,1,0:T(8,128)(2,1)}) custom-call(s32[16]{0:T(128)} %convert_add_fusion.slot_ref, s32[16]{0:T(128)} %cell_ref.1, bf16[32,232,128]{2,1,0:T(8,128)(2,1)S(1)} %all-to-all-done.1.patch_ref, bf16[16,512,768]{2,1,0:T(8,128)(2,1)} %taps.1.refs_0_.refs_1_.refs_2_.refs_3_, ...), custom_call_target="tpu_custom_call" | custom-call | flops 1000 | bytes 1000 | tf_op jit(solution)/shard_map/pieces/pallas_call | solution.py:379
  69.8 7.0 %all-to-all-start.2 = ((bf16[32,240,128]{2,1,0:T(8,128)(2,1)}), bf16[32,240,128]{2,1,0:T(8,128)(2,1)S(1)}, u32[]{:S(2)}, u32[]{:S(2)}) async-start(bf16[32,240,128]{2,1,0:T(8,128)(2,1)} %get-tuple-element.25), calls=%async_computation.2 | async-start | bytes 3932160 | tf_op jit(solution)/shard_map/all_to_all | solution.py:587
  76.8 6.3 %ungroup.1 = bf16[16,128,128]{2,1,0:T(8,128)(2,1)} custom-call(bf16[16,64,256]{2,1,0:T(8,128)(2,1)} %get-tuple-element.26.res_ref), custom_call_target="tpu_custom_call" | custom-call | flops 1000 | bytes 1000 | tf_op jit(solution)/shard_map/ungroup/pallas_call | solution.py:421
  83.1 17.2 %all-to-all-done.2.refs_1_ = bf16[32,240,128]{2,1,0:T(8,128)(2,1)S(1)} async-done(((bf16[32,240,128]{2,1,0:T(8,128)(2,1)}), bf16[32,240,128]{2,1,0:T(8,128)(2,1)S(1)}, u32[]{:S(2)}, u32[]{:S(2)}) %all-to-all-start.2) | async-done | bytes 1966112 | tf_op jit(solution)/shard_map/all_to_all | solution.py:587
  100.3 2.1 %fold.1 = bf16[8,352,128]{2,1,0:T(8,128)(2,1)S(1)} custom-call(s32[16,1,2]{2,1,0:T(1,128)} %copy-done, bf16[32,240,128]{2,1,0:T(8,128)(2,1)S(1)} %all-to-all-done.2.refs_1_), custom_call_target="tpu_custom_call" | custom-call | flops 1000 | bytes 1000 | tf_op jit(solution)/shard_map/fold/pallas_call | solution.py:462
  102.5 16.8 %all_to_all.20.refs_0_ = bf16[8,352,128]{2,1,0:T(8,128)(2,1)S(1)} all-to-all(bf16[8,352,128]{2,1,0:T(8,128)(2,1)S(1)} %fold.1), channel_id=1, replica_groups=mesh['sky'=16,'exp'=8] {'exp'}, dimensions={0} | all-to-all | bytes 1441792 | tf_op jit(solution)/shard_map/all_to_all | solution.py:591
  119.2 1.3 finish.1
  120.5 5.8 %collective-permute-start.2 = (bf16[20,128]{1,0:T(8,128)(2,1)S(1)}, bf16[20,128]{1,0:T(8,128)(2,1)S(1)}, u32[]{:S(2)}, u32[]{:S(2)}) collective-permute-start(bf16[20,128]{1,0:T(8,128)(2,1)S(1)} %get-tuple-element.29), channel_id=1, source_target_pairs={{0,8},{8,16},{16,24},{24,32},{32,40},{40,48},{48,56},{56,64},{64,7... | collective-permute-start | bytes 15368 | tf_op jit(solution)/shard_map/ppermute | solution.py:51
  126.3 1.9 %collective-permute-start.3 = (bf16[20,128]{1,0:T(8,128)(2,1)S(1)}, bf16[20,128]{1,0:T(8,128)(2,1)S(1)}, u32[]{:S(2)}, u32[]{:S(2)}) collective-permute-start(bf16[20,128]{1,0:T(8,128)(2,1)S(1)} %get-tuple-element.30), channel_id=1, source_target_pairs={{8,0},{16,8},{24,16},{32,24},{40,32},{48,40},{56,48},{64,56},{72,6... | collective-permute-start | bytes 15368 | tf_op jit(solution)/shard_map/ppermute | solution.py:51
  128.3 0.0 collective-permute-done.2.above_ref
  128.3 5.7 %collective-permute-done.3.below_ref = bf16[20,128]{1,0:T(8,128)(2,1)S(1)} collective-permute-done((bf16[20,128]{1,0:T(8,128)(2,1)S(1)}, bf16[20,128]{1,0:T(8,128)(2,1)S(1)}, u32[]{:S(2)}, u32[]{:S(2)}) %collective-permute-start.3) | collective-permute-done | bytes 5152 | tf_op jit(solution)/shard_map/ppermute | solution.py:51
  134.0 1.4 rims.1
  (1 shorter events, 0.0 us)
Async XLA Ops:
  3.4 17.7 %all-to-all-start = ((s32[16,1,2]{2,1,0:T(1,128)}), s32[16,1,2]{2,1,0:T(1,128)S(1)}, u32[]{:S(2)}, u32[]{:S(2)}) async-start(s32[16,1,2]{2,1,0:T(1,128)} %broadcast_select_fusion), calls=%async_computation | async-start | bytes 16384 | tf_op jit(solution)/shard_map/all_to_all | solution.py:569
  12.5 8.7 %collective-permute-start.1 = (bf16[20,1024]{1,0:T(8,128)(2,1)S(1)}, bf16[20,1024]{1,0:T(8,128)(2,1)S(1)}, u32[]{:S(2)}, u32[]{:S(2)}) collective-permute-start(bf16[20,1024]{1,0:T(8,128)(2,1)S(1)} %get-tuple-element.34), channel_id=1, source_target_pairs={{8,0},{16,8},{24,16},{32,24},{40,32},{48,40},{56,48},{64,56},{72,6... | collective-permute-start | bytes 122888 | tf_op jit(solution)/shard_map/ppermute | solution.py:51
  15.2 6.9 %collective-permute-start = (bf16[20,1024]{1,0:T(8,128)(2,1)S(1)}, bf16[20,1024]{1,0:T(8,128)(2,1)S(1)}, u32[]{:S(2)}, u32[]{:S(2)}) collective-permute-start(bf16[20,1024]{1,0:T(8,128)(2,1)S(1)} %get-tuple-element.35), channel_id=1, source_target_pairs={{0,8},{8,16},{16,24},{24,32},{32,40},{40,48},{48,56},{56,64},{64,7... | collective-permute-start | bytes 122888 | tf_op jit(solution)/shard_map/ppermute | solution.py:51
  21.2 3.2 %copy-start = (s32[16,1,2]{2,1,0:T(1,128)}, s32[16,1,2]{2,1,0:T(1,128)S(1)}, u32[]{:S(2)}) copy-start(s32[16,1,2]{2,1,0:T(1,128)S(1)} %all-to-all-done.refs_0_) | copy-start | bytes 388
  27.6 8.0 %copy-start.1 = (bf16[16,1681]{1,0:T(8,128)(2,1)S(1)}, bf16[16,1681]{1,0:T(8,128)(2,1)}, u32[]{:S(2)}) copy-start(bf16[16,1681]{1,0:T(8,128)(2,1)} %param.14) | copy-start | bytes 161380
  27.6 29.6 %all-to-all-start.1 = ((bf16[32,232,128]{2,1,0:T(8,128)(2,1)}), bf16[32,232,128]{2,1,0:T(8,128)(2,1)S(1)}, u32[]{:S(2)}, u32[]{:S(2)}) async-start(bf16[32,232,128]{2,1,0:T(8,128)(2,1)} %cut.1), calls=%async_computation.1 | async-start | bytes 3801088 | tf_op jit(solution)/shard_map/all_to_all | solution.py:583
  50.2 4.8 %copy-start.2 = (s32[16,1]{0,1:T(1,128)S(1)}, s32[16,1]{0,1:T(1,128)}, u32[]{:S(2)}) copy-start(s32[16,1]{0,1:T(1,128)} %param.11) | copy-start | bytes 196
  69.8 30.5 %all-to-all-start.2 = ((bf16[32,240,128]{2,1,0:T(8,128)(2,1)}), bf16[32,240,128]{2,1,0:T(8,128)(2,1)S(1)}, u32[]{:S(2)}, u32[]{:S(2)}) async-start(bf16[32,240,128]{2,1,0:T(8,128)(2,1)} %get-tuple-element.25), calls=%async_computation.2 | async-start | bytes 3932160 | tf_op jit(solution)/shard_map/all_to_all | solution.py:587
  120.5 7.7 %collective-permute-start.2 = (bf16[20,128]{1,0:T(8,128)(2,1)S(1)}, bf16[20,128]{1,0:T(8,128)(2,1)S(1)}, u32[]{:S(2)}, u32[]{:S(2)}) collective-permute-start(bf16[20,128]{1,0:T(8,128)(2,1)S(1)} %get-tuple-element.29), channel_id=1, source_target_pairs={{0,8},{8,16},{16,24},{24,32},{32,40},{40,48},{48,56},{56,64},{64,7... | collective-permute-start | bytes 15368 | tf_op jit(solution)/shard_map/ppermute | solution.py:51
  126.3 7.6 %collective-permute-start.3 = (bf16[20,128]{1,0:T(8,128)(2,1)S(1)}, bf16[20,128]{1,0:T(8,128)(2,1)S(1)}, u32[]{:S(2)}, u32[]{:S(2)}) collective-permute-start(bf16[20,128]{1,0:T(8,128)(2,1)S(1)} %get-tuple-element.30), channel_id=1, source_target_pairs={{8,0},{16,8},{24,16},{32,24},{40,32},{48,40},{56,48},{64,56},{72,6... | collective-permute-start | bytes 15368 | tf_op jit(solution)/shard_map/ppermute | solution.py:51

commit v10 on v8

--- a/solution.py
+++ b/solution.py
@@ -149,7 +149,7 @@
             before = turns
         return carry
 
-    lax.fori_loop(0, REACH, per_shift, 0)
+    lax.fori_loop(0, REACH, per_shift, 0, unroll=REACH)
 
 
 def padded_kernels(table):

time: 135 us -> 136 us (level)
  Pallas kernels: 50.7 us -> 47.4 us
  waiting for transfers between devices: 22.9 us -> 25.5 us
    pallas_call x1, Pallas kernels: 16.9 us -> 13.8 us  [build_taps(): pl.pallas_call(taps_kernel, grid=(cells,), in_specs=[pl.BlockSpec((1, TAP...]
    all_to_all x1, waiting for transfers between devices: 0.01 us -> 2.36 us  [shards(): lax.all_to_all(outgoing, 'sky', split_axis=0, concat_axis=0, tiled=True)]
  transfers between devices with their start and end apart: 7 -> 7, of which waited for: 2 -> 3; matrix products, arithmetic and copies ran while one was open for 3% -> 3% of each run, Pallas kernels for 21% -> 18%
where the time goes in v10:
time: 136 us; the launch traced here: 134 us
  Pallas kernels  47.4 us (35%)
  starting transfers between devices  38.7 us (28%)
  waiting for transfers between devices  25.5 us (19%)
  blocking collectives  16.3 us (12%)
  other arithmetic  3.44 us (3%)
  local copies, waits for them, and re-layouts  2.47 us (2%)
    all_to_all x1, waiting for transfers between devices, shards(): lax.all_to_all(adjoints, 'sky', split_axis=0, concat_axis=0, tiled=True)  17.4 us
    all_to_all x1, blocking collectives, shards(): lax.all_to_all(partial, 'exp', split_axis=0, concat_axis=0, tiled=True)  16.3 us
    ppermute x4, starting transfers between devices, from_behind(): return lax.ppermute(x, axis, pairs)  15.1 us
    pallas_call x1, Pallas kernels, build_taps(): pl.pallas_call(taps_kernel, grid=(cells,), in_specs=[pl.BlockSpec((1, TAP...  13.8 us
    pallas_call x1, Pallas kernels, pieces(): pl.pallas_call(pieces_kernel, grid_spec=pltpu.PrefetchScalarGridSpec(num_...  12.3 us
    all_to_all x1, starting transfers between devices, shards(): lax.all_to_all(requests[:, None, :], 'sky', split_axis=0, concat_axis=0,...  8.18 us
    all_to_all x1, starting transfers between devices, shards(): lax.all_to_all(adjoints, 'sky', split_axis=0, concat_axis=0, tiled=True)  7.75 us
    all_to_all x1, starting transfers between devices, shards(): lax.all_to_all(outgoing, 'sky', split_axis=0, concat_axis=0, tiled=True)  7.67 us
  transfers between devices with their start and end apart: 7, of which 3 were waited for; matrix products, arithmetic and copies ran while one was open for 3% of the time, Pallas kernels for 18%

profile of v10, /device:TPU:24, one launch (start us, length us, event | category | flops | bytes accessed | tf_op | source)
XLA Modules:
  0.0 134.4 jit_solution(11536772217661506274)
XLA Ops:
  0.6 0.7 multiply_add_fusion
  1.3 0.8 select_reduce_fusion.1
  2.1 0.7 copy.12
  2.8 8.2 %all-to-all-start = ((s32[16,1,2]{2,1,0:T(1,128)}), s32[16,1,2]{2,1,0:T(1,128)S(1)}, u32[]{:S(2)}, u32[]{:S(2)}) async-start(s32[16,1,2]{2,1,0:T(1,128)} %copy.12), calls=%async_computation | async-start | bytes 16384 | tf_op jit(solution)/shard_map/all_to_all | solution.py:568
  11.0 0.8 fusion.4
  11.8 2.8 %collective-permute-start.1 = (bf16[20,1024]{1,0:T(8,128)(2,1)S(1)}, bf16[20,1024]{1,0:T(8,128)(2,1)S(1)}, u32[]{:S(2)}, u32[]{:S(2)}) collective-permute-start(bf16[20,1024]{1,0:T(8,128)(2,1)S(1)} %get-tuple-element.32), channel_id=1, source_target_pairs={{8,0},{16,8},{24,16},{32,24},{40,32},{48,40},{56,48},{64,56},{72,6... | collective-permute-start | bytes 122888 | tf_op jit(solution)/shard_map/ppermute | solution.py:50
  14.6 5.2 %collective-permute-start = (bf16[20,1024]{1,0:T(8,128)(2,1)S(1)}, bf16[20,1024]{1,0:T(8,128)(2,1)S(1)}, u32[]{:S(2)}, u32[]{:S(2)}) collective-permute-start(bf16[20,1024]{1,0:T(8,128)(2,1)S(1)} %get-tuple-element.33), channel_id=1, source_target_pairs={{0,8},{8,16},{16,24},{24,32},{32,40},{40,48},{48,56},{56,64},{64,7... | collective-permute-start | bytes 122888 | tf_op jit(solution)/shard_map/ppermute | solution.py:50
  19.8 0.7 fusion.1
  20.5 1.2 convert_add_fusion.slot_ref
  21.7 0.0 all-to-all-done.refs_0_
  21.8 0.0 copy-start
  21.8 0.0 collective-permute-done.1.below_ref
  21.8 0.0 collective-permute-done.above_ref
  21.8 2.2 %blocks.1.refs_1_ = f32[38,72,128]{2,1,0:T(8,128)S(1)} custom-call(bf16[256,1024]{1,0:T(8,128)(2,1)} %stripe_ref.1, bf16[20,1024]{1,0:T(8,128)(2,1)S(1)} %collective-permute-done.above_ref, bf16[20,1024]{1,0:T(8,128)(2,1)S(1)} %collective-permute-done.1.below_ref), custom_call_target="tpu_custom_call" | custom-call | flops 1000 | bytes 1000 | tf_op jit(solution)/shard_map/blocks/pallas_call | solution.py:204
  24.0 0.0 copy-done
  24.0 3.2 %cut.1 = bf16[32,232,128]{2,1,0:T(8,128)(2,1)} custom-call(s32[16,1,2]{2,1,0:T(1,128)} %copy-done, f32[38,72,128]{2,1,0:T(8,128)S(1)} %blocks.1.refs_1_), custom_call_target="tpu_custom_call" | custom-call | flops 1000 | bytes 1000 | tf_op jit(solution)/shard_map/cut/pallas_call | solution.py:238
  27.2 0.0 copy-start.1
  27.2 7.7 %all-to-all-start.1 = ((bf16[32,232,128]{2,1,0:T(8,128)(2,1)}), bf16[32,232,128]{2,1,0:T(8,128)(2,1)S(1)}, u32[]{:S(2)}, u32[]{:S(2)}) async-start(bf16[32,232,128]{2,1,0:T(8,128)(2,1)} %cut.1), calls=%async_computation.1 | async-start | bytes 3801088 | tf_op jit(solution)/shard_map/all_to_all | solution.py:583
  34.9 0.0 copy-done.1
  34.9 0.2 reshape.102
  35.1 0.7 pad.4.kernel_ref
  35.9 13.8 %taps.1.refs_0_.refs_1_.refs_2_.refs_3_ = bf16[16,512,768]{2,1,0:T(8,128)(2,1)} custom-call(bf16[16,48,128]{2,1,0:T(8,128)(2,1)} %pad.4.kernel_ref), custom_call_target="tpu_custom_call" | custom-call | flops 1000 | bytes 1000 | tf_op jit(solution)/shard_map/taps/pallas_call | solution.py:162
  49.6 4.8 %regroup.1.refs_4_ = bf16[16,64,256]{2,1,0:T(8,128)(2,1)} custom-call(bf16[16,128,128]{2,1,0:T(8,128)(2,1)} %data_ref, s32[16,128,128]{2,1,0:T(8,128)} %keep_ref), custom_call_target="tpu_custom_call" | custom-call | flops 1000 | bytes 1000 | tf_op jit(solution)/shard_map/regroup/pallas_call | solution.py:99
  54.4 2.4 %all-to-all-done.1.patch_ref = bf16[32,232,128]{2,1,0:T(8,128)(2,1)S(1)} async-done(((bf16[32,232,128]{2,1,0:T(8,128)(2,1)}), bf16[32,232,128]{2,1,0:T(8,128)(2,1)S(1)}, u32[]{:S(2)}, u32[]{:S(2)}) %all-to-all-start.1) | async-done | bytes 1900576 | tf_op jit(solution)/shard_map/all_to_all | solution.py:583
  56.8 12.3 %pieces.1 = (bf16[32,240,128]{2,1,0:T(8,128)(2,1)}, bf16[16,64,256]{2,1,0:T(8,128)(2,1)}) custom-call(s32[16]{0:T(128)} %convert_add_fusion.slot_ref, s32[16]{0:T(128)} %cell_ref.1, bf16[32,232,128]{2,1,0:T(8,128)(2,1)S(1)} %all-to-all-done.1.patch_ref, bf16[16,512,768]{2,1,0:T(8,128)(2,1)} %taps.1.refs_0_.refs_1_.refs_2_.refs_3_, ...), custom_call_target="tpu_custom_call" | custom-call | flops 1000 | bytes 1000 | tf_op jit(solution)/shard_map/pieces/pallas_call | solution.py:378
  69.1 7.7 %all-to-all-start.2 = ((bf16[32,240,128]{2,1,0:T(8,128)(2,1)}), bf16[32,240,128]{2,1,0:T(8,128)(2,1)S(1)}, u32[]{:S(2)}, u32[]{:S(2)}) async-start(bf16[32,240,128]{2,1,0:T(8,128)(2,1)} %get-tuple-element.23), calls=%async_computation.2 | async-start | bytes 3932160 | tf_op jit(solution)/shard_map/all_to_all | solution.py:587
  76.8 6.3 %ungroup.1 = bf16[16,128,128]{2,1,0:T(8,128)(2,1)} custom-call(bf16[16,64,256]{2,1,0:T(8,128)(2,1)} %get-tuple-element.24.res_ref), custom_call_target="tpu_custom_call" | custom-call | flops 1000 | bytes 1000 | tf_op jit(solution)/shard_map/ungroup/pallas_call | solution.py:420
  83.1 17.4 %all-to-all-done.2.refs_1_ = bf16[32,240,128]{2,1,0:T(8,128)(2,1)S(1)} async-done(((bf16[32,240,128]{2,1,0:T(8,128)(2,1)}), bf16[32,240,128]{2,1,0:T(8,128)(2,1)S(1)}, u32[]{:S(2)}, u32[]{:S(2)}) %all-to-all-start.2) | async-done | bytes 1966112 | tf_op jit(solution)/shard_map/all_to_all | solution.py:587
  100.5 2.2 %fold.1 = bf16[8,352,128]{2,1,0:T(8,128)(2,1)S(1)} custom-call(s32[16,1,2]{2,1,0:T(1,128)} %copy-done, bf16[32,240,128]{2,1,0:T(8,128)(2,1)S(1)} %all-to-all-done.2.refs_1_), custom_call_target="tpu_custom_call" | custom-call | flops 1000 | bytes 1000 | tf_op jit(solution)/shard_map/fold/pallas_call | solution.py:461
  102.7 16.3 %all_to_all.20.refs_0_ = bf16[8,352,128]{2,1,0:T(8,128)(2,1)S(1)} all-to-all(bf16[8,352,128]{2,1,0:T(8,128)(2,1)S(1)} %fold.1), channel_id=1, replica_groups=mesh['sky'=16,'exp'=8] {'exp'}, dimensions={0} | all-to-all | bytes 1441792 | tf_op jit(solution)/shard_map/all_to_all | solution.py:591
  119.0 1.3 finish.1
  120.2 5.2 %collective-permute-start.2 = (bf16[20,128]{1,0:T(8,128)(2,1)S(1)}, bf16[20,128]{1,0:T(8,128)(2,1)S(1)}, u32[]{:S(2)}, u32[]{:S(2)}) collective-permute-start(bf16[20,128]{1,0:T(8,128)(2,1)S(1)} %get-tuple-element.27), channel_id=1, source_target_pairs={{0,8},{8,16},{16,24},{24,32},{32,40},{40,48},{48,56},{56,64},{64,7... | collective-permute-start | bytes 15368 | tf_op jit(solution)/shard_map/ppermute | solution.py:50
  125.5 1.9 %collective-permute-start.3 = (bf16[20,128]{1,0:T(8,128)(2,1)S(1)}, bf16[20,128]{1,0:T(8,128)(2,1)S(1)}, u32[]{:S(2)}, u32[]{:S(2)}) collective-permute-start(bf16[20,128]{1,0:T(8,128)(2,1)S(1)} %get-tuple-element.28), channel_id=1, source_target_pairs={{8,0},{16,8},{24,16},{32,24},{40,32},{48,40},{56,48},{64,56},{72,6... | collective-permute-start | bytes 15368 | tf_op jit(solution)/shard_map/ppermute | solution.py:50
  127.4 0.0 collective-permute-done.2.above_ref
  127.4 5.7 %collective-permute-done.3.below_ref = bf16[20,128]{1,0:T(8,128)(2,1)S(1)} collective-permute-done((bf16[20,128]{1,0:T(8,128)(2,1)S(1)}, bf16[20,128]{1,0:T(8,128)(2,1)S(1)}, u32[]{:S(2)}, u32[]{:S(2)}) %collective-permute-start.3) | collective-permute-done | bytes 5152 | tf_op jit(solution)/shard_map/ppermute | solution.py:50
  133.1 1.4 %rims.1 = f32[256,128]{1,0:T(8,128)} custom-call(f32[256,128]{1,0:T(8,128)} %get-tuple-element.26.middle_ref, bf16[20,128]{1,0:T(8,128)(2,1)S(1)} %collective-permute-done.2.above_ref, bf16[20,128]{1,0:T(8,128)(2,1)S(1)} %collective-permute-done.3.below_ref), custom_call_target="tpu_custom_call", output_to_operand_aliasing={{}: (0, {})} | custom-call | flops 1000 | bytes 1000 | tf_op jit(solution)/shard_map/rims/pallas_call | solution.py:538
  (2 shorter events, 0.0 us)
Async XLA Ops:
  2.8 19.0 %all-to-all-start = ((s32[16,1,2]{2,1,0:T(1,128)}), s32[16,1,2]{2,1,0:T(1,128)S(1)}, u32[]{:S(2)}, u32[]{:S(2)}) async-start(s32[16,1,2]{2,1,0:T(1,128)} %copy.12), calls=%async_computation | async-start | bytes 16384 | tf_op jit(solution)/shard_map/all_to_all | solution.py:568
  11.8 10.0 %collective-permute-start.1 = (bf16[20,1024]{1,0:T(8,128)(2,1)S(1)}, bf16[20,1024]{1,0:T(8,128)(2,1)S(1)}, u32[]{:S(2)}, u32[]{:S(2)}) collective-permute-start(bf16[20,1024]{1,0:T(8,128)(2,1)S(1)} %get-tuple-element.32), channel_id=1, source_target_pairs={{8,0},{16,8},{24,16},{32,24},{40,32},{48,40},{56,48},{64,56},{72,6... | collective-permute-start | bytes 122888 | tf_op jit(solution)/shard_map/ppermute | solution.py:50
  14.6 7.2 %collective-permute-start = (bf16[20,1024]{1,0:T(8,128)(2,1)S(1)}, bf16[20,1024]{1,0:T(8,128)(2,1)S(1)}, u32[]{:S(2)}, u32[]{:S(2)}) collective-permute-start(bf16[20,1024]{1,0:T(8,128)(2,1)S(1)} %get-tuple-element.33), channel_id=1, source_target_pairs={{0,8},{8,16},{16,24},{24,32},{32,40},{40,48},{48,56},{56,64},{64,7... | collective-permute-start | bytes 122888 | tf_op jit(solution)/shard_map/ppermute | solution.py:50
  21.8 2.3 %copy-start = (s32[16,1,2]{2,1,0:T(1,128)}, s32[16,1,2]{2,1,0:T(1,128)S(1)}, u32[]{:S(2)}) copy-start(s32[16,1,2]{2,1,0:T(1,128)S(1)} %all-to-all-done.refs_0_) | copy-start | bytes 388
  27.2 7.7 %copy-start.1 = (bf16[16,1681]{1,0:T(8,128)(2,1)S(1)}, bf16[16,1681]{1,0:T(8,128)(2,1)}, u32[]{:S(2)}) copy-start(bf16[16,1681]{1,0:T(8,128)(2,1)} %param.13) | copy-start | bytes 161380
  27.2 29.5 %all-to-all-start.1 = ((bf16[32,232,128]{2,1,0:T(8,128)(2,1)}), bf16[32,232,128]{2,1,0:T(8,128)(2,1)S(1)}, u32[]{:S(2)}, u32[]{:S(2)}) async-start(bf16[32,232,128]{2,1,0:T(8,128)(2,1)} %cut.1), calls=%async_computation.1 | async-start | bytes 3801088 | tf_op jit(solution)/shard_map/all_to_all | solution.py:583
  69.1 31.5 %all-to-all-start.2 = ((bf16[32,240,128]{2,1,0:T(8,128)(2,1)}), bf16[32,240,128]{2,1,0:T(8,128)(2,1)S(1)}, u32[]{:S(2)}, u32[]{:S(2)}) async-start(bf16[32,240,128]{2,1,0:T(8,128)(2,1)} %get-tuple-element.23), calls=%async_computation.2 | async-start | bytes 3932160 | tf_op jit(solution)/shard_map/all_to_all | solution.py:587
  120.2 7.1 %collective-permute-start.2 = (bf16[20,128]{1,0:T(8,128)(2,1)S(1)}, bf16[20,128]{1,0:T(8,128)(2,1)S(1)}, u32[]{:S(2)}, u32[]{:S(2)}) collective-permute-start(bf16[20,128]{1,0:T(8,128)(2,1)S(1)} %get-tuple-element.27), channel_id=1, source_target_pairs={{0,8},{8,16},{16,24},{24,32},{32,40},{40,48},{48,56},{56,64},{64,7... | collective-permute-start | bytes 15368 | tf_op jit(solution)/shard_map/ppermute | solution.py:50
  125.5 7.6 %collective-permute-start.3 = (bf16[20,128]{1,0:T(8,128)(2,1)S(1)}, bf16[20,128]{1,0:T(8,128)(2,1)S(1)}, u32[]{:S(2)}, u32[]{:S(2)}) collective-permute-start(bf16[20,128]{1,0:T(8,128)(2,1)S(1)} %get-tuple-element.28), channel_id=1, source_target_pairs={{8,0},{16,8},{24,16},{32,24},{40,32},{48,40},{56,48},{64,56},{72,6... | collective-permute-start | bytes 15368 | tf_op jit(solution)/shard_map/ppermute | solution.py:50

commit v11 on v8

--- a/solution.py
+++ b/solution.py
@@ -572,14 +572,14 @@
     below = from_behind(sky_model[:HALO], "sky", -1)
     half_rows = (stripe_rows + 2 * HALO + TAIL) // 8
     second = jnp.any(mine & (first[:, None] < code[None, :]), axis=0)
-    slot_index = owner_sky * CAP + second.astype(jnp.int32)
     kernels = padded_kernels(psf_table)
-    asked, above, below, slot_index = lax.optimization_barrier((asked, above, below, slot_index))
+    asked, above, below, second = lax.optimization_barrier((asked, above, below, second))
     blocks = stripe_blocks(sky_model, above, below, half_rows)
     outgoing = cut_patches(asked, blocks, per_row)
-    exposure_data, pixel_mask, kernels, _ = lax.optimization_barrier(
-        (exposure_data, pixel_mask, kernels, outgoing)
+    exposure_data, pixel_mask, kernels, second, _ = lax.optimization_barrier(
+        (exposure_data, pixel_mask, kernels, second, outgoing)
     )
+    slot_index = owner_sky * CAP + second.astype(jnp.int32)
     patches = lax.all_to_all(outgoing, "sky", split_axis=0, concat_axis=0, tiled=True)
     data = regroup(exposure_data, pixel_mask)
     taps = build_taps(kernels)

time: 135 us -> 135 us (level)
    all_to_all x1, waiting for transfers between devices: 17.1 us -> 15.3 us  [shards(): lax.all_to_all(adjoints, 'sky', split_axis=0, concat_axis=0, tiled=True)]
  transfers between devices with their start and end apart: 7 -> 7, of which waited for: 2 -> 3; matrix products, arithmetic and copies ran while one was open for 3% -> 2% of each run, Pallas kernels for 21% -> 21%
where the time goes in v11:
time: 135 us; the launch traced here: 134 us
  Pallas kernels  51.2 us (38%)
  starting transfers between devices  37.9 us (28%)
  waiting for transfers between devices  22 us (16%)
  blocking collectives  16.8 us (12%)
  other arithmetic  2.74 us (2%)
  local copies, waits for them, and re-layouts  2.48 us (2%)
    pallas_call x1, Pallas kernels, build_taps(): pl.pallas_call(taps_kernel, grid=(cells,), in_specs=[pl.BlockSpec((1, TAP...  16.9 us
    all_to_all x1, blocking collectives, shards(): lax.all_to_all(partial, 'exp', split_axis=0, concat_axis=0, tiled=True)  16.8 us
    all_to_all x1, waiting for transfers between devices, shards(): lax.all_to_all(adjoints, 'sky', split_axis=0, concat_axis=0, tiled=True)  15.3 us
    ppermute x4, starting transfers between devices, from_behind(): return lax.ppermute(x, axis, pairs)  14.2 us
    pallas_call x1, Pallas kernels, pieces(): pl.pallas_call(pieces_kernel, grid_spec=pltpu.PrefetchScalarGridSpec(num_...  12.3 us
    all_to_all x1, starting transfers between devices, shards(): lax.all_to_all(requests[:, None, :], 'sky', split_axis=0, concat_axis=0,...  8.18 us
    all_to_all x1, starting transfers between devices, shards(): lax.all_to_all(adjoints, 'sky', split_axis=0, concat_axis=0, tiled=True)  7.88 us
    all_to_all x1, starting transfers between devices, shards(): lax.all_to_all(outgoing, 'sky', split_axis=0, concat_axis=0, tiled=True)  7.67 us
  transfers between devices with their start and end apart: 7, of which 3 were waited for; matrix products, arithmetic and copies ran while one was open for 2% of the time, Pallas kernels for 21%

profile of v11, /device:TPU:24, one launch (start us, length us, event | category | flops | bytes accessed | tf_op | source)
XLA Modules:
  0.0 133.9 jit_solution(1038680674544299788)
XLA Ops:
  0.6 0.7 multiply_add_fusion
  1.3 0.8 select_reduce_fusion.1
  2.1 0.7 copy.12
  2.8 8.2 %all-to-all-start = ((s32[16,1,2]{2,1,0:T(1,128)}), s32[16,1,2]{2,1,0:T(1,128)S(1)}, u32[]{:S(2)}, u32[]{:S(2)}) async-start(s32[16,1,2]{2,1,0:T(1,128)} %copy.12), calls=%async_computation | async-start | bytes 16384 | tf_op jit(solution)/shard_map/all_to_all | solution.py:568
  11.0 0.8 fusion.4
  11.8 2.8 %collective-permute-start.1 = (bf16[20,1024]{1,0:T(8,128)(2,1)S(1)}, bf16[20,1024]{1,0:T(8,128)(2,1)S(1)}, u32[]{:S(2)}, u32[]{:S(2)}) collective-permute-start(bf16[20,1024]{1,0:T(8,128)(2,1)S(1)} %get-tuple-element.34), channel_id=1, source_target_pairs={{8,0},{16,8},{24,16},{32,24},{40,32},{48,40},{56,48},{64,56},{72,6... | collective-permute-start | bytes 122888 | tf_op jit(solution)/shard_map/ppermute | solution.py:50
  14.6 5.2 %collective-permute-start = (bf16[20,1024]{1,0:T(8,128)(2,1)S(1)}, bf16[20,1024]{1,0:T(8,128)(2,1)S(1)}, u32[]{:S(2)}, u32[]{:S(2)}) collective-permute-start(bf16[20,1024]{1,0:T(8,128)(2,1)S(1)} %get-tuple-element.35), channel_id=1, source_target_pairs={{0,8},{8,16},{16,24},{24,32},{32,40},{40,48},{48,56},{56,64},{64,7... | collective-permute-start | bytes 122888 | tf_op jit(solution)/shard_map/ppermute | solution.py:50
  19.8 0.7 fusion.1
  20.5 0.0 all-to-all-done.refs_0_
  20.5 0.0 copy-start
  20.5 0.0 collective-permute-done.1.below_ref
  20.5 1.0 collective-permute-done.above_ref
  21.5 2.2 %blocks.1.refs_1_ = f32[38,72,128]{2,1,0:T(8,128)S(1)} custom-call(bf16[256,1024]{1,0:T(8,128)(2,1)} %stripe_ref.1, bf16[20,1024]{1,0:T(8,128)(2,1)S(1)} %collective-permute-done.above_ref, bf16[20,1024]{1,0:T(8,128)(2,1)S(1)} %collective-permute-done.1.below_ref), custom_call_target="tpu_custom_call" | custom-call | flops 1000 | bytes 1000 | tf_op jit(solution)/shard_map/blocks/pallas_call | solution.py:204
  23.7 0.0 copy-done
  23.7 3.5 %cut.1 = bf16[32,232,128]{2,1,0:T(8,128)(2,1)} custom-call(s32[16,1,2]{2,1,0:T(1,128)} %copy-done, f32[38,72,128]{2,1,0:T(8,128)S(1)} %blocks.1.refs_1_), custom_call_target="tpu_custom_call" | custom-call | flops 1000 | bytes 1000 | tf_op jit(solution)/shard_map/cut/pallas_call | solution.py:238
  27.2 0.0 copy-start.1
  27.2 7.7 %all-to-all-start.1 = ((bf16[32,232,128]{2,1,0:T(8,128)(2,1)}), bf16[32,232,128]{2,1,0:T(8,128)(2,1)S(1)}, u32[]{:S(2)}, u32[]{:S(2)}) async-start(bf16[32,232,128]{2,1,0:T(8,128)(2,1)} %cut.1), calls=%async_computation.1 | async-start | bytes 3801088 | tf_op jit(solution)/shard_map/all_to_all | solution.py:583
  34.9 0.0 copy-done.1
  34.9 0.2 reshape.102
  35.1 0.7 pad.4.kernel_ref
  35.8 16.9 %taps.1.refs_0_.refs_1_.refs_2_.refs_3_ = bf16[16,512,768]{2,1,0:T(8,128)(2,1)} custom-call(bf16[16,48,128]{2,1,0:T(8,128)(2,1)} %pad.4.kernel_ref), custom_call_target="tpu_custom_call" | custom-call | flops 1000 | bytes 1000 | tf_op jit(solution)/shard_map/taps/pallas_call | solution.py:162
  52.8 0.0 copy-start.2
  52.8 4.8 %regroup.1.refs_4_ = bf16[16,64,256]{2,1,0:T(8,128)(2,1)} custom-call(bf16[16,128,128]{2,1,0:T(8,128)(2,1)} %data_ref, s32[16,128,128]{2,1,0:T(8,128)} %keep_ref), custom_call_target="tpu_custom_call" | custom-call | flops 1000 | bytes 1000 | tf_op jit(solution)/shard_map/regroup/pallas_call | solution.py:99
  57.5 0.0 copy-done.2
  57.5 0.5 convert_add_fusion.slot_ref
  58.1 0.0 all-to-all-done.1.patch_ref
  58.1 12.3 %pieces.1 = (bf16[32,240,128]{2,1,0:T(8,128)(2,1)}, bf16[16,64,256]{2,1,0:T(8,128)(2,1)}) custom-call(s32[16]{0:T(128)} %convert_add_fusion.slot_ref, s32[16]{0:T(128)} %cell_ref.1, bf16[32,232,128]{2,1,0:T(8,128)(2,1)S(1)} %all-to-all-done.1.patch_ref, bf16[16,512,768]{2,1,0:T(8,128)(2,1)} %taps.1.refs_0_.refs_1_.refs_2_.refs_3_, ...), custom_call_target="tpu_custom_call" | custom-call | flops 1000 | bytes 1000 | tf_op jit(solution)/shard_map/pieces/pallas_call | solution.py:378
  70.4 7.9 %all-to-all-start.2 = ((bf16[32,240,128]{2,1,0:T(8,128)(2,1)}), bf16[32,240,128]{2,1,0:T(8,128)(2,1)S(1)}, u32[]{:S(2)}, u32[]{:S(2)}) async-start(bf16[32,240,128]{2,1,0:T(8,128)(2,1)} %get-tuple-element.25), calls=%async_computation.2 | async-start | bytes 3932160 | tf_op jit(solution)/shard_map/all_to_all | solution.py:587
  78.2 6.3 %ungroup.1 = bf16[16,128,128]{2,1,0:T(8,128)(2,1)} custom-call(bf16[16,64,256]{2,1,0:T(8,128)(2,1)} %get-tuple-element.26.res_ref), custom_call_target="tpu_custom_call" | custom-call | flops 1000 | bytes 1000 | tf_op jit(solution)/shard_map/ungroup/pallas_call | solution.py:420
  84.6 15.3 %all-to-all-done.2.refs_1_ = bf16[32,240,128]{2,1,0:T(8,128)(2,1)S(1)} async-done(((bf16[32,240,128]{2,1,0:T(8,128)(2,1)}), bf16[32,240,128]{2,1,0:T(8,128)(2,1)S(1)}, u32[]{:S(2)}, u32[]{:S(2)}) %all-to-all-start.2) | async-done | bytes 1966112 | tf_op jit(solution)/shard_map/all_to_all | solution.py:587
  99.9 2.6 %fold.1 = bf16[8,352,128]{2,1,0:T(8,128)(2,1)S(1)} custom-call(s32[16,1,2]{2,1,0:T(1,128)} %copy-done, bf16[32,240,128]{2,1,0:T(8,128)(2,1)S(1)} %all-to-all-done.2.refs_1_), custom_call_target="tpu_custom_call" | custom-call | flops 1000 | bytes 1000 | tf_op jit(solution)/shard_map/fold/pallas_call | solution.py:461
  102.5 16.8 %all_to_all.20.refs_0_ = bf16[8,352,128]{2,1,0:T(8,128)(2,1)S(1)} all-to-all(bf16[8,352,128]{2,1,0:T(8,128)(2,1)S(1)} %fold.1), channel_id=1, replica_groups=mesh['sky'=16,'exp'=8] {'exp'}, dimensions={0} | all-to-all | bytes 1441792 | tf_op jit(solution)/shard_map/all_to_all | solution.py:591
  119.3 1.3 finish.1
  120.6 4.3 %collective-permute-start.2 = (bf16[20,128]{1,0:T(8,128)(2,1)S(1)}, bf16[20,128]{1,0:T(8,128)(2,1)S(1)}, u32[]{:S(2)}, u32[]{:S(2)}) collective-permute-start(bf16[20,128]{1,0:T(8,128)(2,1)S(1)} %get-tuple-element.29), channel_id=1, source_target_pairs={{0,8},{8,16},{16,24},{24,32},{32,40},{40,48},{48,56},{56,64},{64,7... | collective-permute-start | bytes 15368 | tf_op jit(solution)/shard_map/ppermute | solution.py:50
  124.9 1.9 %collective-permute-start.3 = (bf16[20,128]{1,0:T(8,128)(2,1)S(1)}, bf16[20,128]{1,0:T(8,128)(2,1)S(1)}, u32[]{:S(2)}, u32[]{:S(2)}) collective-permute-start(bf16[20,128]{1,0:T(8,128)(2,1)S(1)} %get-tuple-element.30), channel_id=1, source_target_pairs={{8,0},{16,8},{24,16},{32,24},{40,32},{48,40},{56,48},{64,56},{72,6... | collective-permute-start | bytes 15368 | tf_op jit(solution)/shard_map/ppermute | solution.py:50
  126.8 0.0 collective-permute-done.2.above_ref
  126.8 5.7 %collective-permute-done.3.below_ref = bf16[20,128]{1,0:T(8,128)(2,1)S(1)} collective-permute-done((bf16[20,128]{1,0:T(8,128)(2,1)S(1)}, bf16[20,128]{1,0:T(8,128)(2,1)S(1)}, u32[]{:S(2)}, u32[]{:S(2)}) %collective-permute-start.3) | collective-permute-done | bytes 5152 | tf_op jit(solution)/shard_map/ppermute | solution.py:50
  132.5 1.4 %rims.1 = f32[256,128]{1,0:T(8,128)} custom-call(f32[256,128]{1,0:T(8,128)} %get-tuple-element.28.middle_ref, bf16[20,128]{1,0:T(8,128)(2,1)S(1)} %collective-permute-done.2.above_ref, bf16[20,128]{1,0:T(8,128)(2,1)S(1)} %collective-permute-done.3.below_ref), custom_call_target="tpu_custom_call", output_to_operand_aliasing={{}: (0, {})} | custom-call | flops 1000 | bytes 1000 | tf_op jit(solution)/shard_map/rims/pallas_call | solution.py:538
  (2 shorter events, 0.0 us)
Async XLA Ops:
  2.8 17.7 %all-to-all-start = ((s32[16,1,2]{2,1,0:T(1,128)}), s32[16,1,2]{2,1,0:T(1,128)S(1)}, u32[]{:S(2)}, u32[]{:S(2)}) async-start(s32[16,1,2]{2,1,0:T(1,128)} %copy.12), calls=%async_computation | async-start | bytes 16384 | tf_op jit(solution)/shard_map/all_to_all | solution.py:568
  11.8 8.7 %collective-permute-start.1 = (bf16[20,1024]{1,0:T(8,128)(2,1)S(1)}, bf16[20,1024]{1,0:T(8,128)(2,1)S(1)}, u32[]{:S(2)}, u32[]{:S(2)}) collective-permute-start(bf16[20,1024]{1,0:T(8,128)(2,1)S(1)} %get-tuple-element.34), channel_id=1, source_target_pairs={{8,0},{16,8},{24,16},{32,24},{40,32},{48,40},{56,48},{64,56},{72,6... | collective-permute-start | bytes 122888 | tf_op jit(solution)/shard_map/ppermute | solution.py:50
  14.6 6.9 %collective-permute-start = (bf16[20,1024]{1,0:T(8,128)(2,1)S(1)}, bf16[20,1024]{1,0:T(8,128)(2,1)S(1)}, u32[]{:S(2)}, u32[]{:S(2)}) collective-permute-start(bf16[20,1024]{1,0:T(8,128)(2,1)S(1)} %get-tuple-element.35), channel_id=1, source_target_pairs={{0,8},{8,16},{16,24},{24,32},{32,40},{40,48},{48,56},{56,64},{64,7... | collective-permute-start | bytes 122888 | tf_op jit(solution)/shard_map/ppermute | solution.py:50
  20.5 3.2 %copy-start = (s32[16,1,2]{2,1,0:T(1,128)}, s32[16,1,2]{2,1,0:T(1,128)S(1)}, u32[]{:S(2)}) copy-start(s32[16,1,2]{2,1,0:T(1,128)S(1)} %all-to-all-done.refs_0_) | copy-start | bytes 388
  27.2 7.7 %copy-start.1 = (bf16[16,1681]{1,0:T(8,128)(2,1)S(1)}, bf16[16,1681]{1,0:T(8,128)(2,1)}, u32[]{:S(2)}) copy-start(bf16[16,1681]{1,0:T(8,128)(2,1)} %param.13) | copy-start | bytes 161380
  27.2 30.9 %all-to-all-start.1 = ((bf16[32,232,128]{2,1,0:T(8,128)(2,1)}), bf16[32,232,128]{2,1,0:T(8,128)(2,1)S(1)}, u32[]{:S(2)}, u32[]{:S(2)}) async-start(bf16[32,232,128]{2,1,0:T(8,128)(2,1)} %cut.1), calls=%async_computation.1 | async-start | bytes 3801088 | tf_op jit(solution)/shard_map/all_to_all | solution.py:583
  52.8 4.8 %copy-start.2 = (s32[16,1]{0,1:T(1,128)S(1)}, s32[16,1]{0,1:T(1,128)}, u32[]{:S(2)}) copy-start(s32[16,1]{0,1:T(1,128)} %param.10) | copy-start | bytes 196
  70.4 29.5 %all-to-all-start.2 = ((bf16[32,240,128]{2,1,0:T(8,128)(2,1)}), bf16[32,240,128]{2,1,0:T(8,128)(2,1)S(1)}, u32[]{:S(2)}, u32[]{:S(2)}) async-start(bf16[32,240,128]{2,1,0:T(8,128)(2,1)} %get-tuple-element.25), calls=%async_computation.2 | async-start | bytes 3932160 | tf_op jit(solution)/shard_map/all_to_all | solution.py:587
  120.6 6.3 %collective-permute-start.2 = (bf16[20,128]{1,0:T(8,128)(2,1)S(1)}, bf16[20,128]{1,0:T(8,128)(2,1)S(1)}, u32[]{:S(2)}, u32[]{:S(2)}) collective-permute-start(bf16[20,128]{1,0:T(8,128)(2,1)S(1)} %get-tuple-element.29), channel_id=1, source_target_pairs={{0,8},{8,16},{16,24},{24,32},{32,40},{40,48},{48,56},{56,64},{64,7... | collective-permute-start | bytes 15368 | tf_op jit(solution)/shard_map/ppermute | solution.py:50
  124.9 7.6 %collective-permute-start.3 = (bf16[20,128]{1,0:T(8,128)(2,1)S(1)}, bf16[20,128]{1,0:T(8,128)(2,1)S(1)}, u32[]{:S(2)}, u32[]{:S(2)}) collective-permute-start(bf16[20,128]{1,0:T(8,128)(2,1)S(1)} %get-tuple-element.30), channel_id=1, source_target_pairs={{8,0},{16,8},{24,16},{32,24},{40,32},{48,40},{56,48},{64,56},{72,6... | collective-permute-start | bytes 15368 | tf_op jit(solution)/shard_map/ppermute | solution.py:50

commit v12 on v11

--- a/solution.py
+++ b/solution.py
@@ -508,7 +508,7 @@
         lambda *refs: finish_kernel(half_rows, *refs),
         in_specs=[vmem],
         out_specs=[vmem, vmem, vmem],
-        out_shape=[rim, jax.ShapeDtypeStruct((rows, LANES), F32), rim],
+        out_shape=[rim, pltpu.VMEM((rows, LANES), F32), rim],
         scratch_shapes=[
             pltpu.VMEM((CHUNK_ROWS, LANES), F32),
             pltpu.VMEM((8 * half_rows, LANES), F32),
@@ -521,30 +521,19 @@
 def rims_kernel(middle_ref, above_ref, below_ref, out_ref):
     rows = out_ref.shape[0]
     out_ref[...] = middle_ref[...]
-
-    @pl.when(pl.program_id(0) == 0)
-    def _():
-        out_ref[:HALO, :] = out_ref[:HALO, :] + above_ref[...].astype(F32)
-
-    @pl.when(pl.program_id(0) == 1)
-    def _():
-        out_ref[rows - HALO :, :] = out_ref[rows - HALO :, :] + below_ref[...].astype(F32)
+    out_ref[:HALO, :] = out_ref[:HALO, :] + above_ref[...].astype(F32)
+    out_ref[rows - HALO :, :] = out_ref[rows - HALO :, :] + below_ref[...].astype(F32)
 
 
 def add_rims(middle, above, below):
-    rows = 32
-    last = middle.shape[0] // rows - 1
-    block = pl.BlockSpec((rows, LANES), lambda i: (i * last, 0))
     return pl.pallas_call(
         rims_kernel,
-        grid=(2,),
-        in_specs=[block, whole_vmem(), whole_vmem()],
-        out_specs=block,
+        in_specs=[whole_vmem(), whole_vmem(), whole_vmem()],
+        out_specs=whole_vmem(),
         out_shape=jax.ShapeDtypeStruct(middle.shape, F32),
-        input_output_aliases={0: 0},
         cost_estimate=SMALL,
         name="rims",
-    )(middle, on_chip(above), on_chip(below))
+    )(on_chip(middle), on_chip(above), on_chip(below))
 
 
 def shards(sky_model, exposure_data, pixel_mask, block_owner, block_local, psf_cell, psf_table):

time: 135 us -> 133 us (0.985)
  Pallas kernels: 51.2 us -> 49.1 us
where the time goes in v12:
time: 133 us; the launch traced here: 132 us
  Pallas kernels  49.1 us (37%)
  starting transfers between devices  38.1 us (29%)
  waiting for transfers between devices  22 us (17%)
  blocking collectives  17.3 us (13%)
  other arithmetic  2.74 us (2%)
  local copies, waits for them, and re-layouts  2.48 us (2%)
    all_to_all x1, blocking collectives, shards(): lax.all_to_all(partial, 'exp', split_axis=0, concat_axis=0, tiled=True)  17.3 us
    pallas_call x1, Pallas kernels, build_taps(): pl.pallas_call(taps_kernel, grid=(cells,), in_specs=[pl.BlockSpec((1, TAP...  16.9 us
    all_to_all x1, waiting for transfers between devices, shards(): lax.all_to_all(adjoints, 'sky', split_axis=0, concat_axis=0, tiled=True)  15.4 us
    ppermute x4, starting transfers between devices, from_behind(): return lax.ppermute(x, axis, pairs)  14.4 us
    pallas_call x1, Pallas kernels, pieces(): pl.pallas_call(pieces_kernel, grid_spec=pltpu.PrefetchScalarGridSpec(num_...  12.3 us
    all_to_all x1, starting transfers between devices, shards(): lax.all_to_all(requests[:, None, :], 'sky', split_axis=0, concat_axis=0,...  8.18 us
    all_to_all x1, starting transfers between devices, shards(): lax.all_to_all(outgoing, 'sky', split_axis=0, concat_axis=0, tiled=True)  7.99 us
    all_to_all x1, starting transfers between devices, shards(): lax.all_to_all(adjoints, 'sky', split_axis=0, concat_axis=0, tiled=True)  7.5 us
  transfers between devices with their start and end apart: 7, of which 3 were waited for; matrix products, arithmetic and copies ran while one was open for 2% of the time, Pallas kernels for 21%

profile of v12, /device:TPU:24, one launch (start us, length us, event | category | flops | bytes accessed | tf_op | source)
XLA Modules:
  0.0 132.4 jit_solution(11870784330806703130)
XLA Ops:
  0.6 0.7 multiply_add_fusion
  1.3 0.8 select_reduce_fusion.1
  2.1 0.7 copy.11
  2.8 8.2 %all-to-all-start = ((s32[16,1,2]{2,1,0:T(1,128)}), s32[16,1,2]{2,1,0:T(1,128)S(1)}, u32[]{:S(2)}, u32[]{:S(2)}) async-start(s32[16,1,2]{2,1,0:T(1,128)} %copy.11), calls=%async_computation | async-start | bytes 16384 | tf_op jit(solution)/shard_map/all_to_all | solution.py:557
  11.0 0.8 fusion.4
  11.8 2.8 %collective-permute-start.1 = (bf16[20,1024]{1,0:T(8,128)(2,1)S(1)}, bf16[20,1024]{1,0:T(8,128)(2,1)S(1)}, u32[]{:S(2)}, u32[]{:S(2)}) collective-permute-start(bf16[20,1024]{1,0:T(8,128)(2,1)S(1)} %get-tuple-element.34), channel_id=1, source_target_pairs={{8,0},{16,8},{24,16},{32,24},{40,32},{48,40},{56,48},{64,56},{72,6... | collective-permute-start | bytes 122888 | tf_op jit(solution)/shard_map/ppermute | solution.py:50
  14.6 5.2 %collective-permute-start = (bf16[20,1024]{1,0:T(8,128)(2,1)S(1)}, bf16[20,1024]{1,0:T(8,128)(2,1)S(1)}, u32[]{:S(2)}, u32[]{:S(2)}) collective-permute-start(bf16[20,1024]{1,0:T(8,128)(2,1)S(1)} %get-tuple-element.35), channel_id=1, source_target_pairs={{0,8},{8,16},{16,24},{24,32},{32,40},{40,48},{48,56},{56,64},{64,7... | collective-permute-start | bytes 122888 | tf_op jit(solution)/shard_map/ppermute | solution.py:50
  19.8 0.7 fusion.1
  20.5 0.0 all-to-all-done.refs_0_
  20.5 0.0 copy-start
  20.5 0.0 collective-permute-done.1.below_ref
  20.5 1.0 collective-permute-done.above_ref
  21.5 2.2 %blocks.1.refs_1_ = f32[38,72,128]{2,1,0:T(8,128)S(1)} custom-call(bf16[256,1024]{1,0:T(8,128)(2,1)} %stripe_ref.1, bf16[20,1024]{1,0:T(8,128)(2,1)S(1)} %collective-permute-done.above_ref, bf16[20,1024]{1,0:T(8,128)(2,1)S(1)} %collective-permute-done.1.below_ref), custom_call_target="tpu_custom_call" | custom-call | flops 1000 | bytes 1000 | tf_op jit(solution)/shard_map/blocks/pallas_call | solution.py:204
  23.7 0.0 copy-done
  23.7 3.2 %cut.1 = bf16[32,232,128]{2,1,0:T(8,128)(2,1)} custom-call(s32[16,1,2]{2,1,0:T(1,128)} %copy-done, f32[38,72,128]{2,1,0:T(8,128)S(1)} %blocks.1.refs_1_), custom_call_target="tpu_custom_call" | custom-call | flops 1000 | bytes 1000 | tf_op jit(solution)/shard_map/cut/pallas_call | solution.py:238
  26.9 0.0 copy-start.1
  26.9 8.0 %all-to-all-start.1 = ((bf16[32,232,128]{2,1,0:T(8,128)(2,1)}), bf16[32,232,128]{2,1,0:T(8,128)(2,1)S(1)}, u32[]{:S(2)}, u32[]{:S(2)}) async-start(bf16[32,232,128]{2,1,0:T(8,128)(2,1)} %cut.1), calls=%async_computation.1 | async-start | bytes 3801088 | tf_op jit(solution)/shard_map/all_to_all | solution.py:572
  34.9 0.0 copy-done.1
  34.9 0.2 reshape.102
  35.1 0.7 pad.4.kernel_ref
  35.8 16.9 %taps.1.refs_0_.refs_1_.refs_2_.refs_3_ = bf16[16,512,768]{2,1,0:T(8,128)(2,1)} custom-call(bf16[16,48,128]{2,1,0:T(8,128)(2,1)} %pad.4.kernel_ref), custom_call_target="tpu_custom_call" | custom-call | flops 1000 | bytes 1000 | tf_op jit(solution)/shard_map/taps/pallas_call | solution.py:162
  52.8 0.0 copy-start.2
  52.8 4.8 %regroup.1.refs_4_ = bf16[16,64,256]{2,1,0:T(8,128)(2,1)} custom-call(bf16[16,128,128]{2,1,0:T(8,128)(2,1)} %data_ref, s32[16,128,128]{2,1,0:T(8,128)} %keep_ref), custom_call_target="tpu_custom_call" | custom-call | flops 1000 | bytes 1000 | tf_op jit(solution)/shard_map/regroup/pallas_call | solution.py:99
  57.5 0.0 copy-done.2
  57.5 0.5 convert_add_fusion.slot_ref
  58.1 0.0 all-to-all-done.1.patch_ref
  58.1 12.3 %pieces.1 = (bf16[32,240,128]{2,1,0:T(8,128)(2,1)}, bf16[16,64,256]{2,1,0:T(8,128)(2,1)}) custom-call(s32[16]{0:T(128)} %convert_add_fusion.slot_ref, s32[16]{0:T(128)} %cell_ref.1, bf16[32,232,128]{2,1,0:T(8,128)(2,1)S(1)} %all-to-all-done.1.patch_ref, bf16[16,512,768]{2,1,0:T(8,128)(2,1)} %taps.1.refs_0_.refs_1_.refs_2_.refs_3_, ...), custom_call_target="tpu_custom_call" | custom-call | flops 1000 | bytes 1000 | tf_op jit(solution)/shard_map/pieces/pallas_call | solution.py:378
  70.4 7.5 %all-to-all-start.2 = ((bf16[32,240,128]{2,1,0:T(8,128)(2,1)}), bf16[32,240,128]{2,1,0:T(8,128)(2,1)S(1)}, u32[]{:S(2)}, u32[]{:S(2)}) async-start(bf16[32,240,128]{2,1,0:T(8,128)(2,1)} %get-tuple-element.25), calls=%async_computation.2 | async-start | bytes 3932160 | tf_op jit(solution)/shard_map/all_to_all | solution.py:576
  77.9 6.3 %ungroup.1 = bf16[16,128,128]{2,1,0:T(8,128)(2,1)} custom-call(bf16[16,64,256]{2,1,0:T(8,128)(2,1)} %get-tuple-element.26.res_ref), custom_call_target="tpu_custom_call" | custom-call | flops 1000 | bytes 1000 | tf_op jit(solution)/shard_map/ungroup/pallas_call | solution.py:420
  84.2 15.4 %all-to-all-done.2.refs_1_ = bf16[32,240,128]{2,1,0:T(8,128)(2,1)S(1)} async-done(((bf16[32,240,128]{2,1,0:T(8,128)(2,1)}), bf16[32,240,128]{2,1,0:T(8,128)(2,1)S(1)}, u32[]{:S(2)}, u32[]{:S(2)}) %all-to-all-start.2) | async-done | bytes 1966112 | tf_op jit(solution)/shard_map/all_to_all | solution.py:576
  99.6 2.1 %fold.1 = bf16[8,352,128]{2,1,0:T(8,128)(2,1)S(1)} custom-call(s32[16,1,2]{2,1,0:T(1,128)} %copy-done, bf16[32,240,128]{2,1,0:T(8,128)(2,1)S(1)} %all-to-all-done.2.refs_1_), custom_call_target="tpu_custom_call" | custom-call | flops 1000 | bytes 1000 | tf_op jit(solution)/shard_map/fold/pallas_call | solution.py:461
  101.7 17.3 %all_to_all.20.refs_0_ = bf16[8,352,128]{2,1,0:T(8,128)(2,1)S(1)} all-to-all(bf16[8,352,128]{2,1,0:T(8,128)(2,1)S(1)} %fold.1), channel_id=1, replica_groups=mesh['sky'=16,'exp'=8] {'exp'}, dimensions={0} | all-to-all | bytes 1441792 | tf_op jit(solution)/shard_map/all_to_all | solution.py:580
  119.0 0.6 finish.1
  119.6 4.5 %collective-permute-start.2 = (bf16[20,128]{1,0:T(8,128)(2,1)S(1)}, bf16[20,128]{1,0:T(8,128)(2,1)S(1)}, u32[]{:S(2)}, u32[]{:S(2)}) collective-permute-start(bf16[20,128]{1,0:T(8,128)(2,1)S(1)} %get-tuple-element.29), channel_id=1, source_target_pairs={{0,8},{8,16},{16,24},{24,32},{32,40},{40,48},{48,56},{56,64},{64,7... | collective-permute-start | bytes 15368 | tf_op jit(solution)/shard_map/ppermute | solution.py:50
  124.1 1.9 %collective-permute-start.3 = (bf16[20,128]{1,0:T(8,128)(2,1)S(1)}, bf16[20,128]{1,0:T(8,128)(2,1)S(1)}, u32[]{:S(2)}, u32[]{:S(2)}) collective-permute-start(bf16[20,128]{1,0:T(8,128)(2,1)S(1)} %get-tuple-element.30), channel_id=1, source_target_pairs={{8,0},{16,8},{24,16},{32,24},{40,32},{48,40},{56,48},{64,56},{72,6... | collective-permute-start | bytes 15368 | tf_op jit(solution)/shard_map/ppermute | solution.py:50
  126.1 0.0 collective-permute-done.2.above_ref
  126.1 5.7 %collective-permute-done.3.below_ref = bf16[20,128]{1,0:T(8,128)(2,1)S(1)} collective-permute-done((bf16[20,128]{1,0:T(8,128)(2,1)S(1)}, bf16[20,128]{1,0:T(8,128)(2,1)S(1)}, u32[]{:S(2)}, u32[]{:S(2)}) %collective-permute-start.3) | collective-permute-done | bytes 5152 | tf_op jit(solution)/shard_map/ppermute | solution.py:50
  131.8 0.7 rims.1
  (2 shorter events, 0.0 us)
Async XLA Ops:
  2.8 17.7 %all-to-all-start = ((s32[16,1,2]{2,1,0:T(1,128)}), s32[16,1,2]{2,1,0:T(1,128)S(1)}, u32[]{:S(2)}, u32[]{:S(2)}) async-start(s32[16,1,2]{2,1,0:T(1,128)} %copy.11), calls=%async_computation | async-start | bytes 16384 | tf_op jit(solution)/shard_map/all_to_all | solution.py:557
  11.8 8.7 %collective-permute-start.1 = (bf16[20,1024]{1,0:T(8,128)(2,1)S(1)}, bf16[20,1024]{1,0:T(8,128)(2,1)S(1)}, u32[]{:S(2)}, u32[]{:S(2)}) collective-permute-start(bf16[20,1024]{1,0:T(8,128)(2,1)S(1)} %get-tuple-element.34), channel_id=1, source_target_pairs={{8,0},{16,8},{24,16},{32,24},{40,32},{48,40},{56,48},{64,56},{72,6... | collective-permute-start | bytes 122888 | tf_op jit(solution)/shard_map/ppermute | solution.py:50
  14.6 6.9 %collective-permute-start = (bf16[20,1024]{1,0:T(8,128)(2,1)S(1)}, bf16[20,1024]{1,0:T(8,128)(2,1)S(1)}, u32[]{:S(2)}, u32[]{:S(2)}) collective-permute-start(bf16[20,1024]{1,0:T(8,128)(2,1)S(1)} %get-tuple-element.35), channel_id=1, source_target_pairs={{0,8},{8,16},{16,24},{24,32},{32,40},{40,48},{48,56},{56,64},{64,7... | collective-permute-start | bytes 122888 | tf_op jit(solution)/shard_map/ppermute | solution.py:50
  20.5 3.2 %copy-start = (s32[16,1,2]{2,1,0:T(1,128)}, s32[16,1,2]{2,1,0:T(1,128)S(1)}, u32[]{:S(2)}) copy-start(s32[16,1,2]{2,1,0:T(1,128)S(1)} %all-to-all-done.refs_0_) | copy-start | bytes 388
  26.9 8.0 %copy-start.1 = (bf16[16,1681]{1,0:T(8,128)(2,1)S(1)}, bf16[16,1681]{1,0:T(8,128)(2,1)}, u32[]{:S(2)}) copy-start(bf16[16,1681]{1,0:T(8,128)(2,1)} %param.13) | copy-start | bytes 161380
  26.9 31.2 %all-to-all-start.1 = ((bf16[32,232,128]{2,1,0:T(8,128)(2,1)}), bf16[32,232,128]{2,1,0:T(8,128)(2,1)S(1)}, u32[]{:S(2)}, u32[]{:S(2)}) async-start(bf16[32,232,128]{2,1,0:T(8,128)(2,1)} %cut.1), calls=%async_computation.1 | async-start | bytes 3801088 | tf_op jit(solution)/shard_map/all_to_all | solution.py:572
  52.8 4.8 %copy-start.2 = (s32[16,1]{0,1:T(1,128)S(1)}, s32[16,1]{0,1:T(1,128)}, u32[]{:S(2)}) copy-start(s32[16,1]{0,1:T(1,128)} %param.10) | copy-start | bytes 196
  70.4 29.2 %all-to-all-start.2 = ((bf16[32,240,128]{2,1,0:T(8,128)(2,1)}), bf16[32,240,128]{2,1,0:T(8,128)(2,1)S(1)}, u32[]{:S(2)}, u32[]{:S(2)}) async-start(bf16[32,240,128]{2,1,0:T(8,128)(2,1)} %get-tuple-element.25), calls=%async_computation.2 | async-start | bytes 3932160 | tf_op jit(solution)/shard_map/all_to_all | solution.py:576
  119.6 6.5 %collective-permute-start.2 = (bf16[20,128]{1,0:T(8,128)(2,1)S(1)}, bf16[20,128]{1,0:T(8,128)(2,1)S(1)}, u32[]{:S(2)}, u32[]{:S(2)}) collective-permute-start(bf16[20,128]{1,0:T(8,128)(2,1)S(1)} %get-tuple-element.29), channel_id=1, source_target_pairs={{0,8},{8,16},{16,24},{24,32},{32,40},{40,48},{48,56},{56,64},{64,7... | collective-permute-start | bytes 15368 | tf_op jit(solution)/shard_map/ppermute | solution.py:50
  124.1 7.6 %collective-permute-start.3 = (bf16[20,128]{1,0:T(8,128)(2,1)S(1)}, bf16[20,128]{1,0:T(8,128)(2,1)S(1)}, u32[]{:S(2)}, u32[]{:S(2)}) collective-permute-start(bf16[20,128]{1,0:T(8,128)(2,1)S(1)} %get-tuple-element.30), channel_id=1, source_target_pairs={{8,0},{16,8},{24,16},{32,24},{40,32},{48,40},{56,48},{64,56},{72,6... | collective-permute-start | bytes 15368 | tf_op jit(solution)/shard_map/ppermute | solution.py:50
